TPU v7x, 32 devices: a whole 2x2x4 slice. The times are simulated.
32 devices in a mesh: gx: 4 (over x, core), gy: 8 (over z, y).
Axes of the slice: x: 2, y: 2, z: 4, core: 2. Of those that a mesh axis runs over, the one named last changes fastest.
Arguments:
- target_ids: int32 [2, 4, 512], P(None, 'gx', 'gy'), may hold values from 0 to 16383
- labels: int32 [2, 4, 512], P(None, 'gx', 'gy'), may hold values from 0 to 16383
- lengths: int32 [2, 4], replicated, may hold values from 128 to 512, as said below
- memory: bfloat16 [2, 4, 1024, 512], P(None, 'gx', 'gy'), may hold values from -6 to 6
- embedding: bfloat16 [16384, 512], P(('gx', 'gy')), may hold values from -6 to 6
- head: bfloat16 [16384, 512], P(('gx', 'gy')), may hold values from -0.5 to 0.5
- gain_self: bfloat16 [512], P(('gx', 'gy')), may hold values from 0.5 to 1.5
- w_query: bfloat16 [512, 384], P(('gx', 'gy')), may hold values from -0.0625 to 0.0625
- w_key: bfloat16 [512, 384], P(('gx', 'gy')), may hold values from -0.25 to 0.25
- w_value: bfloat16 [512, 384], P(('gx', 'gy')), may hold values from -0.25 to 0.25
- w_out: bfloat16 [512, 384], P(('gx', 'gy')), may hold values from -1.25 to 1.25
- relative_bias: bfloat16 [6, 32], replicated, may hold values from -4 to 4
- gain_cross: bfloat16 [512], P(('gx', 'gy')), may hold values from 0.5 to 1.5
- c_query: bfloat16 [512, 384], P(('gx', 'gy')), may hold values from -0.0625 to 0.0625
- c_key: bfloat16 [512, 384], P(('gx', 'gy')), may hold values from -0.25 to 0.25
- c_value: bfloat16 [512, 384], P(('gx', 'gy')), may hold values from -0.25 to 0.25
- c_out: bfloat16 [512, 384], P(('gx', 'gy')), may hold values from -1.25 to 1.25
- gain_ff: bfloat16 [512], P(('gx', 'gy')), may hold values from 0.5 to 1.5
- w_gate: bfloat16 [512, 1024], P(('gx', 'gy')), may hold values from -0.25 to 0.25
- w_up: bfloat16 [512, 1024], P(('gx', 'gy')), may hold values from -0.25 to 0.25
- w_down: bfloat16 [512, 1024], P(('gx', 'gy')), may hold values from -0.1875 to 0.1875
- gain_final: bfloat16 [512], P(('gx', 'gy')), may hold values from 0.5 to 1.5
Outputs:
- loss: float32 [], replicated
- memory_grad: float32 [2, 4, 1024, 512], P(None, 'gx', 'gy')
- embedding_grad: float32 [16384, 512], P(('gx', 'gy'))
- head_grad: float32 [16384, 512], P(('gx', 'gy'))
- gain_self_grad: float32 [512], P(('gx', 'gy'))
- w_query_grad: float32 [512, 384], P(('gx', 'gy'))
- w_key_grad: float32 [512, 384], P(('gx', 'gy'))
- w_value_grad: float32 [512, 384], P(('gx', 'gy'))
- w_out_grad: float32 [512, 384], P(('gx', 'gy'))
- rel_bias_grad: float32 [6, 32], replicated
- gain_cross_grad: float32 [512], P(('gx', 'gy'))
- c_query_grad: float32 [512, 384], P(('gx', 'gy'))
- c_key_grad: float32 [512, 384], P(('gx', 'gy'))
- c_value_grad: float32 [512, 384], P(('gx', 'gy'))
- c_out_grad: float32 [512, 384], P(('gx', 'gy'))
- gain_ff_grad: float32 [512], P(('gx', 'gy'))
- w_gate_grad: float32 [512, 1024], P(('gx', 'gy'))
- w_up_grad: float32 [512, 1024], P(('gx', 'gy'))
- w_down_grad: float32 [512, 1024], P(('gx', 'gy'))
- gain_final_grad: float32 [512], P(('gx', 'gy'))
Inputs may be any that keep to these rules, and one draw needn't show every extreme that they name: `lengths`: each sequence's count of live target positions; some sequence has all 512, some has a quarter of 512.
All inputs are finite; a program needn't handle non-finite values.
Results may differ from a plain program's by a relative error of at most 0.024.
The roundings to bfloat16 on the way count: a program that leaves them out, or rounds other values in their place, can miss the bound.
Values may be sent and summed in bfloat16 or wider, within the bound.
A program may use at most 320 MiB of HBM per device.

v0:
```python
import functools
import itertools
import math

import jax
import jax.numpy as jnp
import numpy as np
from jax import lax
from jax.experimental import pallas as pl
from jax.experimental.pallas import tpu as pltpu
from jax.sharding import PartitionSpec as P

HEADS = 6
HEAD = 64
HD = HEADS * HEAD
BUCKETS = 32
GAIN_PAD = 128

eps = 1e-06
masked_score = -1000000000.0
bf16 = jnp.bfloat16
f32 = jnp.float32


def flip(position, offset):
    moved = position
    weight = 1
    while weight <= offset:
        if offset & weight:
            moved = moved + weight * (1 - 2 * ((position // weight) % 2))
        weight *= 2
    return moved


def coordinates():
    gx, gy = lax.axis_index("gx"), lax.axis_index("gy")
    return {"a": gx // 2, "c": gx % 2, "s": gy // 2, "h": gy % 2}


def peer_of(dim, offset):
    gx, gy = lax.axis_index("gx"), lax.axis_index("gy")
    if dim == "a":
        return {"gx": 2 * flip(gx // 2, offset) + gx % 2}
    if dim == "c":
        return {"gx": flip(gx, 1)}
    if dim == "plane":
        s, h = offset
        return {"gy": 2 * flip(gy // 2, s) + flip(gy % 2, h)}
    if dim == "s":
        return {"gy": 2 * flip(gy // 2, offset) + gy % 2}
    return {"gy": flip(gy, 1)}


def remote(source, target, send, recv, dim, offset):
    return pltpu.make_async_remote_copy(
        src_ref=source,
        dst_ref=target,
        send_sem=send,
        recv_sem=recv,
        device_id=peer_of(dim, offset),
        device_id_type=pl.DeviceIdType.MESH,
    )


def along_line(position, step):
    half = position // 2
    return (position, flip(position, 1), 2 - half, 3 - 3 * half)[step]


def is_middle(position):
    return (position + 1) // 2 == 1


def across_middle():
    gy = lax.axis_index("gy")
    return {"gy": 2 * (3 - gy // 2) + gy % 2}


def spot_of(dim, position, offset):
    return along_line(position, offset) if dim == "s" else flip(position, offset)


def remote_to(source, target, send, recv, device):
    return pltpu.make_async_remote_copy(
        src_ref=source,
        dst_ref=target,
        send_sem=send,
        recv_sem=recv,
        device_id=device,
        device_id_type=pl.DeviceIdType.MESH,
    )


def each_piece(rows, columns, body, width=16384):
    step = rows
    while step * columns > width and step % 32 == 0:
        step //= 2
    if step == rows:
        body(slice(None))
        return

    def piece(number, carry):
        body(pl.ds(pl.multiple_of(number * step, step), step))
        return carry

    lax.fori_loop(0, rows // step, piece, 0)


LINE_PEERS = [("s", 1), ("m", 1)]


class Gather:
    def __init__(self, block, order, layout, sizes, merged=""):
        self.value = block
        self.order, self.layout, self.sizes, self.merged = order, layout, sizes, merged
        self.out = jax.ShapeDtypeStruct(tuple(sizes[d] for d in layout) + block.shape, block.dtype)
        self.in_spec = pl.BlockSpec(memory_space=pltpu.VMEM)
        self.out_spec = pl.BlockSpec(memory_space=pl.ANY)
        self.transfers = []
        for level, dim in enumerate(order):
            ranges = [(None,) if d in merged else range(sizes[d]) for d in order[:level]]
            for unit in itertools.product(*ranges):
                for offset in range(1, sizes[dim]):
                    self.transfers.append((level, unit, offset))
        self.index = {transfer: number for number, transfer in enumerate(self.transfers)}
        count = len(self.transfers)
        self.line = order[0] == "s"
        self.scratch = [
            pltpu.SemaphoreType.DMA((count,)),
            pltpu.SemaphoreType.DMA((count,)),
            pltpu.SemaphoreType.DMA,
            pltpu.SemaphoreType.DMA((5,)),
        ]
        self.peers = [(d, offset) for d in order for offset in range(1, sizes[d]) if d != "s"]
        if self.line:
            self.peers += LINE_PEERS

    def prepare(self, refs, place):
        self.source, self.target, self.send, self.recv, self.local_sem, self.line_send = refs
        self.place = place
        self.local = pltpu.make_async_copy(
            self.source, self.target.at[tuple(place[d] for d in self.layout)], self.local_sem
        )
        self.local.start()
        self.local_done = False
        self.arrived = set()
        self.sent = []

    def region(self, level, unit, offset):
        where = dict(self.place)
        for d, moved in zip(self.order[:level], unit):
            where[d] = slice(None) if moved is None else spot_of(d, self.place[d], moved)
        if offset:
            dim = self.order[level]
            where[dim] = spot_of(dim, self.place[dim], offset)
        return self.target.at[tuple(where[d] for d in self.layout)]

    def needs(self, level, unit):
        if level == 0:
            return []
        last, before = unit[-1], unit[:-1]
        if last is None:
            dim = self.order[level - 1]
            return self.needs(level - 1, before) + [
                (level - 1, before, offset) for offset in range(1, self.sizes[dim])
            ]
        if last == 0:
            return self.needs(level - 1, before)
        return [(level - 1, before, last)]

    def arrive(self, transfer):
        if transfer in self.arrived:
            return
        self.arrived.add(transfer)
        level, unit, offset = transfer
        number = self.index[transfer]
        there = self.region(level, unit, offset)
        if self.line and level == 0:
            offset = 1
        remote(
            there, there, self.send.at[number], self.recv.at[number], self.order[level], offset
        ).wait_recv()

    def line_copy(self, number):
        held, there = ((0, 1), (0, 2), (1, 3), (2, 2), (3, 3))[number]
        target = self.region(0, (), held)
        device = peer_of("s", 1) if number in (0, 3, 4) else across_middle()
        recv = self.recv.at[self.index[(0, (), there)]]
        source = target if held else self.source
        return remote_to(source, target, self.line_send.at[number], recv, device)

    def line_first(self):
        self.line_copy(0).start()

        @pl.when(is_middle(self.place["s"]))
        def _():
            self.line_copy(1).start()

    def line_next(self, step):
        self.arrive((0, (), step))

        @pl.when(is_middle(self.place["s"]))
        def _():
            self.line_copy(step + 1).start()

    def launch(self, transfer):
        level, unit, offset = transfer
        number = self.index[transfer]
        for need in self.needs(level, unit):
            self.arrive(need)
        target = self.region(level, unit, 0)
        own = all(moved == 0 for moved in unit)
        if None in unit and not self.local_done:
            self.local.wait()
            self.local_done = True
        copy = remote(
            self.source if own else target,
            target,
            self.send.at[number],
            self.recv.at[number],
            self.order[level],
            offset,
        )
        copy.start()
        self.sent.append(copy)

    def events(self):
        found = []
        if self.line:
            found.append((0, self.line_first))
            for step in (1, 2, 3):
                found.append((step, functools.partial(self.line_next, step)))
        for transfer in self.transfers:
            level, unit, offset = transfer
            if self.line and level == 0:
                continue
            key = 0.1 * level + 0.01 * offset
            for d, moved in zip(self.order, unit):
                key += self.sizes[d] - 1 if moved is None else moved
            found.append((key, functools.partial(self.launch, transfer)))
        return found

    def finish(self):
        if not self.local_done:
            self.local.wait()
        for transfer in self.transfers:
            self.arrive(transfer)
        for copy in self.sent:
            copy.wait_send()
        if self.line:
            self.line_copy(0).wait_send()

            @pl.when(is_middle(self.place["s"]))
            def _():
                for number in range(1, 5):
                    self.line_copy(number).wait_send()


class PackedGather(Gather):
    def __init__(self, values, block, pack, *args):
        super().__init__(block, *args)
        self.values, self.pack = values, pack
        self.scratch = [pltpu.VMEM(block.shape, block.dtype)] + self.scratch


class DirectGather:
    def __init__(self, block, sizes):
        self.value = block
        shape = (sizes["s"], 2)
        self.out = jax.ShapeDtypeStruct(shape + block.shape, block.dtype)
        self.in_spec = pl.BlockSpec(memory_space=pltpu.VMEM)
        self.out_spec = pl.BlockSpec(memory_space=pltpu.VMEM)
        self.offsets = list(itertools.product(*(range(size) for size in shape)))[1:]
        count = len(self.offsets)
        self.scratch = [pltpu.SemaphoreType.DMA((count,)), pltpu.SemaphoreType.DMA((count,))]
        self.peers = [("plane", offset) for offset in self.offsets]

    def prepare(self, refs, place):
        self.source, self.target, self.send, self.recv = refs
        self.place = place
        self.target[place["s"], place["h"]] = self.source[...]

    def copy(self, number, arriving):
        offset = self.offsets[number]
        spot = tuple(
            flip(self.place[d], moved) if arriving else self.place[d] for d, moved in zip("sh", offset)
        )
        return remote_to(
            self.source,
            self.target.at[spot],
            self.send.at[number],
            self.recv.at[number],
            peer_of("plane", offset),
        )

    def events(self):
        return [(0, functools.partial(self.start, number)) for number in range(len(self.offsets))]

    def start(self, number):
        self.copy(number, False).start()

    def finish(self):
        for number in range(len(self.offsets)):
            self.copy(number, True).wait()


class Scatter:
    def __init__(self, value, order, layout, sizes, merged="", out_dtype=f32):
        self.value = value
        self.order, self.layout, self.sizes, self.merged = order, layout, sizes, merged
        self.block = value.shape[len(layout) :]
        self.out = jax.ShapeDtypeStruct(self.block, out_dtype)
        self.in_spec = pl.BlockSpec(memory_space=pltpu.VMEM)
        self.out_spec = pl.BlockSpec(memory_space=pltpu.VMEM)
        self.line = order[-1] == "s"
        self.levels = len(order)
        self.units = []
        self.scratch = []
        self.layouts = [layout]
        for level, dim in enumerate(order):
            later = order[level + 1 :]
            ranges = [(None,) if d in merged else range(sizes[d]) for d in later]
            units = sorted(
                itertools.product(*ranges),
                key=lambda unit: (-(unit[-1] or 0) if unit else 0, -sum(moved or 0 for moved in unit)),
            )
            self.units.append(units)
            left = "".join(d for d in self.layouts[-1] if d != dim)
            self.layouts.append(left)
            self.scratch.append(
                pltpu.VMEM(
                    (5 if dim == "s" else sizes[dim] - 1,)
                    + tuple(sizes[d] for d in left)
                    + self.block,
                    value.dtype,
                )
            )
        self.index = {}
        for level, dim in enumerate(order):
            for unit in self.units[level]:
                for offset in range(1, sizes[dim]):
                    self.index[(level, unit, offset)] = len(self.index)
        count = len(self.index)
        self.scratch += [
            pltpu.SemaphoreType.DMA((count,)),
            pltpu.SemaphoreType.DMA((count,)),
            pltpu.SemaphoreType.DMA((2, 5)),
        ]
        self.peers = [(d, offset) for d in order for offset in range(1, sizes[d]) if d != "s"]
        if self.line:
            self.peers += LINE_PEERS

    def prepare(self, refs, place):
        self.source, self.target = refs[0], refs[1]
        self.landing = refs[2 : 2 + self.levels]
        self.send, self.recv, self.line_sems = refs[2 + self.levels :]
        self.place = place
        self.sent = []

    def held(self, level):
        return self.source if level == 0 else self.landing[level - 1].at[0]

    def later(self, level, unit):
        where = {}
        for d, moved in zip(self.order[level + 1 :], unit):
            where[d] = slice(None) if moved is None else spot_of(d, self.place[d], moved)
        return where

    def copy(self, level, unit, offset):
        number = self.index[(level, unit, offset)]
        dim = self.order[level]
        where = self.later(level, unit)
        landed = self.landing[level].at[
            (offset - 1,) + tuple(where[d] for d in self.layouts[level + 1])
        ]
        where[dim] = flip(self.place[dim], offset)
        source = self.held(level).at[tuple(where[d] for d in self.layouts[level])]
        return remote(source, landed, self.send.at[number], self.recv.at[number], dim, offset)

    def launch(self, level, unit, offset):
        copy = self.copy(level, unit, offset)
        copy.start()
        self.sent.append(copy)

    def reduce(self, level, unit):
        dim = self.order[level]
        size = self.sizes[dim]
        for offset in range(1, size):
            self.copy(level, unit, offset).wait_recv()
        where = self.later(level, unit)
        free = [d for d in self.order[level + 1 :] if isinstance(where[d], slice)]
        total = math.prod(self.sizes[d] for d in free)
        rows, columns = self.block
        last = level == self.levels - 1

        def one(number, carry):
            at = dict(where)
            rest = number
            for d in free:
                at[d] = rest % self.sizes[d]
                rest = rest // self.sizes[d]
            spot = tuple(at[d] for d in self.layouts[level + 1])
            at[dim] = self.place[dim]
            mine = tuple(at[d] for d in self.layouts[level])

            def body(piece):
                if not last and size == 2:
                    self.landing[level][(0,) + spot + (piece,)] += self.held(level)[mine + (piece,)]
                    return
                result = self.held(level)[mine + (piece,)].astype(f32)
                for offset in range(1, size):
                    result = result + self.landing[level][(offset - 1,) + spot + (piece,)].astype(f32)
                if last:
                    self.target[(piece,)] = result.astype(self.target.dtype)
                else:
                    self.landing[level][(0,) + spot + (piece,)] = result.astype(self.landing[level].dtype)

            each_piece(rows, columns, body)
            return carry

        if total == 1:
            one(0, 0)
        else:
            lax.fori_loop(0, total, one, 0)
        if not last and not (self.line and level == self.levels - 2):
            ahead, rest = unit[0], unit[1:]
            if ahead is None:
                offsets = range(1, self.sizes[self.order[level + 1]])
            else:
                offsets = [ahead] if ahead else []
            for offset in offsets:
                self.launch(level + 1, rest, offset)

    def line_copy(self, number):
        step, slot = ((1, 0), (2, 1), (3, 2), (3, 3), (2, 4))[number]
        level = self.levels - 1
        block = self.held(level).at[along_line(self.place["s"], step)]
        landed = self.landing[level].at[slot]
        device = peer_of("s", 1) if number < 3 else across_middle()
        return remote_to(block, landed, self.line_sems.at[0, number], self.line_sems.at[1, number], device)

    def line_step(self, step):
        level = self.levels - 1
        middle = is_middle(self.place["s"])
        rows, columns = self.block
        held, landing = self.held(level), self.landing[level]
        position = along_line(self.place["s"], step)

        if step:
            @pl.when(jnp.logical_not(middle))
            def _():
                self.line_copy(step - 1).start()

            @pl.when(middle)
            def _():
                arrived = (0, 3, 1, 2)[step]
                self.line_copy(arrived).wait_recv()

                def body(piece):
                    held[(position, piece)] += landing[(arrived, piece)]

                each_piece(rows, columns, body)
                self.line_copy((0, 0, 4, 3)[step]).start()

            return

        self.line_copy(0).wait_recv()

        @pl.when(middle)
        def _():
            self.line_copy(4).wait_recv()

            def body(piece):
                result = held[(position, piece)].astype(f32) + landing[(0, piece)].astype(f32)
                self.target[(piece,)] = (result + landing[(4, piece)].astype(f32)).astype(
                    self.target.dtype
                )

            each_piece(rows, columns, body)

        @pl.when(jnp.logical_not(middle))
        def _():
            def body(piece):
                result = held[(position, piece)].astype(f32) + landing[(0, piece)].astype(f32)
                self.target[(piece,)] = result.astype(self.target.dtype)

            each_piece(rows, columns, body)

    def events(self):
        found = []
        for number, unit in enumerate(self.units[0]):
            for offset in range(1, self.sizes[self.order[0]]):
                found.append(
                    (-1 + 0.001 * number, functools.partial(self.launch, 0, unit, offset))
                )
        spread = 4 if self.line else 1
        for level in range(self.levels - self.line):
            count = len(self.units[level])
            for number, unit in enumerate(self.units[level]):
                late = 0
                if self.order[-1] == "a":
                    late = 20 if level == self.levels - 1 else 0.9
                found.append(
                    (late + level + spread * number / count, functools.partial(self.reduce, level, unit))
                )
        if self.line:
            for number, step in enumerate((3, 2, 1, 0)):
                found.append(
                    (self.levels - 1 + number + 0.5, functools.partial(self.line_step, step))
                )
        return found

    def finish(self):
        for copy in self.sent:
            copy.wait_send()
        if self.line:
            self.line_copy(0).wait_send()
            middle = is_middle(self.place["s"])

            @pl.when(middle)
            def _():
                for number in (3, 4):
                    self.line_copy(number).wait_send()

            @pl.when(jnp.logical_not(middle))
            def _():
                for number in (1, 2):
                    self.line_copy(number).wait_send()


class MemoryGather:
    def __init__(self, memory, sizes):
        self.value = memory
        self.sizes = sizes
        self.out = jax.ShapeDtypeStruct((sizes["s"], 2) + memory.shape[1:], memory.dtype)
        self.in_spec = pl.BlockSpec(memory_space=pltpu.VMEM)
        self.out_spec = pl.BlockSpec(memory_space=pl.ANY)
        rows = sizes["s"]
        self.scratch = [
            pltpu.SemaphoreType.DMA((2, rows)),
            pltpu.SemaphoreType.DMA((2, rows)),
            pltpu.SemaphoreType.DMA((2, rows, 2)),
            pltpu.SemaphoreType.DMA,
        ]
        self.peers = [("s", offset) for offset in range(1, rows)] + [("h", 1), ("c", 1)]

    def prepare(self, refs, place):
        self.source, self.target, self.along, self.across, self.core, self.local = refs
        self.place = place
        self.mine = place["s"] % 2 == place["c"]

    def row(self, offset):
        return flip(self.place["s"], offset)

    def along_copy(self, offset, arriving):
        to = self.row(offset)
        spot = to if arriving else self.place["s"]
        return remote(
            self.source.at[self.place["s"] // 2 if arriving else to // 2],
            self.target.at[spot, self.place["h"]],
            self.along.at[0, offset],
            self.along.at[1, offset],
            "s",
            offset,
        )

    def across_copy(self, offset, arriving):
        h = self.place["h"]
        own = self.target.at[self.row(offset), 1 - h if arriving else h]
        if offset == 0 and not arriving:
            source = self.source.at[self.place["s"] // 2]
        else:
            source = own
        return remote(source, own, self.across.at[0, offset], self.across.at[1, offset], "h", 1)

    def core_copy(self, offset, other):
        h = self.place["h"]
        own = self.target.at[self.row(offset), 1 - h if other else h]
        source = self.source.at[self.place["s"] // 2] if offset == 0 and not other else own
        return remote(source, own, self.core.at[0, offset, other], self.core.at[1, offset, other], "c", 1)

    def events(self):
        rows = self.sizes["s"]

        def first():
            for offset in range(1, rows):
                @pl.when(self.row(offset) % 2 == self.place["c"])
                def _():
                    self.along_copy(offset, False).start()

            @pl.when(self.mine)
            def _():
                pltpu.make_async_copy(
                    self.source.at[self.place["s"] // 2],
                    self.target.at[self.place["s"], self.place["h"]],
                    self.local,
                ).start()
                self.across_copy(0, False).start()
                self.core_copy(0, 0).start()

        def arrival(offset):
            @pl.when(self.mine)
            def _():
                self.along_copy(offset, True).wait_recv()
                self.across_copy(offset, False).start()
                self.core_copy(offset, 0).start()

        def other(offset):
            @pl.when(self.mine)
            def _():
                self.across_copy(offset, True).wait_recv()
                self.core_copy(offset, 1).start()

        found = [(0.05, first)]
        for offset in range(1, rows):
            found.append((offset + 0.05, functools.partial(arrival, offset)))
        for offset in range(rows):
            found.append((rows + offset, functools.partial(other, offset)))
        return found

    def finish(self):
        rows = self.sizes["s"]
        for offset in range(1, rows):
            @pl.when(self.row(offset) % 2 == self.place["c"])
            def _():
                self.along_copy(offset, False).wait_send()

        @pl.when(self.mine)
        def _():
            pltpu.make_async_copy(
                self.source.at[self.place["s"] // 2],
                self.target.at[self.place["s"], self.place["h"]],
                self.local,
            ).wait()
            for offset in range(rows):
                self.across_copy(offset, False).wait_send()
                for other in range(2):
                    self.core_copy(offset, other).wait_send()

        @pl.when(jnp.logical_not(self.mine))
        def _():
            for offset in range(rows):
                for other in range(2):
                    self.core_copy(offset, other).wait_recv()


class MemoryScatter:
    def __init__(self, value, sizes):
        self.value = value
        self.sizes = sizes
        rows = sizes["s"]
        self.block = value.shape[2:]
        self.out = jax.ShapeDtypeStruct((2,) + self.block, f32)
        self.in_spec = pl.BlockSpec(memory_space=pltpu.VMEM)
        self.out_spec = pl.BlockSpec(memory_space=pltpu.VMEM)
        self.scratch = [
            pltpu.VMEM(value.shape, value.dtype),
            pltpu.VMEM((rows,) + self.block, value.dtype),
            pltpu.VMEM((2,) + self.block, value.dtype),
            pltpu.SemaphoreType.DMA((2, rows, 2)),
            pltpu.SemaphoreType.DMA((2, rows)),
            pltpu.SemaphoreType.DMA((2, rows)),
        ]
        self.peers = [("s", offset) for offset in range(1, rows)] + [("h", 1), ("c", 1)]

    def prepare(self, refs, place):
        self.source, self.target = refs[0], refs[1]
        self.summed, self.halved, self.landed, self.core, self.across, self.along = refs[2:]
        self.place = place
        self.mine = place["s"] % 2 == place["c"]

    def row(self, offset):
        return flip(self.place["s"], offset)

    def core_copy(self, offset, other):
        h = self.place["h"]
        spot = (self.row(offset), flip(h, 1) if other else h)
        return remote(
            self.source.at[spot],
            self.summed.at[spot],
            self.core.at[0, offset, other],
            self.core.at[1, offset, other],
            "c",
            1,
        )

    def across_copy(self, offset):
        row = self.row(offset)
        return remote(
            self.summed.at[row, flip(self.place["h"], 1)],
            self.halved.at[row],
            self.across.at[0, offset],
            self.across.at[1, offset],
            "h",
            1,
        )

    def along_copy(self, offset, arriving):
        to = self.row(offset)
        return remote(
            self.halved.at[to],
            self.landed.at[to // 2 if arriving else self.place["s"] // 2],
            self.along.at[0, offset],
            self.along.at[1, offset],
            "s",
            offset,
        )

    def events(self):
        rows = self.sizes["s"]
        high, wide = self.block
        orders = list(range(1, rows))[::-1] + [0]

        def first():
            @pl.when(jnp.logical_not(self.mine))
            def _():
                for other in (1, 0):
                    for offset in orders:
                        self.core_copy(offset, other).start()

        def level(offset, other):
            @pl.when(self.mine)
            def _():
                self.core_copy(offset, other).wait_recv()
                h = self.place["h"]
                spot = (self.row(offset), flip(h, 1) if other else h)

                def body(piece):
                    total = self.summed[spot + (piece,)].astype(f32) + self.source[
                        spot + (piece,)
                    ].astype(f32)
                    self.summed[spot + (piece,)] = total.astype(self.summed.dtype)

                each_piece(high, wide, body)
                if other:
                    self.across_copy(offset).start()

        def last(offset):
            @pl.when(self.mine)
            def _():
                self.across_copy(offset).wait_recv()
                row = self.row(offset)

                def body(piece):
                    total = self.halved[(row, piece)].astype(f32) + self.summed[
                        (row, self.place["h"], piece)
                    ].astype(f32)
                    self.halved[(row, piece)] = total.astype(self.halved.dtype)
                    if offset == 0:
                        self.target[(self.place["s"] // 2, piece)] = total

                each_piece(high, wide, body)
                if offset:
                    self.along_copy(offset, False).start()

        found = [(-0.95, first)]
        for number, offset in enumerate(orders):
            found.append((0.05 + 0.1 * number, functools.partial(level, offset, 1)))
        for number, offset in enumerate(orders):
            found.append((0.55 + 0.1 * number, functools.partial(level, offset, 0)))
        for number, offset in enumerate(orders):
            found.append((1.05 + 0.2 * number, functools.partial(last, offset)))
        return found

    def finish(self):
        rows = self.sizes["s"]
        high, wide = self.block
        for offset in range(1, rows):
            @pl.when(self.row(offset) % 2 == self.place["c"])
            def _():
                self.along_copy(offset, True).wait_recv()
                number = self.row(offset) // 2

                def body(piece):
                    self.target[(number, piece)] = self.landed[(number, piece)].astype(f32)

                each_piece(high, wide, body)

        @pl.when(self.mine)
        def _():
            for offset in range(rows):
                self.across_copy(offset).wait_send()
            for offset in range(1, rows):
                self.along_copy(offset, False).wait_send()

        @pl.when(jnp.logical_not(self.mine))
        def _():
            for offset in range(rows):
                for other in range(2):
                    self.core_copy(offset, other).wait_send()


def exchange(name, collective_id, jobs):
    values = [getattr(job, "values", None) or [job.value] for job in jobs]
    peers = []
    for job in jobs:
        for peer in job.peers:
            if peer not in peers:
                peers.append(peer)

    def kernel(*refs):
        total = sum(len(held) for held in values)
        results = refs[total : total + len(jobs)]
        scratch = refs[total + len(jobs) :]
        begin = offset = 0
        barrier = pltpu.get_barrier_semaphore()
        place = coordinates()
        middle = is_middle(place["s"])
        awaited = 0
        for peer in peers:
            if peer[0] == "m":
                @pl.when(middle)
                def _():
                    pl.semaphore_signal(
                        barrier, inc=1, device_id=across_middle(), device_id_type=pl.DeviceIdType.MESH
                    )
                continue
            awaited += 1
            pl.semaphore_signal(
                barrier, inc=1, device_id=peer_of(*peer), device_id_type=pl.DeviceIdType.MESH
            )
        for number, job in enumerate(jobs):
            end = begin + len(values[number])
            ins = refs[begin:end]
            if hasattr(job, "pack"):
                job.pack(ins, scratch[offset])
                ins, offset = (scratch[offset],), offset + 1
            mine = len(job.scratch) - hasattr(job, "pack")
            job.prepare(tuple(ins) + (results[number],) + tuple(scratch[offset : offset + mine]), place)
            begin, offset = end, offset + mine
        if ("m", 1) in peers:
            @pl.when(middle)
            def _():
                pl.semaphore_wait(barrier, awaited + 1)

            @pl.when(jnp.logical_not(middle))
            def _():
                pl.semaphore_wait(barrier, awaited)
        else:
            pl.semaphore_wait(barrier, awaited)
        events = [event for job in jobs for event in job.events()]
        for _, act in sorted(events, key=lambda event: event[0]):
            act()
        for job in jobs:
            job.finish()

    return pl.pallas_call(
        kernel,
        name=name,
        out_shape=tuple(job.out for job in jobs),
        in_specs=[job.in_spec for job, held in zip(jobs, values) for _ in held],
        out_specs=tuple(job.out_spec for job in jobs),
        scratch_shapes=[item for job in jobs for item in job.scratch],
        compiler_params=pltpu.CompilerParams(
            collective_id=collective_id, has_side_effects=True, vmem_limit_bytes=60 * 1024 * 1024
        ),
    )(*[value for held in values for value in held])


def packed(block):
    rows, columns = block.shape
    if rows % 16 == 0:
        return block
    return block.reshape(16, rows * columns // 16)


def bucket_edges():
    edges = []
    for target in range(1, 32):
        if target < 16:
            edges.append(target)
        else:
            found = 0
            for distance in range(16, 4096):
                value = 16 + int(math.log(distance / 16.0) / math.log(8.0) * 16.0)
                if found == 0 and value >= target:
                    found = distance
            edges.append(found)
    return edges


def gelu_tanh(value):
    return (
        0.5
        * value
        * (1.0 + jnp.tanh(0.7978845608028654 * (value + 0.044715 * value * value * value)))
    )


def dot(left, right):
    return jnp.einsum("sd,df->sf", left, right, preferred_element_type=f32)


def dot_t(left, right):
    return jnp.einsum("sf,df->sd", left, right, preferred_element_type=f32)


def t_dot(left, right):
    return jnp.einsum("sd,sf->df", left, right, preferred_element_type=f32)


def distance_table(seq):
    edges = np.array(bucket_edges())
    distance = (-np.arange(seq)) % seq
    bucket = (distance[:, None] >= edges[None, :]).sum(axis=1)
    return (np.arange(128)[:, None] == bucket[None, :]).astype(np.float32)


def mm(left, right):
    return lax.dot_general(left, right, (((1,), (0,)), ((), ())), preferred_element_type=f32)


def mm_t(left, right):
    return lax.dot_general(left, right, (((1,), (1,)), ((), ())), preferred_element_type=f32)


def t_mm(left, right):
    return lax.dot_general(left, right, (((0,), (0,)), ((), ())), preferred_element_type=f32)


def inverse_rms(rows):
    return lax.rsqrt(jnp.mean(rows * rows, axis=-1, keepdims=True) + eps)


def rms_back(rows, gain, slope):
    inverse = inverse_rms(rows)
    unit = rows * inverse
    scaled = slope * gain
    back = inverse * (scaled - unit * jnp.mean(unit * scaled, axis=-1, keepdims=True))
    return back, jnp.sum(slope * unit, axis=0, keepdims=True)


def lanes_of(shape):
    return lax.broadcasted_iota(jnp.int32, shape, len(shape) - 1)


def one_half(pair, half):
    inside = (lanes_of(pair.shape) // HEAD) == half
    return jnp.where(inside, pair, jnp.zeros_like(pair))


def joined(first, second):
    return jnp.where(lanes_of(first.shape) < HEAD, first, second)


def pair_of(ref, start, pair):
    return ref[:, start + 2 * HEAD * pair : start + 2 * HEAD * (pair + 1)]


FF_STEP = 256


def in_steps(total, step, body, further=0):
    def one(number, carry):
        here = pl.ds(pl.multiple_of(number * step, step), step)
        if further:
            body(here, pl.ds(pl.multiple_of(number * step + further, step), step))
        else:
            body(here)
        return carry

    lax.fori_loop(0, total // step, one, 0)


class Fetch:
    def __init__(self, sources, targets, sems):
        self.copies = [
            pltpu.make_async_copy(source, target, sems.at[number])
            for number, (source, target) in enumerate(zip(sources, targets))
        ]
        self.targets = targets
        self.ready = set()
        for copy in self.copies:
            copy.start()

    def __getitem__(self, number):
        if number not in self.ready:
            self.ready.add(number)
            self.copies[number].wait()
        return self.targets[number]


def enter_kernel(resid_ref, part_c_ref, query_ref, kv_ref, normed_ref, gains_ref):
    row = lax.broadcasted_iota(jnp.int32, (16, GAIN_PAD), 0)
    pick = (row == lanes_of((16, GAIN_PAD))).astype(bf16)
    gains = mm_t(pick, part_c_ref[:, 5 * HD : 5 * HD + GAIN_PAD])
    gains_ref[...] = gains
    resid = resid_ref[...]
    normed = (resid * inverse_rms(resid) * gains[0:1]).astype(bf16)
    normed_ref[...] = normed
    query_ref[...] = mm(normed, part_c_ref[:, :HD]).astype(bf16)
    kv_ref[...] = mm(normed, part_c_ref[:, HD : 3 * HD]).astype(bf16)


def biased_scores(scores, row, first, length):
    bias = pltpu.roll(jnp.broadcast_to(row, scores.shape), 0, 1, stride=1, stride_axis=0)
    query_pos = first + lax.broadcasted_iota(jnp.int32, scores.shape, 0)
    key_pos = lanes_of(scores.shape)
    mask = (key_pos <= query_pos) & (key_pos < length)
    return jnp.where(mask, scores + bias, masked_score)


def softmax_parts(scores):
    highest = jnp.max(scores, axis=-1, keepdims=True)
    total = highest + jnp.log(jnp.sum(jnp.exp(scores - highest), axis=-1, keepdims=True))
    return total, jnp.exp(scores - total)


def forward_kernel(
    scalars_ref,
    query_ref,
    kv_ref,
    resid0_ref,
    gains_ref,
    table_ref,
    bias_ref,
    memory_hbm,
    part_a_hbm,
    part_b_hbm,
    part_c_hbm,
    attn_self_ref,
    total_self_ref,
    resid1_ref,
    normed_cross_ref,
    query_cross_ref,
    mem_kv_ref,
    attn_cross_ref,
    total_cross_ref,
    resid2_ref,
    normed_ff_ref,
    gate_up_ref,
    hidden_ref,
    resid3_ref,
    final_ref,
    memory_ref,
    part_a_ref,
    part_b_ref,
    part_c_ref,
    sems,
):
    fetched = Fetch(
        (part_c_hbm, part_b_hbm, memory_hbm, part_a_hbm),
        (part_c_ref, part_b_ref, memory_ref, part_a_ref),
        sems,
    )
    first, length = scalars_ref[0], scalars_ref[1]
    ff = hidden_ref.shape[1]
    bias_rows = pltpu.roll(mm(bias_ref[...], table_ref[...]), first, 1)
    lanes = lanes_of(total_self_ref.shape)
    totals = jnp.zeros(total_self_ref.shape, f32)
    for pair in range(HEADS // 2):
        keys, values = pair_of(kv_ref, 0, pair), pair_of(kv_ref, HD, pair)
        outputs = []
        for half in range(2):
            number = 2 * pair + half
            scores = mm_t(one_half(pair_of(query_ref, 0, pair), half), keys)
            scores = biased_scores(scores, bias_rows[number : number + 1], first, length)
            total, shares = softmax_parts(scores)
            totals = jnp.where(lanes == number, total, totals)
            outputs.append(mm(shares.astype(bf16), values))
        attn_self_ref[:, 2 * HEAD * pair : 2 * HEAD * (pair + 1)] = joined(*outputs).astype(bf16)
    total_self_ref[...] = totals

    part_c = fetched[0]
    resid1 = resid0_ref[...] + mm_t(attn_self_ref[...], part_c[:, 3 * HD : 4 * HD])
    resid1_ref[...] = resid1
    normed = (resid1 * inverse_rms(resid1) * gains_ref[1:2]).astype(bf16)
    normed_cross_ref[...] = normed
    query_cross_ref[...] = mm(normed, part_c[:, 4 * HD : 5 * HD]).astype(bf16)

    part_b = fetched[1]
    memory = fetched[2]
    step = min(256, memory.shape[0])

    def project(number, carry):
        rows = pl.ds(pl.multiple_of(number * step, step), step)
        mem_kv_ref[rows, :] = mm(memory[rows, :], part_b[:, ff : ff + 2 * HD]).astype(bf16)
        return carry

    lax.fori_loop(0, memory.shape[0] // step, project, 0)
    total_cross_ref[...] = jnp.zeros(total_cross_ref.shape, f32)

    def cross_pair(place, place_v):
        keys, values = mem_kv_ref[:, place], mem_kv_ref[:, place_v]
        outputs = []
        for half in range(2):
            scores = mm_t(one_half(query_cross_ref[:, place], half), keys)
            total, shares = softmax_parts(scores)
            number = place.start // HEAD + half
            total_cross_ref[...] = jnp.where(lanes == number, total, total_cross_ref[...])
            outputs.append(mm(shares.astype(bf16), values))
        attn_cross_ref[:, place] = joined(*outputs).astype(bf16)

    in_steps(HD, 2 * HEAD, cross_pair, HD)
    resid2 = resid1_ref[...] + mm_t(attn_cross_ref[...], part_b[:, ff + 2 * HD :])
    resid2_ref[...] = resid2
    normed_ff_ref[...] = (resid2 * inverse_rms(resid2) * gains_ref[2:3]).astype(bf16)

    part_a = fetched[3]

    def feed(here, there):
        gate = mm(normed_ff_ref[...], part_a[:, here])
        up = mm(normed_ff_ref[...], part_a[:, there])
        gate_up_ref[:, here] = gate
        gate_up_ref[:, there] = up
        hidden_ref[:, here] = (gelu_tanh(gate) * up).astype(bf16)

    in_steps(ff, FF_STEP, feed, ff)
    resid3 = resid2_ref[...] + mm_t(hidden_ref[...], part_b[:, :ff])
    resid3_ref[...] = resid3
    final_ref[...] = (resid3 * inverse_rms(resid3) * gains_ref[3:4]).astype(bf16)


def attention_back(query, keys, values, scores, total, out_slope):
    shares = jnp.exp(scores - total)
    share_slope = mm_t(out_slope, values)
    inner = jnp.sum(shares * share_slope, axis=-1, keepdims=True)
    score_slope = shares * (share_slope - inner)
    rounded = score_slope.astype(bf16)
    return (
        rounded,
        mm(rounded, keys),
        t_mm(rounded, query),
        t_mm(shares.astype(bf16), out_slope),
    )


def backward_kernel(
    scalars_ref,
    slope_ref,
    resid3_ref,
    hidden_ref,
    gate_up_ref,
    normed_ff_ref,
    resid2_ref,
    attn_cross_ref,
    query_cross_ref,
    total_cross_ref,
    normed_cross_ref,
    resid1_ref,
    attn_self_ref,
    query_ref,
    kv_ref,
    total_self_ref,
    gains_ref,
    table_ref,
    bias_ref,
    mem_kv_hbm,
    memory_hbm,
    part_a_hbm,
    part_b_hbm,
    part_c_hbm,
    grad_a_hbm,
    grad_b_hbm,
    memory_part_hbm,
    grad_c_ref,
    query_slope_ref,
    kv_slope_ref,
    grad1_ref,
    norm_grads_ref,
    bias_grad_ref,
    mem_kv_ref,
    memory_ref,
    part_a_ref,
    part_b_ref,
    part_c_ref,
    grad_a_ref,
    grad_b_ref,
    memory_part_ref,
    gate_up_slope_ref,
    cross_query_slope_ref,
    cross_kv_slope_ref,
    sems,
    out_sems,
):
    fetched = Fetch(
        (part_b_hbm, part_a_hbm, mem_kv_hbm, memory_hbm, part_c_hbm),
        (part_b_ref, part_a_ref, mem_kv_ref, memory_ref, part_c_ref),
        sems,
    )
    first, length = scalars_ref[0], scalars_ref[1]
    ff = hidden_ref.shape[1]
    width = resid3_ref.shape[1]
    norm_grads_ref[...] = jnp.zeros_like(norm_grads_ref)

    grad3, norm_grad = rms_back(resid3_ref[...], gains_ref[3:4], slope_ref[...])
    norm_grads_ref[3:4] = norm_grad
    down_in = grad3.astype(bf16)
    part_b = fetched[0]

    def feed_back(here, there):
        hidden_slope = mm(down_in, part_b[:, here])
        gate, up = gate_up_ref[:, here], gate_up_ref[:, there]
        inner = jnp.tanh(0.7978845608028654 * (gate + 0.044715 * gate * gate * gate))
        activated = 0.5 * gate * (1.0 + inner)
        steep = 0.5 * (1.0 + inner) + 0.5 * gate * (1.0 - inner * inner) * (
            0.7978845608028654 * (1.0 + 3.0 * 0.044715 * gate * gate)
        )
        gate_up_slope_ref[:, here] = (hidden_slope * up * steep).astype(bf16)
        gate_up_slope_ref[:, there] = (hidden_slope * activated).astype(bf16)
        grad_b_ref[:, here] = t_mm(down_in, hidden_ref[:, here]).astype(bf16)

    in_steps(ff, FF_STEP, feed_back, ff)
    part_a = fetched[1]
    back, norm_grad = rms_back(
        resid2_ref[...], gains_ref[2:3], mm_t(gate_up_slope_ref[...], part_a[...])
    )
    norm_grads_ref[2:3] = norm_grad
    grad2 = grad3 + back

    def gate_up_grad(here):
        grad_a_ref[:, here] = t_mm(normed_ff_ref[...], gate_up_slope_ref[:, here]).astype(bf16)

    in_steps(2 * ff, 2 * FF_STEP, gate_up_grad)
    copy_a = pltpu.make_async_copy(grad_a_ref, grad_a_hbm, out_sems.at[0])
    copy_a.start()

    cross_in = grad2.astype(bf16)
    grad_b_ref[:, ff + 2 * HD :] = t_mm(cross_in, attn_cross_ref[...]).astype(bf16)
    out_slope = mm(cross_in, part_b[:, ff + 2 * HD :]).astype(bf16)
    mem_kv = fetched[2]
    cross_query_slope_ref[...] = out_slope

    def cross_pair_back(place, place_v):
        keys, values = mem_kv[:, place], mem_kv[:, place_v]
        parts = []
        for half in range(2):
            lanes = lanes_of(total_cross_ref.shape)
            total = jnp.where(lanes == place.start // HEAD + half, total_cross_ref[...], 0.0)
            query = one_half(query_cross_ref[:, place], half)
            parts.append(
                attention_back(
                    query,
                    keys,
                    values,
                    mm_t(query, keys),
                    jnp.sum(total, axis=-1, keepdims=True),
                    one_half(cross_query_slope_ref[:, place], half),
                )
            )
        cross_query_slope_ref[:, place] = joined(parts[0][1], parts[1][1]).astype(bf16)
        cross_kv_slope_ref[:, place] = (parts[0][2] + parts[1][2]).astype(bf16)
        cross_kv_slope_ref[:, place_v] = (parts[0][3] + parts[1][3]).astype(bf16)

    in_steps(HD, 2 * HEAD, cross_pair_back, HD)
    memory = fetched[3]

    def memory_weights(here, there):
        grad_b_ref[:, there] = t_mm(memory[...], cross_kv_slope_ref[:, here]).astype(bf16)

    in_steps(2 * HD, FF_STEP, memory_weights, ff)
    copy_b = pltpu.make_async_copy(grad_b_ref, grad_b_hbm, out_sems.at[1])
    copy_b.start()
    step = min(256, memory.shape[0])

    def project(number, carry):
        rows = pl.ds(pl.multiple_of(number * step, step), step)
        memory_part_ref[rows, :] = mm_t(
            cross_kv_slope_ref[rows, :], part_b[:, ff : ff + 2 * HD]
        ).astype(bf16)
        return carry

    lax.fori_loop(0, memory.shape[0] // step, project, 0)
    copy_m = pltpu.make_async_copy(memory_part_ref, memory_part_hbm, out_sems.at[2])
    copy_m.start()
    part_c = fetched[4]
    query_slope = cross_query_slope_ref[...]
    grad_c_ref[:, HD : 2 * HD] = t_mm(normed_cross_ref[...], query_slope).astype(bf16)
    back, norm_grad = rms_back(
        resid1_ref[...], gains_ref[1:2], mm_t(query_slope, part_c[:, 4 * HD : 5 * HD])
    )
    norm_grads_ref[1:2] = norm_grad
    grad1 = grad2 + back
    grad1_ref[...] = grad1

    self_in = grad1.astype(bf16)
    grad_c_ref[:, :HD] = t_mm(self_in, attn_self_ref[...]).astype(bf16)
    out_slope = mm(self_in, part_c[:, 3 * HD : 4 * HD]).astype(bf16)
    bias_rows = pltpu.roll(mm(bias_ref[...], table_ref[...]), first, 1)
    bias_sums = jnp.zeros(bias_rows.shape, f32)
    rows, seq = query_ref.shape[0], kv_ref.shape[0]
    reverse = lax.broadcasted_iota(jnp.int32, (rows, rows), 0) + lanes_of((rows, rows)) == rows - 1
    reverse = reverse.astype(bf16)
    for pair in range(HEADS // 2):
        place = slice(2 * HEAD * pair, 2 * HEAD * (pair + 1))
        place_v = slice(HD + 2 * HEAD * pair, HD + 2 * HEAD * (pair + 1))
        keys, values = kv_ref[:, place], kv_ref[:, place_v]
        parts = []
        for half in range(2):
            number = 2 * pair + half
            query = one_half(query_ref[:, place], half)
            scores = biased_scores(
                mm_t(query, keys), bias_rows[number : number + 1], first, length
            )
            part = attention_back(
                query,
                keys,
                values,
                scores,
                total_self_ref[:, number : number + 1],
                one_half(out_slope[:, place], half),
            )
            parts.append(part)
            turned = pltpu.roll(mm(reverse, part[0]), 0, 1, stride=1, stride_axis=0)
            where = lax.broadcasted_iota(jnp.int32, bias_sums.shape, 0) == number
            bias_sums = jnp.where(where, jnp.sum(turned, axis=0, keepdims=True), bias_sums)
        query_slope_ref[:, place] = joined(parts[0][1], parts[1][1]).astype(bf16)
        kv_slope_ref[:, place] = (parts[0][2] + parts[1][2]).astype(bf16)
        kv_slope_ref[:, place_v] = (parts[0][3] + parts[1][3]).astype(bf16)
    bias_sums = pltpu.roll(bias_sums, 2 * seq + 1 - rows - first, 1)
    high = bias_sums.astype(bf16)
    rest = bias_sums - high.astype(f32)
    middle = rest.astype(bf16)
    low = (rest - middle.astype(f32)).astype(bf16)
    table = table_ref[...]
    bias_grad_ref[...] = mm_t(high, table) + (mm_t(middle, table) + mm_t(low, table))
    copy_a.wait()
    copy_b.wait()
    copy_m.wait()


def leave_kernel(
    query_slope_ref,
    kv_slope_ref,
    normed_ref,
    resid0_ref,
    grad1_ref,
    gains_ref,
    norm_grads_ref,
    part_grad_ref,
    part_c_ref,
    grad_c_ref,
    grad0_ref,
):
    normed = normed_ref[...]
    query_slope, kv_slope = query_slope_ref[...], kv_slope_ref[...]
    slope = mm_t(query_slope, part_c_ref[:, :HD]) + mm_t(kv_slope, part_c_ref[:, HD : 3 * HD])
    back, norm_grad = rms_back(resid0_ref[...], gains_ref[0:1], slope)
    grad0_ref[...] = (grad1_ref[...] + back).astype(bf16)
    grad_c_ref[:, :HD] = t_mm(normed, query_slope).astype(bf16)
    grad_c_ref[:, HD : 3 * HD] = t_mm(normed, kv_slope).astype(bf16)
    grad_c_ref[:, 3 * HD : 5 * HD] = part_grad_ref[...]
    where = lax.broadcasted_iota(jnp.int32, norm_grads_ref.shape, 0) == 0
    norm_grads = jnp.where(where, norm_grad, norm_grads_ref[...]).astype(bf16)
    row = lax.broadcasted_iota(jnp.int32, (norm_grads.shape[0], GAIN_PAD), 0)
    spread = (row == lanes_of(row.shape)).astype(bf16)
    grad_c_ref[:, 5 * HD :] = t_mm(norm_grads, spread).astype(bf16)


def local_kernel(name, kernel, outs, args, spaces="", out_spaces="", scratch=()):
    space = {"v": pltpu.VMEM, "s": pltpu.SMEM, "a": pl.ANY}
    spaces = spaces or "v" * len(args)
    out_spaces = out_spaces or "v" * len(outs)
    return pl.pallas_call(
        kernel,
        name=name,
        out_shape=tuple(jax.ShapeDtypeStruct(shape, dtype) for shape, dtype in outs),
        in_specs=[pl.BlockSpec(memory_space=space[letter]) for letter in spaces],
        out_specs=tuple(pl.BlockSpec(memory_space=space[letter]) for letter in out_spaces),
        scratch_shapes=list(scratch),
        compiler_params=pltpu.CompilerParams(vmem_limit_bytes=60 * 1024 * 1024),
    )(*args)


def pack_columns(pieces, block):
    start = 0
    for piece in pieces:
        if piece.shape[0] == 1:
            break
        block[:, start : start + piece.shape[1]] = piece[...]
        start += piece.shape[1]
    gains = pieces[-4:]
    if gains[0].shape[0] == 1:
        rows = gains[0].shape[1]
        where = lax.broadcasted_iota(jnp.int32, (16, rows), 0)
        stacked = jnp.zeros((16, rows), f32)
        for number, gain in enumerate(gains):
            stacked = jnp.where(where == number, gain[...].astype(f32), stacked)
        pick = lax.broadcasted_iota(jnp.int32, (16, GAIN_PAD), 0) == lanes_of((16, GAIN_PAD))
        block[:, start:] = t_mm(stacked.astype(bf16), pick.astype(bf16)).astype(bf16)


def pack_ids(pieces, block):
    block[...] = jnp.zeros_like(block)
    for number, piece in enumerate(pieces):
        micro, _, count = piece.shape
        for which in range(micro):
            block[micro * number + which : micro * number + which + 1, :count] = piece[which]


def tail_kernel(lengths_ref, *refs):
    (a_ref, b_ref, c_ref, small_ref, memory_ref, embedding_ref, head_ref), outs = refs[:7], refs[7:]
    (loss_ref, memory_out, embedding_out, head_out, bias_out), outs = outs[:5], outs[5:]
    memory_out[...] = memory_ref[...]
    embedding_out[...] = embedding_ref[...]
    head_out[...] = head_ref[...]
    total = jnp.sum(small_ref[...], axis=0)
    count = 0
    for first in range(lengths_ref.shape[0]):
        for second in range(lengths_ref.shape[1]):
            count = count + lengths_ref[first, second]
    loss_ref[...] = total[0:1, 64:65] / count.astype(f32)
    bias_out[...] = total[:HEADS, :BUCKETS]
    for ref, pieces in ((a_ref, outs[:2]), (b_ref, outs[2:6]), (c_ref, outs[6:11])):
        start = 0
        for piece in pieces:
            piece[...] = ref[:, start : start + piece.shape[1]]
            start += piece.shape[1]
    turned = jnp.transpose(c_ref[:, 5 * HD :])
    for number, piece in enumerate(outs[11:]):
        piece[...] = turned[number : number + 1]


def per_device(
    target_ids,
    labels,
    lengths,
    memory,
    embedding,
    head,
    gain_self,
    w_query,
    w_key,
    w_value,
    w_out,
    relative_bias,
    gain_cross,
    c_query,
    c_key,
    c_value,
    c_out,
    gain_ff,
    w_gate,
    w_up,
    w_down,
    gain_final,
):
    micro = target_ids.shape[0]
    seq_dev = target_ids.shape[2]
    mem_dev = memory.shape[2]
    voc_dev, width = embedding.shape
    ff = w_gate.shape[1]
    n_gx = lax.axis_size("gx")
    n_gy = lax.axis_size("gy")
    column = lax.axis_index("gy")
    row_group = lax.axis_index("gx")
    devices = n_gx * n_gy
    sizes = {"a": n_gx // 2, "c": 2, "s": n_gy // 2, "h": 2}
    assert sizes["s"] == 2 * micro
    place = coordinates()
    seq = seq_dev * n_gy
    plane = sizes["s"] * seq
    tok_dev = seq // 4
    tokens = plane // 2
    span = n_gx * voc_dev
    merged = "" if sizes["a"] == 2 else "ashc"

    rows_dev = width // devices
    whole_tiles = rows_dev % 16 == 0
    groups = (
        (w_gate, w_up),
        (w_down, c_key, c_value, c_out),
        (w_query, w_key, w_value, w_out, c_query),
    )
    gains = (gain_self, gain_cross, gain_ff, gain_final)
    widths = [sum(piece.shape[1] for piece in group) for group in groups]
    widths[2] += GAIN_PAD
    orders = ("shac", "sahc", "sahc")
    if whole_tiles:
        operands = list(groups)
        operands[2] += tuple(gain.reshape(1, rows_dev) for gain in gains)
        weights = [
            PackedGather(
                group,
                jax.ShapeDtypeStruct((rows_dev, count), bf16),
                pack_columns,
                order,
                "acsh",
                sizes,
                merged,
            )
            for group, count, order in zip(operands, widths, orders)
        ]
    else:
        shards = [jnp.concatenate(group, axis=1) for group in groups]
        columns_of = jnp.pad(jnp.stack(gains, axis=1), ((0, 0), (0, GAIN_PAD - 4)))
        shards[2] = jnp.concatenate([shards[2], columns_of], axis=1)
        weights = [
            Gather(packed(part), order, "acsh", sizes, merged) for part, order in zip(shards, orders)
        ]
    part_a, part_b, part_c, embed_rows, ids, memory_all = exchange(
        "gather_weights",
        0,
        weights
        + [
            Gather(embedding, "ac", "ac", sizes),
            PackedGather(
                (target_ids, labels),
                jax.ShapeDtypeStruct((8, 128), jnp.int32),
                pack_ids,
                "shc",
                "shc",
                sizes,
                "shc",
            ),
            MemoryGather(memory.reshape(micro, mem_dev, width), sizes),
        ],
    )
    part_a, part_b, part_c = (
        full.reshape(width, count) for full, count in zip((part_a, part_b, part_c), widths)
    )
    embed_rows = embed_rows.reshape(span, width)
    memory_all = memory_all.reshape(n_gy * mem_dev, width)
    ids = ids[..., : 2 * micro, :seq_dev].reshape(n_gy, 2, 2, micro, seq_dev)
    ids = ids.transpose(2, 3, 1, 0, 4).reshape(2, sizes["s"] * 2, 2, tok_dev)
    ids = lax.dynamic_index_in_dim(ids, place["c"], axis=2, keepdims=False).reshape(2, tokens)

    def local_of(index):
        shard = index // voc_dev
        return jnp.where(shard % n_gy == column, shard // n_gy * voc_dev + index % voc_dev, -1)

    local_ids = local_of(ids[0])
    targets = local_of(ids[1])
    columns = jnp.arange(span, dtype=jnp.int32)

    picked_rows = dot((local_ids[:, None] == columns[None, :]).astype(bf16), embed_rows).astype(bf16)
    tok_layout = (sizes["s"], 2, tok_dev, width)
    resid0, head_rows = exchange(
        "rows",
        1,
        [
            Scatter(picked_rows.reshape(tok_layout), "hs", "sh", sizes),
            Gather(head, "ac", "ac", sizes),
        ],
    )
    head_rows = head_rows.reshape(span, width)

    plane_lengths = lax.dynamic_slice_in_dim(lengths, 2 * place["a"], 2, axis=1).reshape(-1)
    live_length = lax.dynamic_index_in_dim(plane_lengths, place["s"], keepdims=False)
    scalars = jnp.stack([(2 * place["h"] + place["c"]) * tok_dev, live_length])
    table = jnp.asarray(distance_table(seq), bf16)
    bias_pad = jnp.pad(relative_bias, ((0, 8 - HEADS), (0, 128 - BUCKETS)))
    query_self, own_kv, normed_self, gain_rows = local_kernel(
        "enter",
        enter_kernel,
        [((tok_dev, HD), bf16), ((tok_dev, 2 * HD), bf16), ((tok_dev, width), bf16), ((16, width), f32)],
        [resid0, part_c],
    )
    (self_kv_all,) = exchange("self_keys", 2, [Gather(own_kv, "hc", "hc", sizes)])
    self_kv_all = self_kv_all.reshape(seq, 2 * HD)
    rows_f32, rows_bf16, rows_heads = ((tok_dev, width), f32), ((tok_dev, width), bf16), ((tok_dev, HD), bf16)
    totals_shape = ((tok_dev, 128), f32)
    all_mem = n_gy * mem_dev
    (
        attn_self,
        total_self,
        resid1,
        normed_cross,
        query_cross,
        mem_kv,
        attn_cross,
        total_cross,
        resid2,
        normed_ff,
        gate_up,
        hidden,
        resid3,
        final_rows,
    ) = local_kernel(
        "forward",
        forward_kernel,
        [
            rows_heads,
            totals_shape,
            rows_f32,
            rows_bf16,
            rows_heads,
            ((all_mem, 2 * HD), bf16),
            rows_heads,
            totals_shape,
            rows_f32,
            rows_bf16,
            ((tok_dev, 2 * ff), f32),
            ((tok_dev, ff), bf16),
            rows_f32,
            rows_bf16,
        ],
        [scalars, query_self, self_kv_all, resid0, gain_rows, table, bias_pad]
        + [memory_all, part_a, part_b, part_c],
        "svvvvvvaaaa",
        scratch=[pltpu.VMEM(full.shape, bf16) for full in (memory_all, part_a, part_b, part_c)]
        + [pltpu.SemaphoreType.DMA((4,))],
    )

    (states,) = exchange("final_rows", 3, [Gather(final_rows, "sh", "sh", sizes, merged)])
    states = states.reshape(tokens, width)
    logits = dot_t(states, head_rows)
    highest = jnp.max(logits, axis=1)
    own_total = highest + jnp.log(jnp.sum(jnp.exp(logits - highest[:, None]), axis=1))
    (totals,) = exchange("totals", 4, [DirectGather(own_total.reshape(tokens // 128, 128), sizes)])
    totals = totals.reshape(n_gy, tokens)
    top = jnp.max(totals, axis=0)
    log_total = top + jnp.log(jnp.sum(jnp.exp(totals - top[None]), axis=0))
    index = jnp.arange(tokens, dtype=jnp.int32)
    position = (2 * (index // tok_dev % 2) + place["c"]) * tok_dev + index % tok_dev
    alive = (position < jnp.repeat(plane_lengths, 2 * tok_dev)).astype(f32)
    hit = columns[None, :] == targets[:, None]
    picked = jnp.sum(jnp.where(hit, logits, 0.0), axis=1)
    loss_part = jnp.where(column == 0, jnp.sum(alive * log_total), 0.0) - jnp.sum(alive * picked)
    slope = ((jnp.exp(logits - log_total[:, None]) - hit.astype(f32)) * alive[:, None]).astype(bf16)
    head_part = t_dot(slope, states).astype(bf16)
    final_part = dot(slope, head_rows).astype(bf16)
    final_slope, head_grad = exchange(
        "final_slopes",
        5,
        [
            Scatter(final_part.reshape(tok_layout), "hs", "sh", sizes),
            Scatter(head_part.reshape(sizes["a"], 2, voc_dev, width), "ca", "ac", sizes),
        ],
    )

    grad_a, grad_b, memory_part, part_grad_c, query_slope, kv_slope, grad1, norm_grads, bias_grad = (
        local_kernel(
            "backward",
            backward_kernel,
            [
                (part_a.shape, bf16),
                (part_b.shape, bf16),
                (memory_all.shape, bf16),
                ((width, 2 * HD), bf16),
                rows_heads,
                ((seq, 2 * HD), bf16),
                rows_f32,
                (gain_rows.shape, f32),
                ((8, 128), f32),
            ],
            [scalars, final_slope, resid3, hidden, gate_up, normed_ff, resid2, attn_cross]
            + [query_cross, total_cross, normed_cross, resid1, attn_self, query_self, self_kv_all]
            + [total_self, gain_rows, table, bias_pad, mem_kv, memory_all, part_a, part_b, part_c],
            "s" + "v" * 18 + "a" * 5,
            "aaa" + "v" * 6,
            [
                pltpu.VMEM(full.shape, bf16)
                for full in (mem_kv, memory_all, part_a, part_b, part_c, part_a, part_b, memory_all)
            ]
            + [
                pltpu.VMEM((tok_dev, 2 * ff), bf16),
                pltpu.VMEM((tok_dev, HD), bf16),
                pltpu.VMEM(mem_kv.shape, bf16),
                pltpu.SemaphoreType.DMA((5,)),
                pltpu.SemaphoreType.DMA((3,)),
            ],
        )
    )
    (kv_slope,) = exchange(
        "key_slopes",
        6,
        [Scatter(kv_slope.reshape(2, 2, tok_dev, 2 * HD), "ch", "hc", sizes, "", bf16)],
    )
    grad_c, grad0 = local_kernel(
        "leave",
        leave_kernel,
        [(part_c.shape, bf16), rows_bf16],
        [query_slope, kv_slope, normed_self, resid0, grad1, gain_rows, norm_grads, part_grad_c, part_c],
    )
    (slopes,) = exchange("row_slopes", 7, [Gather(grad0, "sh", "sh", sizes, merged)])
    embed_part = t_dot(
        (local_ids[:, None] == columns[None, :]).astype(bf16), slopes.reshape(tokens, width)
    ).astype(bf16)
    sums = (grad_a, grad_b, grad_c)
    at_loss = (jnp.arange(8)[:, None] == 0) & (jnp.arange(128)[None, :] == 64)
    small = jnp.where(at_loss, loss_part, bias_grad)
    device_layout = (sizes["a"], 2, sizes["s"], 2)
    blocks = [part.reshape(device_layout + packed_shape(part, devices)) for part in sums]
    grad_a, grad_b, grad_c, embedding_grad, memory_grad, small = exchange(
        "scatter_weights",
        8,
        [
            Scatter(part, order[::-1], "acsh", sizes, merged)
            for part, order in zip(blocks, orders)
        ]
        + [
            Scatter(embed_part.reshape(sizes["a"], 2, voc_dev, width), "ca", "ac", sizes),
            MemoryScatter(memory_part.reshape(sizes["s"], 2, mem_dev, width), sizes),
            Gather(small, "shac", "acsh", sizes, "ashc"),
        ],
    )
    small = small.reshape(devices, 8, 128)
    memory_grad = memory_grad.reshape(micro, 1, mem_dev, width)
    if whole_tiles:
        pieces = [piece.shape[1] for group in groups for piece in group]
        outs = [
            ((1, 1), f32),
            (memory_grad.shape, f32),
            (embedding_grad.shape, f32),
            (head_grad.shape, f32),
            ((HEADS, BUCKETS), f32),
        ]
        outs += [((rows_dev, count), f32) for count in pieces] + [((1, rows_dev), f32)] * 4
        results = local_kernel(
            "tail",
            tail_kernel,
            outs,
            [lengths, grad_a, grad_b, grad_c, small, memory_grad, embedding_grad, head_grad],
            "s" + "v" * 7,
        )
        loss, memory_grad, embedding_grad, head_grad, bias_total = results[:5]
        loss = loss.reshape(())
        cut = results[5:16]
        gain_out = [gain.reshape(rows_dev) for gain in results[16:]]
    else:
        grad_a, grad_b, grad_c = (
            grad.reshape(rows_dev, count) for grad, count in zip((grad_a, grad_b, grad_c), widths)
        )
        small = jnp.sum(small, axis=0)
        loss = small[0, 64] / jnp.sum(lengths).astype(f32)
        bias_total = small[:HEADS, :BUCKETS]
        cut = []
        for grad, group in zip((grad_a, grad_b, grad_c), groups):
            start = 0
            for piece in group:
                cut.append(grad[:, start : start + piece.shape[1]])
                start += piece.shape[1]
        gain_out = [grad_c[:, 5 * HD + number] for number in range(4)]
    gate_grad, up_grad, down_grad, c_key_grad, c_value_grad, c_out_grad = cut[:6]
    query_grad, key_grad, value_grad, out_grad, c_query_grad = cut[6:]
    return (
        loss,
        memory_grad,
        embedding_grad,
        head_grad,
        gain_out[0],
        query_grad,
        key_grad,
        value_grad,
        out_grad,
        bias_total,
        gain_out[1],
        c_query_grad,
        c_key_grad,
        c_value_grad,
        c_out_grad,
        gain_out[2],
        gate_grad,
        up_grad,
        down_grad,
        gain_out[3],
    )


def packed_shape(part, count):
    rows, columns = part.shape[0] // count, part.shape[1]
    if rows % 16 == 0:
        return (rows, columns)
    return (16, rows * columns // 16)


def solution(mesh):
    placed = (
        P(None, "gx", "gy"),
        P(None, "gx", "gy"),
        P(),
        P(None, "gx", "gy", None),
        P(("gx", "gy"), None),
        P(("gx", "gy"), None),
        P(("gx", "gy")),
        P(("gx", "gy"), None),
        P(("gx", "gy"), None),
        P(("gx", "gy"), None),
        P(("gx", "gy"), None),
        P(),
        P(("gx", "gy")),
        P(("gx", "gy"), None),
        P(("gx", "gy"), None),
        P(("gx", "gy"), None),
        P(("gx", "gy"), None),
        P(("gx", "gy")),
        P(("gx", "gy"), None),
        P(("gx", "gy"), None),
        P(("gx", "gy"), None),
        P(("gx", "gy")),
    )
    return jax.shard_map(
        per_device,
        mesh=mesh,
        in_specs=placed,
        out_specs=(
            P(),
            P(None, "gx", "gy", None),
            P(("gx", "gy"), None),
            P(("gx", "gy"), None),
            P(("gx", "gy")),
            P(("gx", "gy"), None),
            P(("gx", "gy"), None),
            P(("gx", "gy"), None),
            P(("gx", "gy"), None),
            P(),
            P(("gx", "gy")),
            P(("gx", "gy"), None),
            P(("gx", "gy"), None),
            P(("gx", "gy"), None),
            P(("gx", "gy"), None),
            P(("gx", "gy")),
            P(("gx", "gy"), None),
            P(("gx", "gy"), None),
            P(("gx", "gy"), None),
            P(("gx", "gy")),
        ),
        check_vma=False,
    )
```

profile of v0, /device:TPU:0, one launch (start us, length us, event | category | flops | bytes accessed | tf_op | source)
XLA Modules:
  0.0 323.0 jit_solution(18432338079587663051)
XLA Ops:
  0.7 54.1 %gather_weights.1 = (bf16[2,2,4,2,16,2048]{5,4,3,2,1,0:T(8,128)(2,1)}, bf16[2,2,4,2,16,2176]{5,4,3,2,1,0:T(8,128)(2,1)}, bf16[2,2,4,2,16,2048]{5,4,3,2,1,0:T(8,1...) custom-call(bf16[16,1024]{1,0:T(8,128)(2,1)} %refs_0_.1, ...), custom_call_target="tpu_custom_call" | custom-call | tf_op jit(solution)/shard_map/gather_weights/pallas_call | solution.py:847
  54.8 0.8 slice.11
  55.6 0.1 reshape.440
  55.8 4.9 %fusion.5 = bf16[1024,512]{1,0:T(8,128)(2,1)} fusion(bf16[2048,512]{1,0:T(8,128)(2,1)} %bitcast.99, s32[1024]{0:T(1024)S(1)} %get-tuple-element.158), kind=kOutput, calls=%fused_computation.11 | convolution fusion | flops 2150105088 | bytes 3149824 | tf_op jit(solution)/shard_map/sd,df->sf/dot_general | solution.py:891
  60.7 0.0 copy-start.2
  60.7 0.0 copy-start.3
  60.7 33.1 %rows.1 = (f32[128,512]{1,0:T(8,128)}, bf16[2,2,512,512]{3,2,1,0:T(8,128)(2,1)}) custom-call(bf16[4,2,128,512]{3,2,1,0:T(8,128)(2,1)} %bitcast.79, bf16[512,512]{1,0:T(8,128)(2,1)} %refs_1_.3), custom_call_target="tpu_custom_call" | custom-call | tf_op jit(solution)/shard_map/rows/pallas_call | solution.py:847
  93.8 2.9 enter.1
  96.7 9.6 %self_keys.1 = bf16[2,2,128,768]{3,2,1,0:T(8,128)(2,1)} custom-call(bf16[128,768]{1,0:T(8,128)(2,1)} %get-tuple-element.90.refs_0_), custom_call_target="tpu_custom_call" | custom-call | tf_op jit(solution)/shard_map/self_keys/pallas_call | solution.py:847
  106.4 0.0 copy-done.2
  106.4 0.1 constant_dynamic-slice_fusion.2
  106.5 0.1 reshape.433
  106.6 0.6 dynamic_slice.12
  107.1 1.2 pad_add_fusion.scalars_ref
  108.4 0.0 copy-done.3
  108.4 0.6 pad.4.bias_ref
  109.0 0.0 copy-start.4
  109.0 14.0 %forward.1 = (bf16[128,384]{1,0:T(8,128)(2,1)}, f32[128,128]{1,0:T(8,128)}, f32[128,512]{1,0:T(8,128)}, bf16[128,512]{1,0:T(8,128)(2,1)}, bf16[128,384]{1,0:T(8,...) custom-call(s32[2]{0:T(128)} %pad_add_fusion.scalars_ref, ...), custom_call_target="tpu_custom_call" | custom-call | tf_op jit(solution)/shard_map/forward/pallas_call | solution.py:1354
  123.0 20.8 %final_rows.1 = bf16[4,2,128,512]{3,2,1,0:T(8,128)(2,1)} custom-call(bf16[128,512]{1,0:T(8,128)(2,1)} %get-tuple-element.95.refs_0_), custom_call_target="tpu_custom_call" | custom-call | tf_op jit(solution)/shard_map/final_rows/pallas_call | solution.py:847
  143.8 0.0 copy-done.4
  143.8 3.7 %fusion.49 = (f32[1024]{0:T(1024)S(1)}, f32[1024,2048]{1,0:T(8,128)S(1)}) fusion(bf16[1024,512]{1,0:T(8,128)(2,1)} %bitcast.77, bf16[2048,512]{1,0:T(8,128)(2,1)S(1)} %bitcast.97), kind=kOutput, calls=%fused_computation.122 | convolution fusion | flops 2149579776 | bytes 11538432 | tf_op jit(solution)/shard_map/sf,df->sd/dot_general | solution.py:895
  147.5 0.0 copy-start
  147.5 3.2 select_reduce_fusion
  150.7 0.0 copy-done
  150.7 0.1 broadcast_bitcast_fusion
  150.8 0.6 select_reduce_fusion.1
  151.4 0.6 add_bitcast_fusion.1.refs_0_
  152.0 7.9 %totals.1 = f32[4,2,8,128]{3,2,1,0:T(8,128)} custom-call(f32[8,128]{1,0:T(8,128)} %add_bitcast_fusion.1.refs_0_), custom_call_target="tpu_custom_call" | custom-call | tf_op jit(solution)/shard_map/totals/pallas_call | solution.py:847
  160.0 0.8 reduce_max.19
  160.7 0.8 exponential_reduce_fusion.1
  161.5 0.1 broadcast_in_dim.33
  161.6 0.1 broadcast_in_dim.34
  161.7 0.1 iota.165
  161.8 0.7 select_reduce_fusion.2
  163.8 0.0 copy-start.1
  163.8 5.1 %multiply_convert_fusion = bf16[1024,2048]{1,0:T(8,128)(2,1)S(1)} fusion(f32[1024,2048]{1,0:T(8,128)} %copy-done, f32[1024]{0:T(1024)S(1)} %fusion.45, s32[1024]{0:T(1024)S(1)} %get-tuple-element.159, f32[1024]{0:T(1024)S(1)} %get-tuple-element.155), kind=kLoop, calls=%fused_computation.1 | loop fusion | flops 12582912 | bytes 12595200 | tf_op jit(solution)/shard_map/convert_element_type | solution.py:1610
  168.9 0.0 copy-done.1
  168.9 3.7 %convolution_convert_fusion = bf16[2048,512]{1,0:T(8,128)(2,1)} fusion(bf16[1024,2048]{1,0:T(8,128)(2,1)S(1)} %multiply_convert_fusion, bf16[1024,512]{1,0:T(8,128)(2,1)S(1)} %bitcast.78), kind=kOutput, calls=%fused_computation.9 | convolution fusion | flops 2148532224 | bytes 7340032 | tf_op jit(solution)/shard_map/sd,sf->df/dot_general | solution.py:899
  172.7 3.3 %convolution_convert_fusion.1 = bf16[1024,512]{1,0:T(8,128)(2,1)} fusion(bf16[1024,2048]{1,0:T(8,128)(2,1)S(1)} %multiply_convert_fusion, bf16[2048,512]{1,0:T(8,128)(2,1)S(1)} %bitcast.98), kind=kOutput, calls=%fused_computation.12 | convolution fusion | flops 2148007936 | bytes 7340032 | tf_op jit(solution)/shard_map/sd,df->sf/dot_general | solution.py:891
  176.0 24.6 %final_slopes.1 = (f32[128,512]{1,0:T(8,128)}, f32[512,512]{1,0:T(8,128)}) custom-call(bf16[4,2,128,512]{3,2,1,0:T(8,128)(2,1)} %bitcast.76, bf16[2,2,512,512]{3,2,1,0:T(8,128)(2,1)} %bitcast.71), custom_call_target="tpu_custom_call" | custom-call | tf_op jit(solution)/shard_map/final_slopes/pallas_call | solution.py:847
  200.5 20.1 %backward.1 = (bf16[512,2048]{1,0:T(8,128)(2,1)}, bf16[512,2176]{1,0:T(8,128)(2,1)}, bf16[1024,512]{1,0:T(8,128)(2,1)}, bf16[512,768]{1,0:T(8,128)(2,1)}, bf16[1...) custom-call(s32[2]{0:T(128)} %pad_add_fusion.scalars_ref, ...), custom_call_target="tpu_custom_call" | custom-call | tf_op jit(solution)/shard_map/backward/pallas_call | solution.py:1354
  220.6 1.4 and_select_fusion.refs_5_
  222.0 11.4 %key_slopes.1.kv_slope_ref = bf16[128,768]{1,0:T(8,128)(2,1)} custom-call(bf16[2,2,128,768]{3,2,1,0:T(8,128)(2,1)} %bitcast.81), custom_call_target="tpu_custom_call" | custom-call | tf_op jit(solution)/shard_map/key_slopes/pallas_call | solution.py:847
  233.4 4.4 %leave.1 = (bf16[512,2048]{1,0:T(8,128)(2,1)}, bf16[128,512]{1,0:T(8,128)(2,1)}) custom-call(bf16[128,384]{1,0:T(8,128)(2,1)} %get-tuple-element.113.query_slope_ref, bf16[128,768]{1,0:T(8,128)(2,1)} %key_slopes.1.kv_slope_ref, bf16[128,512]{1,0:T(8,128)(2,1)} %get-tuple-element.115.normed_ref, f32[128,512]{1,0:T(8,128)} %get-tuple-element.87.resid_ref.resid0_ref, ...), custom_call_target="tpu_custom_call" | custom-call | tf_op jit(solution)/shard_map/leave/pallas_call | solution.py:1354
  237.8 19.4 %row_slopes.1 = bf16[4,2,128,512]{3,2,1,0:T(8,128)(2,1)} custom-call(bf16[128,512]{1,0:T(8,128)(2,1)} %get-tuple-element.120.refs_0_), custom_call_target="tpu_custom_call" | custom-call | tf_op jit(solution)/shard_map/row_slopes/pallas_call | solution.py:847
  257.2 5.4 %fusion.4 = bf16[2048,512]{1,0:T(8,128)(2,1)} fusion(bf16[1024,512]{1,0:T(8,128)(2,1)} %bitcast.80, s32[1024]{0:T(1024)S(1)} %get-tuple-element.158), kind=kOutput, calls=%fused_computation.10 | convolution fusion | flops 2150629376 | bytes 3149824 | tf_op jit(solution)/shard_map/sd,sf->df/dot_general | solution.py:899
  262.6 56.6 %scatter_weights.1 = (f32[16,2048]{1,0:T(8,128)}, f32[16,2176]{1,0:T(8,128)}, f32[16,2048]{1,0:T(8,128)}, f32[512,512]{1,0:T(8,128)}, f32[2,128,512]{2,1,0:T(8,128)}, /*index=5*/f32[2,2,4,2,8,128]{5,4,3,2,1,0:T(8,128)}) custom-call(bf16[2,2,4,2,16,2048]{5,4,3,2,1,0:T(8,128)(2,1)} %bitcast.72, bf16[2,2,4,2,16,2176]{5,4,3,2,1,0:T(8,128)(2,1)} %bitcast.70, ...), custom_call_target="tpu_custom_call" | custom-call | tf_op jit(solution)/shard_map/scatter_weights/pallas_call | solution.py:847
  319.2 3.6 %tail.1 = (f32[1,1]{1,0:T(1,128)}, f32[2,1,128,512]{3,2,1,0:T(8,128)}, f32[512,512]{1,0:T(8,128)}, f32[512,512]{1,0:T(8,128)}, f32[6,32]{1,0:T(8,128)}, /*index=...) custom-call(s32[2,4]{1,0:T(2,128)} %lengths_ref.1, ...), custom_call_target="tpu_custom_call" | custom-call | tf_op jit(solution)/shard_map/tail/pallas_call | solution.py:1354
  (12 shorter events, 0.1 us)
Async XLA Ops:
  60.7 45.7 %copy-start.2 = (s32[2,4]{1,0:T(2,128)S(1)}, s32[2,4]{1,0:T(2,128)}, u32[]{:S(2)}) copy-start(s32[2,4]{1,0:T(2,128)} %lengths_ref.1) | copy-start | bytes 100
  60.7 47.7 %copy-start.3 = (bf16[6,32]{1,0:T(8,128)(2,1)S(1)}, bf16[6,32]{1,0:T(8,128)(2,1)}, u32[]{:S(2)}) copy-start(bf16[6,32]{1,0:T(8,128)(2,1)} %param.34) | copy-start | bytes 1156
  109.0 34.8 %copy-start.4 = (bf16[2,2,512,512]{3,2,1,0:T(8,128)(2,1)S(1)}, bf16[2,2,512,512]{3,2,1,0:T(8,128)(2,1)}, u32[]{:S(2)}) copy-start(bf16[2,2,512,512]{3,2,1,0:T(8,128)(2,1)} %get-tuple-element.96) | copy-start | bytes 6291460
  147.5 3.2 copy-start
  163.8 5.2 %copy-start.1 = (bf16[4,2,128,512]{3,2,1,0:T(8,128)(2,1)S(1)}, bf16[4,2,128,512]{3,2,1,0:T(8,128)(2,1)}, u32[]{:S(2)}) copy-start(bf16[4,2,128,512]{3,2,1,0:T(8,128)(2,1)} %final_rows.1) | copy-start | bytes 3145732
where the time goes:
time: 325 us; the launch traced here: 323 us
  Pallas kernels  283 us (87%)
  matrix products  21 us (6%)
  other arithmetic  14.4 us (4%)
    pallas_call x9, Pallas kernels, exchange(): pl.pallas_call(kernel, name=name, out_shape=tuple((job.out for job in job...  237 us
    pallas_call x5, Pallas kernels, local_kernel(): pl.pallas_call(kernel, name=name, out_shape=tuple((jax.ShapeDtypeStruct(s...  45.1 us
    dot_general x2, matrix products, t_dot(): return jnp.einsum('sd,sf->df', left, right, preferred_element_type=f32)  9.08 us
    dot_general x2, matrix products, dot(): return jnp.einsum('sd,df->sf', left, right, preferred_element_type=f32)  8.24 us

commit v1 on v0

--- a/solution.py
+++ b/solution.py
@@ -110,8 +110,9 @@
 
 
 class Gather:
-    def __init__(self, block, order, layout, sizes, merged=""):
+    def __init__(self, block, order, layout, sizes, merged="", late=0):
         self.value = block
+        self.late = late
         self.order, self.layout, self.sizes, self.merged = order, layout, sizes, merged
         self.out = jax.ShapeDtypeStruct(tuple(sizes[d] for d in layout) + block.shape, block.dtype)
         self.in_spec = pl.BlockSpec(memory_space=pltpu.VMEM)
@@ -203,17 +204,12 @@
         def _():
             self.line_copy(step + 1).start()
 
-    def launch(self, transfer):
+    def copy(self, transfer):
         level, unit, offset = transfer
         number = self.index[transfer]
-        for need in self.needs(level, unit):
-            self.arrive(need)
         target = self.region(level, unit, 0)
         own = all(moved == 0 for moved in unit)
-        if None in unit and not self.local_done:
-            self.local.wait()
-            self.local_done = True
-        copy = remote(
+        return remote(
             self.source if own else target,
             target,
             self.send.at[number],
@@ -221,8 +217,16 @@
             self.order[level],
             offset,
         )
-        copy.start()
-        self.sent.append(copy)
+
+    def launch(self, transfer):
+        level, unit, offset = transfer
+        for need in self.needs(level, unit):
+            self.arrive(need)
+        if None in unit and not self.local_done:
+            self.local.wait()
+            self.local_done = True
+        self.copy(transfer).start()
+        self.sent.append(transfer)
 
     def events(self):
         found = []
@@ -237,6 +241,8 @@
             key = 0.1 * level + 0.01 * offset
             for d, moved in zip(self.order, unit):
                 key += self.sizes[d] - 1 if moved is None else moved
+            if self.late and self.needs(level, unit):
+                key += self.late
             found.append((key, functools.partial(self.launch, transfer)))
         return found
 
@@ -245,8 +251,8 @@
             self.local.wait()
         for transfer in self.transfers:
             self.arrive(transfer)
-        for copy in self.sent:
-            copy.wait_send()
+        for transfer in self.sent:
+            self.copy(transfer).wait_send()
         if self.line:
             self.line_copy(0).wait_send()
 
@@ -278,7 +284,6 @@
     def prepare(self, refs, place):
         self.source, self.target, self.send, self.recv = refs
         self.place = place
-        self.target[place["s"], place["h"]] = self.source[...]
 
     def copy(self, number, arriving):
         offset = self.offsets[number]
@@ -294,14 +299,24 @@
         )
 
     def events(self):
-        return [(0, functools.partial(self.start, number)) for number in range(len(self.offsets))]
-
-    def start(self, number):
-        self.copy(number, False).start()
+        return [(0, self.begin)]
+
+    def begin(self):
+        for number in range(len(self.offsets)):
+            self.copy(number, False).start()
+        self.target[self.place["s"], self.place["h"]] = self.source[...]
 
     def finish(self):
+        self.receive()
+        self.drain()
+
+    def receive(self):
         for number in range(len(self.offsets)):
-            self.copy(number, True).wait()
+            self.copy(number, True).wait_recv()
+
+    def drain(self):
+        for number in range(len(self.offsets)):
+            self.copy(number, False).wait_send()
 
 
 class Scatter:
@@ -378,9 +393,8 @@
         return remote(source, landed, self.send.at[number], self.recv.at[number], dim, offset)
 
     def launch(self, level, unit, offset):
-        copy = self.copy(level, unit, offset)
-        copy.start()
-        self.sent.append(copy)
+        self.copy(level, unit, offset).start()
+        self.sent.append((level, unit, offset))
 
     def reduce(self, level, unit):
         dim = self.order[level]
@@ -439,29 +453,28 @@
         device = peer_of("s", 1) if number < 3 else across_middle()
         return remote_to(block, landed, self.line_sems.at[0, number], self.line_sems.at[1, number], device)
 
-    def line_step(self, step):
+    def line_step(self, step, ends=True, middles=True):
         level = self.levels - 1
         middle = is_middle(self.place["s"])
         rows, columns = self.block
         held, landing = self.held(level), self.landing[level]
         position = along_line(self.place["s"], step)
 
+        def pass_on():
+            arrived = (0, 3, 1, 2)[step]
+            self.line_copy(arrived).wait_recv()
+
+            def body(piece):
+                held[(position, piece)] += landing[(arrived, piece)]
+
+            each_piece(rows, columns, body)
+            self.line_copy((0, 0, 4, 3)[step]).start()
+
         if step:
-            @pl.when(jnp.logical_not(middle))
-            def _():
-                self.line_copy(step - 1).start()
-
-            @pl.when(middle)
-            def _():
-                arrived = (0, 3, 1, 2)[step]
-                self.line_copy(arrived).wait_recv()
-
-                def body(piece):
-                    held[(position, piece)] += landing[(arrived, piece)]
-
-                each_piece(rows, columns, body)
-                self.line_copy((0, 0, 4, 3)[step]).start()
-
+            if ends:
+                pl.when(jnp.logical_not(middle))(lambda: self.line_copy(step - 1).start())
+            if middles:
+                pl.when(middle)(pass_on)
             return
 
         self.line_copy(0).wait_recv()
@@ -511,8 +524,8 @@
         return found
 
     def finish(self):
-        for copy in self.sent:
-            copy.wait_send()
+        for transfer in self.sent:
+            self.copy(*transfer).wait_send()
         if self.line:
             self.line_copy(0).wait_send()
             middle = is_middle(self.place["s"])
@@ -790,35 +803,60 @@
                     self.core_copy(offset, other).wait_send()
 
 
-def exchange(name, collective_id, jobs):
-    values = [getattr(job, "values", None) or [job.value] for job in jobs]
+def peers_of(jobs):
     peers = []
     for job in jobs:
         for peer in job.peers:
             if peer not in peers:
                 peers.append(peer)
+    return peers
+
+
+def greet(peers, place):
+    barrier = pltpu.get_barrier_semaphore()
+    middle = is_middle(place["s"])
+    awaited = 0
+    for peer in peers:
+        if peer[0] == "m":
+            @pl.when(middle)
+            def _():
+                pl.semaphore_signal(
+                    barrier, inc=1, device_id=across_middle(), device_id_type=pl.DeviceIdType.MESH
+                )
+            continue
+        awaited += 1
+        pl.semaphore_signal(
+            barrier, inc=1, device_id=peer_of(*peer), device_id_type=pl.DeviceIdType.MESH
+        )
+    return awaited
+
+
+def welcome(peers, place, awaited):
+    barrier = pltpu.get_barrier_semaphore()
+    middle = is_middle(place["s"])
+    if ("m", 1) in peers:
+        @pl.when(middle)
+        def _():
+            pl.semaphore_wait(barrier, awaited + 1)
+
+        @pl.when(jnp.logical_not(middle))
+        def _():
+            pl.semaphore_wait(barrier, awaited)
+    else:
+        pl.semaphore_wait(barrier, awaited)
+
+
+def exchange(name, collective_id, jobs):
+    values = [getattr(job, "values", None) or [job.value] for job in jobs]
+    peers = peers_of(jobs)
 
     def kernel(*refs):
         total = sum(len(held) for held in values)
         results = refs[total : total + len(jobs)]
         scratch = refs[total + len(jobs) :]
         begin = offset = 0
-        barrier = pltpu.get_barrier_semaphore()
         place = coordinates()
-        middle = is_middle(place["s"])
-        awaited = 0
-        for peer in peers:
-            if peer[0] == "m":
-                @pl.when(middle)
-                def _():
-                    pl.semaphore_signal(
-                        barrier, inc=1, device_id=across_middle(), device_id_type=pl.DeviceIdType.MESH
-                    )
-                continue
-            awaited += 1
-            pl.semaphore_signal(
-                barrier, inc=1, device_id=peer_of(*peer), device_id_type=pl.DeviceIdType.MESH
-            )
+        awaited = greet(peers, place)
         for number, job in enumerate(jobs):
             end = begin + len(values[number])
             ins = refs[begin:end]
@@ -828,16 +866,7 @@
             mine = len(job.scratch) - hasattr(job, "pack")
             job.prepare(tuple(ins) + (results[number],) + tuple(scratch[offset : offset + mine]), place)
             begin, offset = end, offset + mine
-        if ("m", 1) in peers:
-            @pl.when(middle)
-            def _():
-                pl.semaphore_wait(barrier, awaited + 1)
-
-            @pl.when(jnp.logical_not(middle))
-            def _():
-                pl.semaphore_wait(barrier, awaited)
-        else:
-            pl.semaphore_wait(barrier, awaited)
+        welcome(peers, place, awaited)
         events = [event for job in jobs for event in job.events()]
         for _, act in sorted(events, key=lambda event: event[0]):
             act()
@@ -1411,6 +1440,162 @@
         piece[...] = turned[number : number + 1]
 
 
+def vocabulary(name, collective_id, final_rows, head_rows, targets, alive, sizes):
+    span, width = head_rows.shape
+    tok_dev = final_rows.shape[0]
+    lines = sizes["s"]
+    blocks = 2 * lines
+    step_rows = min(512, span)
+    gather = Gather(final_rows, "sh", "sh", sizes)
+    direct = DirectGather(jax.ShapeDtypeStruct((blocks, tok_dev), f32), sizes)
+    scatter = Scatter(jax.ShapeDtypeStruct((lines, 2, tok_dev, width), bf16), "hs", "sh", sizes)
+    jobs = (gather, direct, scatter)
+    peers = peers_of(jobs)
+
+    def kernel(*refs):
+        final_ref, head_ref, targets_ref, alive_ref = refs[:4]
+        slope_ref, head_part_ref, picked_ref, log_total_ref = refs[4:8]
+        states, totals, own_total, logits, turned, value = refs[8:14]
+        rest = refs[14:]
+        place = coordinates()
+        awaited = greet(peers, place)
+        counts = [len(job.scratch) for job in jobs]
+        gather.prepare((final_ref, states) + rest[: counts[0]], place)
+        direct.prepare((own_total, totals) + rest[counts[0] : counts[0] + counts[1]], place)
+        scatter.prepare((value, slope_ref) + rest[counts[0] + counts[1] :], place)
+        welcome(peers, place, awaited)
+        position = place["s"]
+        half = position // 2
+
+        def spot(token, other):
+            far, second = token // 2, token % 2
+            near_row = position + second * (1 - 2 * (position % 2))
+            far_row = 2 - half + second * (1 - 2 * half)
+            row = near_row + far * (far_row - near_row)
+            side = place["h"] + other * (1 - 2 * place["h"])
+            return row, side, 2 * row + side
+
+        def chunk_of(number):
+            return pl.ds(pl.multiple_of(number * step_rows, step_rows), step_rows)
+
+        def hits(number, target):
+            rows = lax.broadcasted_iota(jnp.int32, (step_rows, tok_dev), 0) + number * step_rows
+            return rows == target
+
+        def bring(step):
+            token, other = step // 2, step % 2
+            if step == 0:
+                gather.line_first()
+                gather.launch((1, (0,), 1))
+                gather.local.wait()
+                gather.local_done = True
+            if other:
+                gather.arrive((1, (token,), 1))
+                if token + 1 < lines:
+                    gather.line_next(token + 1)
+                    gather.launch((1, (token + 1,), 1))
+
+        def forward_step(step, carry):
+            for number in range(blocks):
+                pl.when(step == number)(functools.partial(bring, number))
+            row, side, number = spot(step // 2, step % 2)
+            block = states[row, side]
+            target = targets_ref[pl.ds(number, 1), :]
+
+            def scores(chunk, best):
+                found = mm_t(head_ref[chunk_of(chunk), :], block)
+                logits[number, chunk_of(chunk), :] = found
+                return jnp.maximum(best, jnp.max(found, axis=0, keepdims=True))
+
+            count = span // step_rows
+            best = lax.fori_loop(0, count, scores, jnp.full((1, tok_dev), -3.0e38, f32))
+
+            def spread(chunk, sums):
+                found = logits[number, chunk_of(chunk), :]
+                hit = hits(chunk, target)
+                return (
+                    sums[0] + jnp.sum(jnp.exp(found - best), axis=0, keepdims=True),
+                    sums[1] + jnp.sum(jnp.where(hit, found, 0.0), axis=0, keepdims=True),
+                )
+
+            zero = jnp.zeros((1, tok_dev), f32)
+            total, picked = lax.fori_loop(0, count, spread, (zero, zero))
+            own_total[pl.ds(number, 1), :] = best + jnp.log(total)
+            picked_ref[pl.ds(number, 1), :] = picked
+            return carry
+
+        lax.fori_loop(0, blocks, forward_step, 0)
+        direct.begin()
+        direct.receive()
+        parts = totals[...].reshape((blocks,) + own_total.shape)
+        top = jnp.max(parts, axis=0)
+        log_total_ref[...] = top + jnp.log(jnp.sum(jnp.exp(parts - top[None]), axis=0))
+
+        def backward_step(step, carry):
+            row, side, number = spot(lines - 1 - step // 2, 1 - step % 2)
+            lanes = pl.ds(pl.multiple_of(number * tok_dev, tok_dev), tok_dev)
+            target = targets_ref[pl.ds(number, 1), :]
+            live = alive_ref[pl.ds(number, 1), :]
+            log_total = log_total_ref[pl.ds(number, 1), :]
+
+            def slopes(chunk, inner):
+                share = jnp.exp(logits[number, chunk_of(chunk), :] - log_total)
+                slope = (share - jnp.where(hits(chunk, target), 1.0, 0.0)) * live
+                turned[chunk_of(chunk), lanes] = slope.astype(bf16)
+                return inner
+
+            lax.fori_loop(0, span // step_rows, slopes, 0)
+            value[row, side] = t_mm(turned[:, lanes], head_ref[...]).astype(bf16)
+            for which in range(lines):
+                pl.when(step == 2 * which)(
+                    functools.partial(scatter.launch, 0, (lines - 1 - which,), 1)
+                )
+            return carry
+
+        lax.fori_loop(0, blocks, backward_step, 0)
+        for token in (3, 2):
+            scatter.reduce(0, (token,))
+            scatter.line_step(token, middles=False)
+
+        def head_chunk(number, carry):
+            rows = pl.ds(pl.multiple_of(number * 256, 256), 256)
+            every = states[...].reshape(blocks * tok_dev, width)
+            head_part_ref[rows, :] = mm(turned[rows, :], every).astype(bf16)
+            return carry
+
+        lax.fori_loop(0, span // 256, head_chunk, 0)
+        scatter.line_step(3, ends=False)
+        scatter.line_step(2, ends=False)
+        for token in (1, 0):
+            scatter.reduce(0, (token,))
+            scatter.line_step(token)
+        gather.finish()
+        direct.drain()
+        scatter.finish()
+
+    vmem = pl.BlockSpec(memory_space=pltpu.VMEM)
+    rows = jax.ShapeDtypeStruct((blocks, tok_dev), f32)
+    return pl.pallas_call(
+        kernel,
+        name=name,
+        out_shape=(scatter.out, jax.ShapeDtypeStruct(head_rows.shape, bf16), rows, rows),
+        in_specs=[vmem] * 4,
+        out_specs=(vmem,) * 4,
+        scratch_shapes=[
+            pltpu.VMEM(gather.out.shape, bf16),
+            pltpu.VMEM(direct.out.shape, f32),
+            pltpu.VMEM((blocks, tok_dev), f32),
+            pltpu.VMEM((blocks, span, tok_dev), f32),
+            pltpu.VMEM((span, blocks * tok_dev), bf16),
+            pltpu.VMEM(scatter.value.shape, bf16),
+        ]
+        + [item for job in jobs for item in job.scratch],
+        compiler_params=pltpu.CompilerParams(
+            collective_id=collective_id, has_side_effects=True, vmem_limit_bytes=60 * 1024 * 1024
+        ),
+    )(final_rows, head_rows, targets, alive)
+
+
 def per_device(
     target_ids,
     labels,
@@ -1493,7 +1678,7 @@
         0,
         weights
         + [
-            Gather(embedding, "ac", "ac", sizes),
+            Gather(embedding, "ac", "ac", sizes, "", 20),
             PackedGather(
                 (target_ids, labels),
                 jax.ShapeDtypeStruct((8, 128), jnp.int32),
@@ -1530,7 +1715,7 @@
         1,
         [
             Scatter(picked_rows.reshape(tok_layout), "hs", "sh", sizes),
-            Gather(head, "ac", "ac", sizes),
+            Gather(head, "ac", "ac", sizes, "", 20),
         ],
     )
     head_rows = head_rows.reshape(span, width)
@@ -1592,32 +1777,35 @@
         + [pltpu.SemaphoreType.DMA((4,))],
     )
 
-    (states,) = exchange("final_rows", 3, [Gather(final_rows, "sh", "sh", sizes, merged)])
-    states = states.reshape(tokens, width)
-    logits = dot_t(states, head_rows)
-    highest = jnp.max(logits, axis=1)
-    own_total = highest + jnp.log(jnp.sum(jnp.exp(logits - highest[:, None]), axis=1))
-    (totals,) = exchange("totals", 4, [DirectGather(own_total.reshape(tokens // 128, 128), sizes)])
-    totals = totals.reshape(n_gy, tokens)
-    top = jnp.max(totals, axis=0)
-    log_total = top + jnp.log(jnp.sum(jnp.exp(totals - top[None]), axis=0))
     index = jnp.arange(tokens, dtype=jnp.int32)
     position = (2 * (index // tok_dev % 2) + place["c"]) * tok_dev + index % tok_dev
     alive = (position < jnp.repeat(plane_lengths, 2 * tok_dev)).astype(f32)
-    hit = columns[None, :] == targets[:, None]
-    picked = jnp.sum(jnp.where(hit, logits, 0.0), axis=1)
+    if span <= 2048 and tok_dev == 128:
+        by_block = (n_gy, tok_dev)
+        final_slope, head_part, picked, log_total = vocabulary(
+            "vocabulary", 3, final_rows, head_rows, targets.reshape(by_block), alive.reshape(by_block), sizes
+        )
+        picked, log_total = picked.reshape(tokens), log_total.reshape(tokens)
+    else:
+        (states,) = exchange("final_rows", 3, [Gather(final_rows, "sh", "sh", sizes, merged)])
+        states = states.reshape(tokens, width)
+        logits = dot_t(states, head_rows)
+        highest = jnp.max(logits, axis=1)
+        own_total = highest + jnp.log(jnp.sum(jnp.exp(logits - highest[:, None]), axis=1))
+        (totals,) = exchange("totals", 4, [DirectGather(own_total.reshape(tokens // 128, 128), sizes)])
+        totals = totals.reshape(n_gy, tokens)
+        top = jnp.max(totals, axis=0)
+        log_total = top + jnp.log(jnp.sum(jnp.exp(totals - top[None]), axis=0))
+        hit = columns[None, :] == targets[:, None]
+        picked = jnp.sum(jnp.where(hit, logits, 0.0), axis=1)
+        slope = jnp.exp(logits - log_total[:, None]) - hit.astype(f32)
+        slope = (slope * alive[:, None]).astype(bf16)
+        head_part = t_dot(slope, states).astype(bf16)
+        final_part = dot(slope, head_rows).astype(bf16)
+        (final_slope,) = exchange(
+            "final_slopes", 5, [Scatter(final_part.reshape(tok_layout), "hs", "sh", sizes)]
+        )
     loss_part = jnp.where(column == 0, jnp.sum(alive * log_total), 0.0) - jnp.sum(alive * picked)
-    slope = ((jnp.exp(logits - log_total[:, None]) - hit.astype(f32)) * alive[:, None]).astype(bf16)
-    head_part = t_dot(slope, states).astype(bf16)
-    final_part = dot(slope, head_rows).astype(bf16)
-    final_slope, head_grad = exchange(
-        "final_slopes",
-        5,
-        [
-            Scatter(final_part.reshape(tok_layout), "hs", "sh", sizes),
-            Scatter(head_part.reshape(sizes["a"], 2, voc_dev, width), "ca", "ac", sizes),
-        ],
-    )
 
     grad_a, grad_b, memory_part, part_grad_c, query_slope, kv_slope, grad1, norm_grads, bias_grad = (
         local_kernel(
@@ -1663,7 +1851,14 @@
         [(part_c.shape, bf16), rows_bf16],
         [query_slope, kv_slope, normed_self, resid0, grad1, gain_rows, norm_grads, part_grad_c, part_c],
     )
-    (slopes,) = exchange("row_slopes", 7, [Gather(grad0, "sh", "sh", sizes, merged)])
+    slopes, head_grad = exchange(
+        "row_slopes",
+        7,
+        [
+            Gather(grad0, "sh", "sh", sizes, merged),
+            Scatter(head_part.reshape(sizes["a"], 2, voc_dev, width), "ca", "ac", sizes),
+        ],
+    )
     embed_part = t_dot(
         (local_ids[:, None] == columns[None, :]).astype(bf16), slopes.reshape(tokens, width)
     ).astype(bf16)

time: 325 us -> 299 us (0.920)
  matrix products: 21 us -> 10.3 us
  other arithmetic: 14.4 us -> 5.28 us
  Pallas kernels: 283 us -> 277 us
    pallas_call x9 -> x6, Pallas kernels: 237 us -> 178 us  [exchange(): pl.pallas_call(kernel, name=name, out_shape=tuple((job.out for job in job...]
    pallas_call x0 -> x1, Pallas kernels: none -> 53.9 us  [vocabulary(): pl.pallas_call(kernel, name=name, out_shape=(scatter.out, jax.ShapeDtypeS...]
    convert_element_type x1 -> x0, other arithmetic: 5.14 us -> none  [per_device(): ((jnp.exp(logits - log_total[:, None]) - hit.astype(f32)) * alive[:, None...]
    reduce_sum x3 -> x0, other arithmetic: 4.66 us -> none  [the longest x1 3.19 us: per_device(): picked = jnp.sum(jnp.where(hit, logits, 0.0), axis=1)]
    dot_general x2 -> x1, matrix products: 9.08 us -> 5.35 us  [t_dot(): return jnp.einsum('sd,sf->df', left, right, preferred_element_type=f32)]
    dot_general x1 -> x0, matrix products: 3.69 us -> none  [dot_t(): return jnp.einsum('sf,df->sd', left, right, preferred_element_type=f32)]
    dot_general x2 -> x1, matrix products: 8.24 us -> 4.94 us  [dot(): return jnp.einsum('sd,df->sf', left, right, preferred_element_type=f32)]
where the time goes in v1:
time: 299 us; the launch traced here: 297 us
  Pallas kernels  277 us (93%)
  matrix products  10.3 us (3%)
  other arithmetic  5.28 us (2%)
    pallas_call x6, Pallas kernels, exchange(): pl.pallas_call(kernel, name=name, out_shape=tuple((job.out for job in job...  178 us
    pallas_call x1, Pallas kernels, vocabulary(): pl.pallas_call(kernel, name=name, out_shape=(scatter.out, jax.ShapeDtypeS...  53.9 us
    pallas_call x5, Pallas kernels, local_kernel(): pl.pallas_call(kernel, name=name, out_shape=tuple((jax.ShapeDtypeStruct(s...  44.9 us

profile of v1, /device:TPU:0, one launch (start us, length us, event | category | flops | bytes accessed | tf_op | source)
XLA Modules:
  0.0 297.2 jit_solution(3347307052466410582)
XLA Ops:
  0.7 54.8 %gather_weights.1 = (bf16[2,2,4,2,16,2048]{5,4,3,2,1,0:T(8,128)(2,1)}, bf16[2,2,4,2,16,2176]{5,4,3,2,1,0:T(8,128)(2,1)}, bf16[2,2,4,2,16,2048]{5,4,3,2,1,0:T(8,1...) custom-call(bf16[16,1024]{1,0:T(8,128)(2,1)} %refs_0_.1, ...), custom_call_target="tpu_custom_call" | custom-call | tf_op jit(solution)/shard_map/gather_weights/pallas_call | solution.py:876
  55.5 0.8 slice.11
  56.4 0.1 reshape.270
  56.5 4.9 %fusion.5 = bf16[1024,512]{1,0:T(8,128)(2,1)} fusion(bf16[2048,512]{1,0:T(8,128)(2,1)} %bitcast.76, s32[1024]{0:T(1024)S(1)} %fusion.9), kind=kOutput, calls=%fused_computation.6 | convolution fusion | flops 2150105088 | bytes 3149824 | tf_op jit(solution)/shard_map/sd,df->sf/dot_general | solution.py:920
  61.5 25.5 %rows.1 = (f32[128,512]{1,0:T(8,128)}, bf16[2,2,512,512]{3,2,1,0:T(8,128)(2,1)}) custom-call(bf16[4,2,128,512]{3,2,1,0:T(8,128)(2,1)} %bitcast.63, bf16[512,512]{1,0:T(8,128)(2,1)} %refs_1_.3), custom_call_target="tpu_custom_call" | custom-call | tf_op jit(solution)/shard_map/rows/pallas_call | solution.py:876
  87.0 0.0 copy-start
  87.0 0.0 copy-start.1
  87.0 2.9 enter.1
  90.0 9.7 %self_keys.1 = bf16[2,2,128,768]{3,2,1,0:T(8,128)(2,1)} custom-call(bf16[128,768]{1,0:T(8,128)(2,1)} %get-tuple-element.94.refs_0_), custom_call_target="tpu_custom_call" | custom-call | tf_op jit(solution)/shard_map/self_keys/pallas_call | solution.py:876
  99.8 0.0 copy-done
  99.8 0.1 constant_dynamic-slice_fusion.2
  99.8 0.1 reshape.263
  99.9 0.6 dynamic_slice.12
  100.5 1.2 pad_add_fusion.scalars_ref
  101.7 0.0 copy-done.1
  101.7 0.6 pad.4.bias_ref
  102.3 13.9 %forward.1 = (bf16[128,384]{1,0:T(8,128)(2,1)}, f32[128,128]{1,0:T(8,128)}, f32[128,512]{1,0:T(8,128)}, bf16[128,512]{1,0:T(8,128)(2,1)}, bf16[128,384]{1,0:T(8,...) custom-call(s32[2]{0:T(128)} %pad_add_fusion.scalars_ref, ...), custom_call_target="tpu_custom_call" | custom-call | tf_op jit(solution)/shard_map/forward/pallas_call | solution.py:1383
  116.2 0.6 fusion.13.refs_2_
  116.9 0.1 broadcast_in_dim.20
  116.9 0.1 broadcast_in_dim.21
  117.0 0.7 fusion.28.refs_3_
  117.7 53.9 %vocabulary.1 = (f32[128,512]{1,0:T(8,128)}, bf16[2048,512]{1,0:T(8,128)(2,1)}, f32[8,128]{1,0:T(8,128)}, f32[8,128]{1,0:T(8,128)}) custom-call(bf16[128,512]{1,0:T(8,128)(2,1)} %get-tuple-element.99.refs_0_, bf16[2048,512]{1,0:T(8,128)(2,1)} %bitcast.57, s32[8,128]{1,0:T(8,128)} %fusion.13.refs_2_, f32[8,128]{1,0:T(8,128)} %fusion.28.refs_3_), custom_call_target="tpu_custom_call" | custom-call | tf_op jit(solution)/shard_map/vocabulary/pallas_call | solution.py:1578
  171.6 1.4 select_reduce_fusion
  174.3 20.0 %backward.1 = (bf16[512,2048]{1,0:T(8,128)(2,1)}, bf16[512,2176]{1,0:T(8,128)(2,1)}, bf16[1024,512]{1,0:T(8,128)(2,1)}, bf16[512,768]{1,0:T(8,128)(2,1)}, bf16[1...) custom-call(s32[2]{0:T(128)} %pad_add_fusion.scalars_ref, ...), custom_call_target="tpu_custom_call" | custom-call | tf_op jit(solution)/shard_map/backward/pallas_call | solution.py:1383
  194.4 1.4 and_select_fusion.refs_5_
  195.7 9.5 %key_slopes.1.kv_slope_ref = bf16[128,768]{1,0:T(8,128)(2,1)} custom-call(bf16[2,2,128,768]{3,2,1,0:T(8,128)(2,1)} %bitcast.64), custom_call_target="tpu_custom_call" | custom-call | tf_op jit(solution)/shard_map/key_slopes/pallas_call | solution.py:876
  205.2 4.4 %leave.1 = (bf16[512,2048]{1,0:T(8,128)(2,1)}, bf16[128,512]{1,0:T(8,128)(2,1)}) custom-call(bf16[128,384]{1,0:T(8,128)(2,1)} %get-tuple-element.117.query_slope_ref, bf16[128,768]{1,0:T(8,128)(2,1)} %key_slopes.1.kv_slope_ref, bf16[128,512]{1,0:T(8,128)(2,1)} %get-tuple-element.119.normed_ref, f32[128,512]{1,0:T(8,128)} %get-tuple-element.91.resid_ref.resid0_ref, ...), custom_call_target="tpu_custom_call" | custom-call | tf_op jit(solution)/shard_map/leave/pallas_call | solution.py:1383
  209.6 21.5 %row_slopes.1 = (bf16[4,2,128,512]{3,2,1,0:T(8,128)(2,1)}, f32[512,512]{1,0:T(8,128)}) custom-call(bf16[128,512]{1,0:T(8,128)(2,1)} %get-tuple-element.124.refs_0_, bf16[2,2,512,512]{3,2,1,0:T(8,128)(2,1)} %bitcast.58), custom_call_target="tpu_custom_call" | custom-call | tf_op jit(solution)/shard_map/row_slopes/pallas_call | solution.py:876
  231.1 5.3 %fusion.4 = bf16[2048,512]{1,0:T(8,128)(2,1)} fusion(bf16[1024,512]{1,0:T(8,128)(2,1)} %bitcast.77, s32[1024]{0:T(1024)S(1)} %fusion.9), kind=kOutput, calls=%fused_computation.5 | convolution fusion | flops 2150629376 | bytes 3149824 | tf_op jit(solution)/shard_map/sd,sf->df/dot_general | solution.py:928
  236.4 57.0 %scatter_weights.1 = (f32[16,2048]{1,0:T(8,128)}, f32[16,2176]{1,0:T(8,128)}, f32[16,2048]{1,0:T(8,128)}, f32[512,512]{1,0:T(8,128)}, f32[2,128,512]{2,1,0:T(8,128)}, /*index=5*/f32[2,2,4,2,8,128]{5,4,3,2,1,0:T(8,128)}) custom-call(bf16[2,2,4,2,16,2048]{5,4,3,2,1,0:T(8,128)(2,1)} %bitcast.59, bf16[2,2,4,2,16,2176]{5,4,3,2,1,0:T(8,128)(2,1)} %bitcast.56, ...), custom_call_target="tpu_custom_call" | custom-call | tf_op jit(solution)/shard_map/scatter_weights/pallas_call | solution.py:876
  293.5 3.6 %tail.1 = (f32[1,1]{1,0:T(1,128)}, f32[2,1,128,512]{3,2,1,0:T(8,128)}, f32[512,512]{1,0:T(8,128)}, f32[512,512]{1,0:T(8,128)}, f32[6,32]{1,0:T(8,128)}, /*index=...) custom-call(s32[2,4]{1,0:T(2,128)} %lengths_ref.1, ...), custom_call_target="tpu_custom_call" | custom-call | tf_op jit(solution)/shard_map/tail/pallas_call | solution.py:1383
  (5 shorter events, 0.1 us)
Async XLA Ops:
  87.0 12.7 %copy-start = (s32[2,4]{1,0:T(2,128)S(1)}, s32[2,4]{1,0:T(2,128)}, u32[]{:S(2)}) copy-start(s32[2,4]{1,0:T(2,128)} %lengths_ref.1) | copy-start | bytes 100
  87.0 14.7 %copy-start.1 = (bf16[6,32]{1,0:T(8,128)(2,1)S(1)}, bf16[6,32]{1,0:T(8,128)(2,1)}, u32[]{:S(2)}) copy-start(bf16[6,32]{1,0:T(8,128)(2,1)} %param.34) | copy-start | bytes 1156

commit v2 on v1

--- a/solution.py
+++ b/solution.py
@@ -44,8 +44,11 @@
     if dim == "c":
         return {"gx": flip(gx, 1)}
     if dim == "plane":
-        s, h = offset
-        return {"gy": 2 * flip(gy // 2, s) + flip(gy % 2, h)}
+        s, h, c = offset + (0,) * (3 - len(offset))
+        there = {"gy": 2 * flip(gy // 2, s) + flip(gy % 2, h)}
+        if c:
+            there["gx"] = flip(gx, 1)
+        return there
     if dim == "s":
         return {"gy": 2 * flip(gy // 2, offset) + gy % 2}
     return {"gy": flip(gy, 1)}
@@ -270,9 +273,10 @@
 
 
 class DirectGather:
-    def __init__(self, block, sizes):
+    def __init__(self, block, sizes, dims="sh"):
         self.value = block
-        shape = (sizes["s"], 2)
+        self.dims = dims
+        shape = tuple(sizes[d] for d in dims)
         self.out = jax.ShapeDtypeStruct(shape + block.shape, block.dtype)
         self.in_spec = pl.BlockSpec(memory_space=pltpu.VMEM)
         self.out_spec = pl.BlockSpec(memory_space=pltpu.VMEM)
@@ -288,7 +292,7 @@
     def copy(self, number, arriving):
         offset = self.offsets[number]
         spot = tuple(
-            flip(self.place[d], moved) if arriving else self.place[d] for d, moved in zip("sh", offset)
+            flip(self.place[d], moved) if arriving else self.place[d] for d, moved in zip(self.dims, offset)
         )
         return remote_to(
             self.source,
@@ -304,7 +308,7 @@
     def begin(self):
         for number in range(len(self.offsets)):
             self.copy(number, False).start()
-        self.target[self.place["s"], self.place["h"]] = self.source[...]
+        self.target[tuple(self.place[d] for d in self.dims)] = self.source[...]
 
     def finish(self):
         self.receive()
@@ -966,6 +970,15 @@
 def one_half(pair, half):
     inside = (lanes_of(pair.shape) // HEAD) == half
     return jnp.where(inside, pair, jnp.zeros_like(pair))
+
+
+def both_halves(pair):
+    return jnp.concatenate([one_half(pair, 0), one_half(pair, 1)], axis=0)
+
+
+def joined_rows(stacked):
+    rows = stacked.shape[0] // 2
+    return joined(stacked[:rows], stacked[rows:])
 
 
 def joined(first, second):
@@ -1252,24 +1265,27 @@
 
     def cross_pair_back(place, place_v):
         keys, values = mem_kv[:, place], mem_kv[:, place_v]
-        parts = []
-        for half in range(2):
-            lanes = lanes_of(total_cross_ref.shape)
-            total = jnp.where(lanes == place.start // HEAD + half, total_cross_ref[...], 0.0)
-            query = one_half(query_cross_ref[:, place], half)
-            parts.append(
-                attention_back(
-                    query,
-                    keys,
-                    values,
-                    mm_t(query, keys),
-                    jnp.sum(total, axis=-1, keepdims=True),
-                    one_half(cross_query_slope_ref[:, place], half),
-                )
+        lanes = lanes_of(total_cross_ref.shape)
+        totals = [
+            jnp.sum(
+                jnp.where(lanes == place.start // HEAD + half, total_cross_ref[...], 0.0),
+                axis=-1,
+                keepdims=True,
             )
-        cross_query_slope_ref[:, place] = joined(parts[0][1], parts[1][1]).astype(bf16)
-        cross_kv_slope_ref[:, place] = (parts[0][2] + parts[1][2]).astype(bf16)
-        cross_kv_slope_ref[:, place_v] = (parts[0][3] + parts[1][3]).astype(bf16)
+            for half in range(2)
+        ]
+        query = both_halves(query_cross_ref[:, place])
+        part = attention_back(
+            query,
+            keys,
+            values,
+            mm_t(query, keys),
+            jnp.concatenate(totals, axis=0),
+            both_halves(cross_query_slope_ref[:, place]),
+        )
+        cross_query_slope_ref[:, place] = joined_rows(part[1]).astype(bf16)
+        cross_kv_slope_ref[:, place] = part[2].astype(bf16)
+        cross_kv_slope_ref[:, place_v] = part[3].astype(bf16)
 
     in_steps(HD, 2 * HEAD, cross_pair_back, HD)
     memory = fetched[3]
@@ -1314,28 +1330,36 @@
         place = slice(2 * HEAD * pair, 2 * HEAD * (pair + 1))
         place_v = slice(HD + 2 * HEAD * pair, HD + 2 * HEAD * (pair + 1))
         keys, values = kv_ref[:, place], kv_ref[:, place_v]
-        parts = []
+        query = both_halves(query_ref[:, place])
+        products = mm_t(query, keys)
+        scores, totals = [], []
         for half in range(2):
             number = 2 * pair + half
-            query = one_half(query_ref[:, place], half)
-            scores = biased_scores(
-                mm_t(query, keys), bias_rows[number : number + 1], first, length
+            scores.append(
+                biased_scores(
+                    products[half * rows : (half + 1) * rows],
+                    bias_rows[number : number + 1],
+                    first,
+                    length,
+                )
             )
-            part = attention_back(
-                query,
-                keys,
-                values,
-                scores,
-                total_self_ref[:, number : number + 1],
-                one_half(out_slope[:, place], half),
-            )
-            parts.append(part)
-            turned = pltpu.roll(mm(reverse, part[0]), 0, 1, stride=1, stride_axis=0)
-            where = lax.broadcasted_iota(jnp.int32, bias_sums.shape, 0) == number
+            totals.append(total_self_ref[:, number : number + 1])
+        part = attention_back(
+            query,
+            keys,
+            values,
+            jnp.concatenate(scores, axis=0),
+            jnp.concatenate(totals, axis=0),
+            both_halves(out_slope[:, place]),
+        )
+        for half in range(2):
+            turned = mm(reverse, part[0][half * rows : (half + 1) * rows])
+            turned = pltpu.roll(turned, 0, 1, stride=1, stride_axis=0)
+            where = lax.broadcasted_iota(jnp.int32, bias_sums.shape, 0) == 2 * pair + half
             bias_sums = jnp.where(where, jnp.sum(turned, axis=0, keepdims=True), bias_sums)
-        query_slope_ref[:, place] = joined(parts[0][1], parts[1][1]).astype(bf16)
-        kv_slope_ref[:, place] = (parts[0][2] + parts[1][2]).astype(bf16)
-        kv_slope_ref[:, place_v] = (parts[0][3] + parts[1][3]).astype(bf16)
+        query_slope_ref[:, place] = joined_rows(part[1]).astype(bf16)
+        kv_slope_ref[:, place] = part[2].astype(bf16)
+        kv_slope_ref[:, place_v] = part[3].astype(bf16)
     bias_sums = pltpu.roll(bias_sums, 2 * seq + 1 - rows - first, 1)
     high = bias_sums.astype(bf16)
     rest = bias_sums - high.astype(f32)
@@ -1594,6 +1618,129 @@
             collective_id=collective_id, has_side_effects=True, vmem_limit_bytes=60 * 1024 * 1024
         ),
     )(final_rows, head_rows, targets, alive)
+
+
+def opening(name, collective_id, weights, embedding, ids, memory, head, sizes):
+    voc_dev, width = embedding.shape
+    n_gy = 2 * sizes["s"]
+    n_gx = 2 * sizes["a"]
+    span = n_gx * voc_dev
+    lines = sizes["s"]
+    micro, _, seq_dev = ids[0].shape
+    tok_dev = 2 * seq_dev
+    table = Gather(embedding, "ac", "ac", sizes)
+    codes = DirectGather(jax.ShapeDtypeStruct((8, 128), jnp.int32), sizes, "shc")
+    memories = MemoryGather(memory, sizes)
+    heads = Gather(head, "ac", "ac", sizes, "", 20)
+    sums = Scatter(jax.ShapeDtypeStruct((lines, 2, tok_dev, width), bf16), "hs", "sh", sizes)
+    jobs = list(weights) + [table, codes, memories, heads, sums]
+    peers = peers_of(jobs)
+    operands = [list(job.values) for job in weights] + [[embedding], list(ids), [memory], [head]]
+    flat = [value for group in operands for value in group]
+
+    def kernel(*refs):
+        ins = list(refs[: len(flat)])
+        outs = list(refs[len(flat) : len(flat) + 7])
+        rest = list(refs[len(flat) + 7 :])
+        place = coordinates()
+        awaited = greet(peers, place)
+
+        def take(source, count):
+            taken = tuple(source[:count])
+            del source[:count]
+            return taken
+
+        rows_ref, value, code = rest.pop(0), rest.pop(0), rest.pop(0)
+        for job in weights:
+            pieces = take(ins, len(job.values))
+            block = rest.pop(0)
+            job.pack(pieces, block)
+            job.prepare((block, outs.pop(0)) + take(rest, len(job.scratch) - 1), place)
+        table.prepare((ins.pop(0), rows_ref) + take(rest, len(table.scratch)), place)
+        pack_ids(take(ins, 2), code)
+        ids_ref = outs.pop(0)
+        codes.prepare((code, ids_ref) + take(rest, len(codes.scratch)), place)
+        memories.prepare((ins.pop(0), outs.pop(0)) + take(rest, len(memories.scratch)), place)
+        heads.prepare((ins.pop(0), outs.pop(0)) + take(rest, len(heads.scratch)), place)
+        sums.prepare((value, outs.pop(0)) + take(rest, len(sums.scratch)), place)
+        welcome(peers, place, awaited)
+
+        def tables_here():
+            codes.receive()
+            table.local.wait()
+            table.local_done = True
+            for transfer in table.transfers:
+                table.arrive(transfer)
+
+        def pick(token):
+            row = along_line(place["s"], token)
+
+            def one(other, carry):
+                side = place["h"] + (1 - other) * (1 - 2 * place["h"])
+                index = jnp.concatenate(
+                    [
+                        ids_ref[2 * side + place["c"], which, row % 2, pl.ds(row // 2, 1), :][:, :seq_dev]
+                        for which in range(2)
+                    ],
+                    axis=1,
+                )
+                shard = index // voc_dev
+                held = shard % n_gy == 2 * place["s"] + place["h"]
+                index = jnp.where(held, shard // n_gy * voc_dev + index % voc_dev, -1)
+                at = lax.broadcasted_iota(jnp.int32, (span, tok_dev), 0) == index
+                every = rows_ref[...].reshape(span, width)
+                value[row, side] = t_mm(jnp.where(at, 1.0, 0.0).astype(bf16), every).astype(bf16)
+                pl.when(other == 0)(functools.partial(sums.launch, 0, (token,), 1))
+                return carry
+
+            lax.fori_loop(0, 2, one, 0)
+
+        events = [event for job in list(weights) + [memories, heads] for event in job.events()]
+        events.append((-2, codes.begin))
+        for transfer in table.transfers:
+            level, unit, _ = transfer
+            key = -1 if level == 0 else TABLE_KEY if unit[0] else 0.1
+            events.append((key, functools.partial(table.launch, transfer)))
+        events.append((TABLE_KEY + 0.05, tables_here))
+        for number, token in enumerate((3, 2, 1, 0)):
+            events.append((PICK_KEY + PICK_STEP * number, functools.partial(pick, token)))
+            key = SUM_KEY + SUM_STEP * number
+            events.append((key, functools.partial(sums.reduce, 0, (token,))))
+            if token:
+                events.append((key + 0.01, functools.partial(sums.line_step, token, middles=False)))
+                events.append((LINE_KEY + SUM_STEP * number, functools.partial(sums.line_step, token, ends=False)))
+            else:
+                events.append((LINE_KEY + SUM_STEP * number, functools.partial(sums.line_step, token)))
+        for _, act in sorted(events, key=lambda event: event[0]):
+            act()
+        for job in jobs:
+            if job is codes:
+                job.drain()
+            else:
+                job.finish()
+
+    vmem = pl.BlockSpec(memory_space=pltpu.VMEM)
+    anywhere = pl.BlockSpec(memory_space=pl.ANY)
+    scratch = [
+        pltpu.VMEM(table.out.shape, bf16),
+        pltpu.VMEM(sums.value.shape, bf16),
+        pltpu.VMEM((8, 128), jnp.int32),
+    ]
+    return pl.pallas_call(
+        kernel,
+        name=name,
+        out_shape=tuple(job.out for job in weights)
+        + (codes.out, memories.out, heads.out, sums.out),
+        in_specs=[vmem] * len(flat),
+        out_specs=(anywhere,) * 3 + (vmem, anywhere, anywhere, vmem),
+        scratch_shapes=scratch + [item for job in jobs for item in job.scratch],
+        compiler_params=pltpu.CompilerParams(
+            collective_id=collective_id, has_side_effects=True, vmem_limit_bytes=60 * 1024 * 1024
+        ),
+    )(*flat)
+
+
+TABLE_KEY, PICK_KEY, PICK_STEP, SUM_KEY, SUM_STEP, LINE_KEY = 0.55, 0.65, 0.05, 1.3, 0.3, 1.9
 
 
 def per_device(
@@ -1650,7 +1797,8 @@
     gains = (gain_self, gain_cross, gain_ff, gain_final)
     widths = [sum(piece.shape[1] for piece in group) for group in groups]
     widths[2] += GAIN_PAD
-    orders = ("shac", "sahc", "sahc")
+    orders = ("shac", "shac", "sahc")
+    ways_back = ("cahs", "chas", "chas")
     if whole_tiles:
         operands = list(groups)
         operands[2] += tuple(gain.reshape(1, rows_dev) for gain in gains)
@@ -1673,28 +1821,40 @@
         weights = [
             Gather(packed(part), order, "acsh", sizes, merged) for part, order in zip(shards, orders)
         ]
-    part_a, part_b, part_c, embed_rows, ids, memory_all = exchange(
-        "gather_weights",
-        0,
-        weights
-        + [
-            Gather(embedding, "ac", "ac", sizes, "", 20),
-            PackedGather(
-                (target_ids, labels),
-                jax.ShapeDtypeStruct((8, 128), jnp.int32),
-                pack_ids,
-                "shc",
-                "shc",
-                sizes,
-                "shc",
-            ),
-            MemoryGather(memory.reshape(micro, mem_dev, width), sizes),
-        ],
-    )
+    small_tables = whole_tiles and span <= 2048 and tok_dev == 128
+    if small_tables:
+        part_a, part_b, part_c, ids, memory_all, head_rows, resid0 = opening(
+            "start",
+            0,
+            weights,
+            embedding,
+            (target_ids, labels),
+            memory.reshape(micro, mem_dev, width),
+            head,
+            sizes,
+        )
+    else:
+        part_a, part_b, part_c, embed_rows, ids, memory_all = exchange(
+            "gather_weights",
+            0,
+            weights
+            + [
+                Gather(embedding, "ac", "ac", sizes, "", 20),
+                PackedGather(
+                    (target_ids, labels),
+                    jax.ShapeDtypeStruct((8, 128), jnp.int32),
+                    pack_ids,
+                    "shc",
+                    "shc",
+                    sizes,
+                    "shc",
+                ),
+                MemoryGather(memory.reshape(micro, mem_dev, width), sizes),
+            ],
+        )
     part_a, part_b, part_c = (
         full.reshape(width, count) for full, count in zip((part_a, part_b, part_c), widths)
     )
-    embed_rows = embed_rows.reshape(span, width)
     memory_all = memory_all.reshape(n_gy * mem_dev, width)
     ids = ids[..., : 2 * micro, :seq_dev].reshape(n_gy, 2, 2, micro, seq_dev)
     ids = ids.transpose(2, 3, 1, 0, 4).reshape(2, sizes["s"] * 2, 2, tok_dev)
@@ -1708,16 +1868,18 @@
     targets = local_of(ids[1])
     columns = jnp.arange(span, dtype=jnp.int32)
 
-    picked_rows = dot((local_ids[:, None] == columns[None, :]).astype(bf16), embed_rows).astype(bf16)
     tok_layout = (sizes["s"], 2, tok_dev, width)
-    resid0, head_rows = exchange(
-        "rows",
-        1,
-        [
-            Scatter(picked_rows.reshape(tok_layout), "hs", "sh", sizes),
-            Gather(head, "ac", "ac", sizes, "", 20),
-        ],
-    )
+    if not small_tables:
+        chosen = (local_ids[:, None] == columns[None, :]).astype(bf16)
+        picked_rows = dot(chosen, embed_rows.reshape(span, width)).astype(bf16)
+        resid0, head_rows = exchange(
+            "rows",
+            1,
+            [
+                Scatter(picked_rows.reshape(tok_layout), "hs", "sh", sizes),
+                Gather(head, "ac", "ac", sizes, "", 20),
+            ],
+        )
     head_rows = head_rows.reshape(span, width)
 
     plane_lengths = lax.dynamic_slice_in_dim(lengths, 2 * place["a"], 2, axis=1).reshape(-1)
@@ -1780,7 +1942,7 @@
     index = jnp.arange(tokens, dtype=jnp.int32)
     position = (2 * (index // tok_dev % 2) + place["c"]) * tok_dev + index % tok_dev
     alive = (position < jnp.repeat(plane_lengths, 2 * tok_dev)).astype(f32)
-    if span <= 2048 and tok_dev == 128:
+    if small_tables:
         by_block = (n_gy, tok_dev)
         final_slope, head_part, picked, log_total = vocabulary(
             "vocabulary", 3, final_rows, head_rows, targets.reshape(by_block), alive.reshape(by_block), sizes
@@ -1871,8 +2033,8 @@
         "scatter_weights",
         8,
         [
-            Scatter(part, order[::-1], "acsh", sizes, merged)
-            for part, order in zip(blocks, orders)
+            Scatter(part, order, "acsh", sizes, merged)
+            for part, order in zip(blocks, ways_back)
         ]
         + [
             Scatter(embed_part.reshape(sizes["a"], 2, voc_dev, width), "ca", "ac", sizes),

time: 299 us -> 285 us (0.953)
  Pallas kernels: 277 us -> 268 us
  matrix products: 10.3 us -> 5.33 us
    pallas_call x6 -> x4, Pallas kernels: 178 us -> 98.4 us  [exchange(): pl.pallas_call(kernel, name=name, out_shape=tuple((job.out for job in job...]
    pallas_call x0 -> x1, Pallas kernels: none -> 73 us  [opening(): pl.pallas_call(kernel, name=name, out_shape=tuple((job.out for job in wei...]
    dot_general x1 -> x0, matrix products: 4.94 us -> none  [dot(): return jnp.einsum('sd,df->sf', left, right, preferred_element_type=f32)]
where the time goes in v2:
time: 285 us; the launch traced here: 283 us
  Pallas kernels  268 us (94%)
  matrix products  5.33 us (2%)
  other arithmetic  5.26 us (2%)
    pallas_call x4, Pallas kernels, exchange(): pl.pallas_call(kernel, name=name, out_shape=tuple((job.out for job in job...  98.4 us
    pallas_call x1, Pallas kernels, opening(): pl.pallas_call(kernel, name=name, out_shape=tuple((job.out for job in wei...  73 us
    pallas_call x1, Pallas kernels, vocabulary(): pl.pallas_call(kernel, name=name, out_shape=(scatter.out, jax.ShapeDtypeS...  51.9 us
    pallas_call x5, Pallas kernels, local_kernel(): pl.pallas_call(kernel, name=name, out_shape=tuple((jax.ShapeDtypeStruct(s...  44.2 us

profile of v2, /device:TPU:0, one launch (start us, length us, event | category | flops | bytes accessed | tf_op | source)
XLA Modules:
  0.0 282.7 jit_solution(16696393889747042526)
XLA Ops:
  0.7 0.8 constant_dynamic-slice_fusion.2
  1.5 0.1 reshape.257
  1.5 0.6 dynamic_slice.12
  2.1 1.2 pad_add_fusion.scalars_ref
  3.4 0.0 copy-start.1
  3.4 73.0 %start.1 = (bf16[2,2,4,2,16,2048]{5,4,3,2,1,0:T(8,128)(2,1)}, bf16[2,2,4,2,16,2176]{5,4,3,2,1,0:T(8,128)(2,1)}, bf16[2,2,4,2,16,2048]{5,4,3,2,1,0:T(8,128)(2,1)}...) custom-call(bf16[16,1024]{1,0:T(8,128)(2,1)} %refs_0_.1, ...), custom_call_target="tpu_custom_call" | custom-call | tf_op jit(solution)/shard_map/start/pallas_call | solution.py:1729
  76.4 2.9 %enter.1 = (bf16[128,384]{1,0:T(8,128)(2,1)}, bf16[128,768]{1,0:T(8,128)(2,1)}, bf16[128,512]{1,0:T(8,128)(2,1)}, f32[16,512]{1,0:T(8,128)}) custom-call(f32[128,512]{1,0:T(8,128)} %get-tuple-element.88.resid_ref.resid0_ref, bf16[512,2048]{1,0:T(8,128)(2,1)} %bitcast.41), custom_call_target="tpu_custom_call" | custom-call | tf_op jit(solution)/shard_map/enter/pallas_call | solution.py:1407
  79.3 9.7 %self_keys.1 = bf16[2,2,128,768]{3,2,1,0:T(8,128)(2,1)} custom-call(bf16[128,768]{1,0:T(8,128)(2,1)} %get-tuple-element.91.refs_0_), custom_call_target="tpu_custom_call" | custom-call | tf_op jit(solution)/shard_map/self_keys/pallas_call | solution.py:880
  89.0 0.0 copy-done.1
  89.1 0.6 pad.4.bias_ref
  89.6 0.0 copy-start
  89.6 13.9 %forward.1 = (bf16[128,384]{1,0:T(8,128)(2,1)}, f32[128,128]{1,0:T(8,128)}, f32[128,512]{1,0:T(8,128)}, bf16[128,512]{1,0:T(8,128)(2,1)}, bf16[128,384]{1,0:T(8,...) custom-call(s32[2]{0:T(128)} %pad_add_fusion.scalars_ref, ...), custom_call_target="tpu_custom_call" | custom-call | tf_op jit(solution)/shard_map/forward/pallas_call | solution.py:1407
  103.6 0.0 copy-done
  103.6 0.1 reshape.270
  103.7 0.6 fusion.6.refs_2_
  104.4 0.1 broadcast_in_dim.18
  104.4 0.1 broadcast_in_dim.19
  104.5 0.7 fusion.25.refs_3_
  105.2 51.9 %vocabulary.1 = (f32[128,512]{1,0:T(8,128)}, bf16[2048,512]{1,0:T(8,128)(2,1)}, f32[8,128]{1,0:T(8,128)}, f32[8,128]{1,0:T(8,128)}) custom-call(bf16[128,512]{1,0:T(8,128)(2,1)} %get-tuple-element.96.refs_0_, bf16[2048,512]{1,0:T(8,128)(2,1)} %bitcast.55, s32[8,128]{1,0:T(8,128)} %fusion.6.refs_2_, f32[8,128]{1,0:T(8,128)} %fusion.25.refs_3_), custom_call_target="tpu_custom_call" | custom-call | tf_op jit(solution)/shard_map/vocabulary/pallas_call | solution.py:1602
  157.1 1.4 select_reduce_fusion
  159.7 19.3 %backward.1 = (bf16[512,2048]{1,0:T(8,128)(2,1)}, bf16[512,2176]{1,0:T(8,128)(2,1)}, bf16[1024,512]{1,0:T(8,128)(2,1)}, bf16[512,768]{1,0:T(8,128)(2,1)}, bf16[1...) custom-call(s32[2]{0:T(128)} %pad_add_fusion.scalars_ref, ...), custom_call_target="tpu_custom_call" | custom-call | tf_op jit(solution)/shard_map/backward/pallas_call | solution.py:1407
  179.1 1.4 and_select_fusion.refs_5_
  180.4 9.9 %key_slopes.1.kv_slope_ref = bf16[128,768]{1,0:T(8,128)(2,1)} custom-call(bf16[2,2,128,768]{3,2,1,0:T(8,128)(2,1)} %bitcast.60), custom_call_target="tpu_custom_call" | custom-call | tf_op jit(solution)/shard_map/key_slopes/pallas_call | solution.py:880
  190.3 4.4 %leave.1 = (bf16[512,2048]{1,0:T(8,128)(2,1)}, bf16[128,512]{1,0:T(8,128)(2,1)}) custom-call(bf16[128,384]{1,0:T(8,128)(2,1)} %get-tuple-element.115.query_slope_ref, bf16[128,768]{1,0:T(8,128)(2,1)} %key_slopes.1.kv_slope_ref, bf16[128,512]{1,0:T(8,128)(2,1)} %get-tuple-element.117.normed_ref, f32[128,512]{1,0:T(8,128)} %get-tuple-element.88.resid_ref.resid0_ref, ...), custom_call_target="tpu_custom_call" | custom-call | tf_op jit(solution)/shard_map/leave/pallas_call | solution.py:1407
  194.7 22.8 %row_slopes.1 = (bf16[4,2,128,512]{3,2,1,0:T(8,128)(2,1)}, f32[512,512]{1,0:T(8,128)}) custom-call(bf16[128,512]{1,0:T(8,128)(2,1)} %get-tuple-element.122.refs_0_, bf16[2,2,512,512]{3,2,1,0:T(8,128)(2,1)} %bitcast.54), custom_call_target="tpu_custom_call" | custom-call | tf_op jit(solution)/shard_map/row_slopes/pallas_call | solution.py:880
  217.5 5.3 %fusion.2 = bf16[2048,512]{1,0:T(8,128)(2,1)} fusion(bf16[1024,512]{1,0:T(8,128)(2,1)} %bitcast.72, s32[1024]{0:T(1024)S(1)} %fusion.16), kind=kOutput, calls=%fused_computation.3 | convolution fusion | flops 2150629376 | bytes 3149824 | tf_op jit(solution)/shard_map/sd,sf->df/dot_general | solution.py:932
  222.9 56.0 %scatter_weights.1 = (f32[16,2048]{1,0:T(8,128)}, f32[16,2176]{1,0:T(8,128)}, f32[16,2048]{1,0:T(8,128)}, f32[512,512]{1,0:T(8,128)}, f32[2,128,512]{2,1,0:T(8,128)}, /*index=5*/f32[2,2,4,2,8,128]{5,4,3,2,1,0:T(8,128)}) custom-call(bf16[2,2,4,2,16,2048]{5,4,3,2,1,0:T(8,128)(2,1)} %bitcast.56, bf16[2,2,4,2,16,2176]{5,4,3,2,1,0:T(8,128)(2,1)} %bitcast.53, ...), custom_call_target="tpu_custom_call" | custom-call | tf_op jit(solution)/shard_map/scatter_weights/pallas_call | solution.py:880
  278.9 3.6 %tail.1 = (f32[1,1]{1,0:T(1,128)}, f32[2,1,128,512]{3,2,1,0:T(8,128)}, f32[512,512]{1,0:T(8,128)}, f32[512,512]{1,0:T(8,128)}, f32[6,32]{1,0:T(8,128)}, /*index=...) custom-call(s32[2,4]{1,0:T(2,128)} %lengths_ref.1, ...), custom_call_target="tpu_custom_call" | custom-call | tf_op jit(solution)/shard_map/tail/pallas_call | solution.py:1407
  (6 shorter events, 0.1 us)
Async XLA Ops:
  3.4 85.7 %copy-start.1 = (bf16[6,32]{1,0:T(8,128)(2,1)S(1)}, bf16[6,32]{1,0:T(8,128)(2,1)}, u32[]{:S(2)}) copy-start(bf16[6,32]{1,0:T(8,128)(2,1)} %param.34) | copy-start | bytes 1156
  89.6 14.0 %copy-start = (s32[4,2,2,8,128]{4,3,2,1,0:T(8,128)S(1)}, s32[4,2,2,8,128]{4,3,2,1,0:T(8,128)}, u32[]{:S(2)}) copy-start(s32[4,2,2,8,128]{4,3,2,1,0:T(8,128)} %get-tuple-element.98) | copy-start | bytes 196612

commit v3 on v2

--- a/solution.py
+++ b/solution.py
@@ -1048,8 +1048,14 @@
     return total, jnp.exp(scores - total)
 
 
+def query_span(lengths_ref, rows):
+    place = coordinates()
+    length = lengths_ref[place["s"] // 2, 2 * place["a"] + place["s"] % 2]
+    return (2 * place["h"] + place["c"]) * rows, length
+
+
 def forward_kernel(
-    scalars_ref,
+    lengths_ref,
     query_ref,
     kv_ref,
     resid0_ref,
@@ -1085,9 +1091,9 @@
         (part_c_ref, part_b_ref, memory_ref, part_a_ref),
         sems,
     )
-    first, length = scalars_ref[0], scalars_ref[1]
+    first, length = query_span(lengths_ref, query_ref.shape[0])
     ff = hidden_ref.shape[1]
-    bias_rows = pltpu.roll(mm(bias_ref[...], table_ref[...]), first, 1)
+    bias_rows = pltpu.roll(mm(bias_ref[...], table_ref[:BUCKETS, :]), first, 1)
     lanes = lanes_of(total_self_ref.shape)
     totals = jnp.zeros(total_self_ref.shape, f32)
     for pair in range(HEADS // 2):
@@ -1168,7 +1174,7 @@
 
 
 def backward_kernel(
-    scalars_ref,
+    lengths_ref,
     slope_ref,
     resid3_ref,
     hidden_ref,
@@ -1220,7 +1226,7 @@
         (part_b_ref, part_a_ref, mem_kv_ref, memory_ref, part_c_ref),
         sems,
     )
-    first, length = scalars_ref[0], scalars_ref[1]
+    first, length = query_span(lengths_ref, query_ref.shape[0])
     ff = hidden_ref.shape[1]
     width = resid3_ref.shape[1]
     norm_grads_ref[...] = jnp.zeros_like(norm_grads_ref)
@@ -1321,8 +1327,8 @@
     self_in = grad1.astype(bf16)
     grad_c_ref[:, :HD] = t_mm(self_in, attn_self_ref[...]).astype(bf16)
     out_slope = mm(self_in, part_c[:, 3 * HD : 4 * HD]).astype(bf16)
-    bias_rows = pltpu.roll(mm(bias_ref[...], table_ref[...]), first, 1)
-    bias_sums = jnp.zeros(bias_rows.shape, f32)
+    bias_rows = pltpu.roll(mm(bias_ref[...], table_ref[:BUCKETS, :]), first, 1)
+    bias_sums = jnp.zeros((8, bias_rows.shape[1]), f32)
     rows, seq = query_ref.shape[0], kv_ref.shape[0]
     reverse = lax.broadcasted_iota(jnp.int32, (rows, rows), 0) + lanes_of((rows, rows)) == rows - 1
     reverse = reverse.astype(bf16)
@@ -1433,6 +1439,13 @@
         block[:, start:] = t_mm(stacked.astype(bf16), pick.astype(bf16)).astype(bf16)
 
 
+def pack_rows(pieces, block):
+    start = 0
+    for piece in pieces:
+        block[start : start + piece.shape[0], :] = piece[...]
+        start += piece.shape[0]
+
+
 def pack_ids(pieces, block):
     block[...] = jnp.zeros_like(block)
     for number, piece in enumerate(pieces):
@@ -1452,7 +1465,7 @@
     for first in range(lengths_ref.shape[0]):
         for second in range(lengths_ref.shape[1]):
             count = count + lengths_ref[first, second]
-    loss_ref[...] = total[0:1, 64:65] / count.astype(f32)
+    loss_ref[...] = jnp.sum(total[8:], keepdims=True) / count.astype(f32)
     bias_out[...] = total[:HEADS, :BUCKETS]
     for ref, pieces in ((a_ref, outs[:2]), (b_ref, outs[2:6]), (c_ref, outs[6:11])):
         start = 0
@@ -1464,7 +1477,7 @@
         piece[...] = turned[number : number + 1]
 
 
-def vocabulary(name, collective_id, final_rows, head_rows, targets, alive, sizes):
+def vocabulary(name, collective_id, final_rows, head_rows, targets, lengths, sizes):
     span, width = head_rows.shape
     tok_dev = final_rows.shape[0]
     lines = sizes["s"]
@@ -1477,10 +1490,10 @@
     peers = peers_of(jobs)
 
     def kernel(*refs):
-        final_ref, head_ref, targets_ref, alive_ref = refs[:4]
-        slope_ref, head_part_ref, picked_ref, log_total_ref = refs[4:8]
-        states, totals, own_total, logits, turned, value = refs[8:14]
-        rest = refs[14:]
+        final_ref, head_ref, targets_ref, lengths_ref = refs[:4]
+        slope_ref, head_part_ref, loss_ref = refs[4:7]
+        states, totals, own_total, logits, turned, value, picked_ref, log_total_ref = refs[7:15]
+        rest = refs[15:]
         place = coordinates()
         awaited = greet(peers, place)
         counts = [len(job.scratch) for job in jobs]
@@ -1559,8 +1572,12 @@
             row, side, number = spot(lines - 1 - step // 2, 1 - step % 2)
             lanes = pl.ds(pl.multiple_of(number * tok_dev, tok_dev), tok_dev)
             target = targets_ref[pl.ds(number, 1), :]
-            live = alive_ref[pl.ds(number, 1), :]
             log_total = log_total_ref[pl.ds(number, 1), :]
+            length = lengths_ref[row // 2, 2 * place["a"] + row % 2]
+            spots = (2 * side + place["c"]) * tok_dev + lax.broadcasted_iota(jnp.int32, (1, tok_dev), 1)
+            live = jnp.where(spots < length, 1.0, 0.0)
+            shown = log_total * (1 - jnp.minimum(2 * position + place["h"], 1)).astype(f32)
+            loss_ref[pl.ds(number, 1), :] = live * (shown - picked_ref[pl.ds(number, 1), :])
 
             def slopes(chunk, inner):
                 share = jnp.exp(logits[number, chunk_of(chunk), :] - log_total)
@@ -1602,9 +1619,9 @@
     return pl.pallas_call(
         kernel,
         name=name,
-        out_shape=(scatter.out, jax.ShapeDtypeStruct(head_rows.shape, bf16), rows, rows),
-        in_specs=[vmem] * 4,
-        out_specs=(vmem,) * 4,
+        out_shape=(scatter.out, jax.ShapeDtypeStruct(head_rows.shape, bf16), rows),
+        in_specs=[vmem] * 3 + [pl.BlockSpec(memory_space=pltpu.SMEM)],
+        out_specs=(vmem,) * 3,
         scratch_shapes=[
             pltpu.VMEM(gather.out.shape, bf16),
             pltpu.VMEM(direct.out.shape, f32),
@@ -1612,12 +1629,14 @@
             pltpu.VMEM((blocks, span, tok_dev), f32),
             pltpu.VMEM((span, blocks * tok_dev), bf16),
             pltpu.VMEM(scatter.value.shape, bf16),
+            pltpu.VMEM((blocks, tok_dev), f32),
+            pltpu.VMEM((blocks, tok_dev), f32),
         ]
         + [item for job in jobs for item in job.scratch],
         compiler_params=pltpu.CompilerParams(
             collective_id=collective_id, has_side_effects=True, vmem_limit_bytes=60 * 1024 * 1024
         ),
-    )(final_rows, head_rows, targets, alive)
+    )(final_rows, head_rows, targets, lengths)
 
 
 def opening(name, collective_id, weights, embedding, ids, memory, head, sizes):
@@ -1640,8 +1659,8 @@
 
     def kernel(*refs):
         ins = list(refs[: len(flat)])
-        outs = list(refs[len(flat) : len(flat) + 7])
-        rest = list(refs[len(flat) + 7 :])
+        outs = list(refs[len(flat) : len(flat) + 8])
+        rest = list(refs[len(flat) + 8 :])
         place = coordinates()
         awaited = greet(peers, place)
 
@@ -1650,7 +1669,7 @@
             del source[:count]
             return taken
 
-        rows_ref, value, code = rest.pop(0), rest.pop(0), rest.pop(0)
+        rows_ref, value, code, ids_ref = (rest.pop(0) for _ in range(4))
         for job in weights:
             pieces = take(ins, len(job.values))
             block = rest.pop(0)
@@ -1658,7 +1677,7 @@
             job.prepare((block, outs.pop(0)) + take(rest, len(job.scratch) - 1), place)
         table.prepare((ins.pop(0), rows_ref) + take(rest, len(table.scratch)), place)
         pack_ids(take(ins, 2), code)
-        ids_ref = outs.pop(0)
+        local_ref, target_ref = outs.pop(0), outs.pop(0)
         codes.prepare((code, ids_ref) + take(rest, len(codes.scratch)), place)
         memories.prepare((ins.pop(0), outs.pop(0)) + take(rest, len(memories.scratch)), place)
         heads.prepare((ins.pop(0), outs.pop(0)) + take(rest, len(heads.scratch)), place)
@@ -1677,16 +1696,22 @@
 
             def one(other, carry):
                 side = place["h"] + (1 - other) * (1 - 2 * place["h"])
-                index = jnp.concatenate(
-                    [
-                        ids_ref[2 * side + place["c"], which, row % 2, pl.ds(row // 2, 1), :][:, :seq_dev]
-                        for which in range(2)
-                    ],
-                    axis=1,
-                )
-                shard = index // voc_dev
-                held = shard % n_gy == 2 * place["s"] + place["h"]
-                index = jnp.where(held, shard // n_gy * voc_dev + index % voc_dev, -1)
+                indices = []
+                for kind, ref in enumerate((local_ref, target_ref)):
+                    line = pl.ds(micro * kind + row // 2, 1)
+                    index = jnp.concatenate(
+                        [
+                            ids_ref[2 * side + place["c"], which, row % 2, line, :][:, :seq_dev]
+                            for which in range(2)
+                        ],
+                        axis=1,
+                    )
+                    shard = index // voc_dev
+                    held = shard % n_gy == 2 * place["s"] + place["h"]
+                    index = jnp.where(held, shard // n_gy * voc_dev + index % voc_dev, -1)
+                    ref[pl.ds(2 * row + side, 1), :] = index
+                    indices.append(index)
+                index = indices[0]
                 at = lax.broadcasted_iota(jnp.int32, (span, tok_dev), 0) == index
                 every = rows_ref[...].reshape(span, width)
                 value[row, side] = t_mm(jnp.where(at, 1.0, 0.0).astype(bf16), every).astype(bf16)
@@ -1725,14 +1750,16 @@
         pltpu.VMEM(table.out.shape, bf16),
         pltpu.VMEM(sums.value.shape, bf16),
         pltpu.VMEM((8, 128), jnp.int32),
+        pltpu.VMEM(codes.out.shape, jnp.int32),
     ]
+    places = jax.ShapeDtypeStruct((n_gy, tok_dev), jnp.int32)
     return pl.pallas_call(
         kernel,
         name=name,
         out_shape=tuple(job.out for job in weights)
-        + (codes.out, memories.out, heads.out, sums.out),
+        + (places, places, memories.out, heads.out, sums.out),
         in_specs=[vmem] * len(flat),
-        out_specs=(anywhere,) * 3 + (vmem, anywhere, anywhere, vmem),
+        out_specs=(anywhere,) * 3 + (vmem, vmem, anywhere, anywhere, vmem),
         scratch_shapes=scratch + [item for job in jobs for item in job.scratch],
         compiler_params=pltpu.CompilerParams(
             collective_id=collective_id, has_side_effects=True, vmem_limit_bytes=60 * 1024 * 1024
@@ -1823,7 +1850,7 @@
         ]
     small_tables = whole_tiles and span <= 2048 and tok_dev == 128
     if small_tables:
-        part_a, part_b, part_c, ids, memory_all, head_rows, resid0 = opening(
+        part_a, part_b, part_c, local_ids, targets, memory_all, head_rows, resid0 = opening(
             "start",
             0,
             weights,
@@ -1856,16 +1883,19 @@
         full.reshape(width, count) for full, count in zip((part_a, part_b, part_c), widths)
     )
     memory_all = memory_all.reshape(n_gy * mem_dev, width)
-    ids = ids[..., : 2 * micro, :seq_dev].reshape(n_gy, 2, 2, micro, seq_dev)
-    ids = ids.transpose(2, 3, 1, 0, 4).reshape(2, sizes["s"] * 2, 2, tok_dev)
-    ids = lax.dynamic_index_in_dim(ids, place["c"], axis=2, keepdims=False).reshape(2, tokens)
-
-    def local_of(index):
-        shard = index // voc_dev
-        return jnp.where(shard % n_gy == column, shard // n_gy * voc_dev + index % voc_dev, -1)
-
-    local_ids = local_of(ids[0])
-    targets = local_of(ids[1])
+    if small_tables:
+        local_ids = local_ids.reshape(tokens)
+    else:
+        ids = ids[..., : 2 * micro, :seq_dev].reshape(n_gy, 2, 2, micro, seq_dev)
+        ids = ids.transpose(2, 3, 1, 0, 4).reshape(2, sizes["s"] * 2, 2, tok_dev)
+        ids = lax.dynamic_index_in_dim(ids, place["c"], axis=2, keepdims=False).reshape(2, tokens)
+
+        def local_of(index):
+            shard = index // voc_dev
+            return jnp.where(shard % n_gy == column, shard // n_gy * voc_dev + index % voc_dev, -1)
+
+        local_ids = local_of(ids[0])
+        targets = local_of(ids[1])
     columns = jnp.arange(span, dtype=jnp.int32)
 
     tok_layout = (sizes["s"], 2, tok_dev, width)
@@ -1883,10 +1913,7 @@
     head_rows = head_rows.reshape(span, width)
 
     plane_lengths = lax.dynamic_slice_in_dim(lengths, 2 * place["a"], 2, axis=1).reshape(-1)
-    live_length = lax.dynamic_index_in_dim(plane_lengths, place["s"], keepdims=False)
-    scalars = jnp.stack([(2 * place["h"] + place["c"]) * tok_dev, live_length])
     table = jnp.asarray(distance_table(seq), bf16)
-    bias_pad = jnp.pad(relative_bias, ((0, 8 - HEADS), (0, 128 - BUCKETS)))
     query_self, own_kv, normed_self, gain_rows = local_kernel(
         "enter",
         enter_kernel,
@@ -1932,23 +1959,21 @@
             rows_f32,
             rows_bf16,
         ],
-        [scalars, query_self, self_kv_all, resid0, gain_rows, table, bias_pad]
+        [lengths, query_self, self_kv_all, resid0, gain_rows, table, relative_bias]
         + [memory_all, part_a, part_b, part_c],
         "svvvvvvaaaa",
         scratch=[pltpu.VMEM(full.shape, bf16) for full in (memory_all, part_a, part_b, part_c)]
         + [pltpu.SemaphoreType.DMA((4,))],
     )
 
-    index = jnp.arange(tokens, dtype=jnp.int32)
-    position = (2 * (index // tok_dev % 2) + place["c"]) * tok_dev + index % tok_dev
-    alive = (position < jnp.repeat(plane_lengths, 2 * tok_dev)).astype(f32)
     if small_tables:
-        by_block = (n_gy, tok_dev)
-        final_slope, head_part, picked, log_total = vocabulary(
-            "vocabulary", 3, final_rows, head_rows, targets.reshape(by_block), alive.reshape(by_block), sizes
+        final_slope, head_part, loss_rows = vocabulary(
+            "vocabulary", 3, final_rows, head_rows, targets, lengths, sizes
         )
-        picked, log_total = picked.reshape(tokens), log_total.reshape(tokens)
     else:
+        index = jnp.arange(tokens, dtype=jnp.int32)
+        position = (2 * (index // tok_dev % 2) + place["c"]) * tok_dev + index % tok_dev
+        alive = (position < jnp.repeat(plane_lengths, 2 * tok_dev)).astype(f32)
         (states,) = exchange("final_rows", 3, [Gather(final_rows, "sh", "sh", sizes, merged)])
         states = states.reshape(tokens, width)
         logits = dot_t(states, head_rows)
@@ -1967,7 +1992,8 @@
         (final_slope,) = exchange(
             "final_slopes", 5, [Scatter(final_part.reshape(tok_layout), "hs", "sh", sizes)]
         )
-    loss_part = jnp.where(column == 0, jnp.sum(alive * log_total), 0.0) - jnp.sum(alive * picked)
+        loss_rows = alive * (jnp.where(column == 0, log_total, 0.0) - picked)
+        loss_rows = loss_rows.reshape(tokens // 128, 128)
 
     grad_a, grad_b, memory_part, part_grad_c, query_slope, kv_slope, grad1, norm_grads, bias_grad = (
         local_kernel(
@@ -1984,9 +2010,9 @@
                 (gain_rows.shape, f32),
                 ((8, 128), f32),
             ],
-            [scalars, final_slope, resid3, hidden, gate_up, normed_ff, resid2, attn_cross]
+            [lengths, final_slope, resid3, hidden, gate_up, normed_ff, resid2, attn_cross]
             + [query_cross, total_cross, normed_cross, resid1, attn_self, query_self, self_kv_all]
-            + [total_self, gain_rows, table, bias_pad, mem_kv, memory_all, part_a, part_b, part_c],
+            + [total_self, gain_rows, table, relative_bias, mem_kv, memory_all, part_a, part_b, part_c],
             "s" + "v" * 18 + "a" * 5,
             "aaa" + "v" * 6,
             [
@@ -2025,8 +2051,6 @@
         (local_ids[:, None] == columns[None, :]).astype(bf16), slopes.reshape(tokens, width)
     ).astype(bf16)
     sums = (grad_a, grad_b, grad_c)
-    at_loss = (jnp.arange(8)[:, None] == 0) & (jnp.arange(128)[None, :] == 64)
-    small = jnp.where(at_loss, loss_part, bias_grad)
     device_layout = (sizes["a"], 2, sizes["s"], 2)
     blocks = [part.reshape(device_layout + packed_shape(part, devices)) for part in sums]
     grad_a, grad_b, grad_c, embedding_grad, memory_grad, small = exchange(
@@ -2039,10 +2063,18 @@
         + [
             Scatter(embed_part.reshape(sizes["a"], 2, voc_dev, width), "ca", "ac", sizes),
             MemoryScatter(memory_part.reshape(sizes["s"], 2, mem_dev, width), sizes),
-            Gather(small, "shac", "acsh", sizes, "ashc"),
+            PackedGather(
+                (bias_grad, loss_rows),
+                jax.ShapeDtypeStruct((16, 128), f32),
+                pack_rows,
+                "shac",
+                "acsh",
+                sizes,
+                "ashc",
+            ),
         ],
     )
-    small = small.reshape(devices, 8, 128)
+    small = small.reshape(devices, 16, 128)
     memory_grad = memory_grad.reshape(micro, 1, mem_dev, width)
     if whole_tiles:
         pieces = [piece.shape[1] for group in groups for piece in group]
@@ -2070,7 +2102,7 @@
             grad.reshape(rows_dev, count) for grad, count in zip((grad_a, grad_b, grad_c), widths)
         )
         small = jnp.sum(small, axis=0)
-        loss = small[0, 64] / jnp.sum(lengths).astype(f32)
+        loss = jnp.sum(small[8:]) / jnp.sum(lengths).astype(f32)
         bias_total = small[:HEADS, :BUCKETS]
         cut = []
         for grad, group in zip((grad_a, grad_b, grad_c), groups):

time: 285 us -> 276 us (0.968)
  other arithmetic: 5.26 us -> 0 us
where the time goes in v3:
time: 276 us; the launch traced here: 274 us
  Pallas kernels  268 us (97%)
  matrix products  5.34 us (2%)
    pallas_call x4, Pallas kernels, exchange(): pl.pallas_call(kernel, name=name, out_shape=tuple((job.out for job in job...  98.2 us
    pallas_call x1, Pallas kernels, opening(): pl.pallas_call(kernel, name=name, out_shape=tuple((job.out for job in wei...  73 us
    pallas_call x1, Pallas kernels, vocabulary(): pl.pallas_call(kernel, name=name, out_shape=(scatter.out, jax.ShapeDtypeS...  52.2 us
    pallas_call x5, Pallas kernels, local_kernel(): pl.pallas_call(kernel, name=name, out_shape=tuple((jax.ShapeDtypeStruct(s...  44.2 us

profile of v3, /device:TPU:0, one launch (start us, length us, event | category | flops | bytes accessed | tf_op | source)
XLA Modules:
  0.0 273.9 jit_solution(14187609820475538222)
XLA Ops:
  0.7 73.0 %start.1 = (bf16[2,2,4,2,16,2048]{5,4,3,2,1,0:T(8,128)(2,1)}, bf16[2,2,4,2,16,2176]{5,4,3,2,1,0:T(8,128)(2,1)}, bf16[2,2,4,2,16,2048]{5,4,3,2,1,0:T(8,128)(2,1)}...) custom-call(bf16[16,1024]{1,0:T(8,128)(2,1)} %refs_0_.1, ...), custom_call_target="tpu_custom_call" | custom-call | tf_op jit(solution)/shard_map/start/pallas_call | solution.py:1756
  73.7 2.9 %enter.1 = (bf16[128,384]{1,0:T(8,128)(2,1)}, bf16[128,768]{1,0:T(8,128)(2,1)}, bf16[128,512]{1,0:T(8,128)(2,1)}, f32[16,512]{1,0:T(8,128)}) custom-call(f32[128,512]{1,0:T(8,128)} %get-tuple-element.88.resid_ref.resid0_ref, bf16[512,2048]{1,0:T(8,128)(2,1)} %bitcast.28), custom_call_target="tpu_custom_call" | custom-call | tf_op jit(solution)/shard_map/enter/pallas_call | solution.py:1413
  76.6 9.7 %self_keys.1 = bf16[2,2,128,768]{3,2,1,0:T(8,128)(2,1)} custom-call(bf16[128,768]{1,0:T(8,128)(2,1)} %get-tuple-element.91.refs_0_), custom_call_target="tpu_custom_call" | custom-call | tf_op jit(solution)/shard_map/self_keys/pallas_call | solution.py:880
  86.4 13.9 %forward.1 = (bf16[128,384]{1,0:T(8,128)(2,1)}, f32[128,128]{1,0:T(8,128)}, f32[128,512]{1,0:T(8,128)}, bf16[128,512]{1,0:T(8,128)(2,1)}, bf16[128,384]{1,0:T(8,...) custom-call(s32[2,4]{1,0:T(2,128)} %lengths_ref.5, ...), custom_call_target="tpu_custom_call" | custom-call | tf_op jit(solution)/shard_map/forward/pallas_call | solution.py:1413
  100.3 52.2 %vocabulary.1 = (f32[128,512]{1,0:T(8,128)}, bf16[2048,512]{1,0:T(8,128)(2,1)}, f32[8,128]{1,0:T(8,128)}) custom-call(bf16[128,512]{1,0:T(8,128)(2,1)} %get-tuple-element.96.refs_0_, bf16[2048,512]{1,0:T(8,128)(2,1)} %bitcast.42, s32[8,128]{1,0:T(8,128)} %get-tuple-element.98.refs_2_, s32[2,4]{1,0:T(2,128)} %lengths_ref.5), custom_call_target="tpu_custom_call" | custom-call | tf_op jit(solution)/shard_map/vocabulary/pallas_call | solution.py:1619
  152.5 19.3 %backward.1 = (bf16[512,2048]{1,0:T(8,128)(2,1)}, bf16[512,2176]{1,0:T(8,128)(2,1)}, bf16[1024,512]{1,0:T(8,128)(2,1)}, bf16[512,768]{1,0:T(8,128)(2,1)}, bf16[1...) custom-call(s32[2,4]{1,0:T(2,128)} %lengths_ref.5, ...), custom_call_target="tpu_custom_call" | custom-call | tf_op jit(solution)/shard_map/backward/pallas_call | solution.py:1413
  171.8 9.8 %key_slopes.1.kv_slope_ref = bf16[128,768]{1,0:T(8,128)(2,1)} custom-call(bf16[2,2,128,768]{3,2,1,0:T(8,128)(2,1)} %bitcast.47), custom_call_target="tpu_custom_call" | custom-call | tf_op jit(solution)/shard_map/key_slopes/pallas_call | solution.py:880
  181.6 0.0 copy-start
  181.6 4.4 %leave.1 = (bf16[512,2048]{1,0:T(8,128)(2,1)}, bf16[128,512]{1,0:T(8,128)(2,1)}) custom-call(bf16[128,384]{1,0:T(8,128)(2,1)} %get-tuple-element.115.query_slope_ref, bf16[128,768]{1,0:T(8,128)(2,1)} %key_slopes.1.kv_slope_ref, bf16[128,512]{1,0:T(8,128)(2,1)} %get-tuple-element.117.normed_ref, f32[128,512]{1,0:T(8,128)} %get-tuple-element.88.resid_ref.resid0_ref, ...), custom_call_target="tpu_custom_call" | custom-call | tf_op jit(solution)/shard_map/leave/pallas_call | solution.py:1413
  186.1 22.7 %row_slopes.1 = (bf16[4,2,128,512]{3,2,1,0:T(8,128)(2,1)}, f32[512,512]{1,0:T(8,128)}) custom-call(bf16[128,512]{1,0:T(8,128)(2,1)} %get-tuple-element.123.refs_0_, bf16[2,2,512,512]{3,2,1,0:T(8,128)(2,1)} %bitcast.41), custom_call_target="tpu_custom_call" | custom-call | tf_op jit(solution)/shard_map/row_slopes/pallas_call | solution.py:880
  208.8 0.0 copy-done
  208.8 5.3 %fusion.2 = bf16[2048,512]{1,0:T(8,128)(2,1)} fusion(bf16[1024,512]{1,0:T(8,128)(2,1)} %bitcast.55, s32[1024]{0:T(1024)S(1)} %bitcast.56), kind=kOutput, calls=%fused_computation.3 | convolution fusion | flops 2150629376 | bytes 3149824 | tf_op jit(solution)/shard_map/sd,sf->df/dot_general | solution.py:932
  214.1 55.9 %scatter_weights.1 = (f32[16,2048]{1,0:T(8,128)}, f32[16,2176]{1,0:T(8,128)}, f32[16,2048]{1,0:T(8,128)}, f32[512,512]{1,0:T(8,128)}, f32[2,128,512]{2,1,0:T(8,128)}, /*index=5*/f32[2,2,4,2,16,128]{5,4,3,2,1,0:T(8,128)}) custom-call(bf16[2,2,4,2,16,2048]{5,4,3,2,1,0:T(8,128)(2,1)} %bitcast.43, bf16[2,2,4,2,16,2176]{5,4,3,2,1,0:T(8,128)(2,1)} %bitcast.40, ...), custom_call_target="tpu_custom_call" | custom-call | tf_op jit(solution)/shard_map/scatter_weights/pallas_call | solution.py:880
  270.1 3.6 %tail.1 = (f32[1,1]{1,0:T(1,128)}, f32[2,1,128,512]{3,2,1,0:T(8,128)}, f32[512,512]{1,0:T(8,128)}, f32[512,512]{1,0:T(8,128)}, f32[6,32]{1,0:T(8,128)}, /*index=...) custom-call(s32[2,4]{1,0:T(2,128)} %lengths_ref.5, ...), custom_call_target="tpu_custom_call" | custom-call | tf_op jit(solution)/shard_map/tail/pallas_call | solution.py:1413
Async XLA Ops:
  181.6 27.2 %copy-start = (s32[8,128]{1,0:T(8,128)S(1)}, s32[8,128]{1,0:T(8,128)}, u32[]{:S(2)}) copy-start(s32[8,128]{1,0:T(8,128)} %get-tuple-element.122) | copy-start | bytes 12292

commit v4 on v3

--- a/solution.py
+++ b/solution.py
@@ -263,6 +263,43 @@
             def _():
                 for number in range(1, 5):
                     self.line_copy(number).wait_send()
+
+
+class Work:
+    def __init__(self, values, out, act, key, columns=None):
+        self.values, self.act, self.key = list(values), act, key
+        self.columns = columns or [None] * len(self.values)
+        self.out = jax.ShapeDtypeStruct(*out)
+        self.in_spec = self.out_spec = pl.BlockSpec(memory_space=pl.ANY)
+        shapes = [
+            value.shape if cut is None else (value.shape[0], cut[1])
+            for value, cut in zip(self.values, self.columns)
+        ]
+        self.scratch = [pltpu.VMEM(shape, value.dtype) for shape, value in zip(shapes, self.values)]
+        self.scratch += [pltpu.VMEM(*out), pltpu.SemaphoreType.DMA((len(shapes) + 1,))]
+        self.peers = []
+
+    def prepare(self, refs, place):
+        count = len(self.values)
+        self.held, self.result, sems = refs[count + 1 : 2 * count + 1], refs[-2], refs[-1]
+        self.copies = []
+        for number, (source, cut, held) in enumerate(zip(refs, self.columns, self.held)):
+            source = source if cut is None else source.at[:, cut[0] : cut[0] + cut[1]]
+            self.copies.append(pltpu.make_async_copy(source, held, sems.at[number]))
+            self.copies[-1].start()
+        self.back = pltpu.make_async_copy(self.result, refs[count], sems.at[count])
+
+    def events(self):
+        return [(self.key, self.run)]
+
+    def run(self):
+        for copy in self.copies:
+            copy.wait()
+        self.act(self.held, self.result)
+        self.back.start()
+
+    def finish(self):
+        self.back.wait()
 
 
 class PackedGather(Gather):
@@ -1062,7 +1099,7 @@
     gains_ref,
     table_ref,
     bias_ref,
-    memory_hbm,
+    mem_kv_hbm,
     part_a_hbm,
     part_b_hbm,
     part_c_hbm,
@@ -1071,7 +1108,6 @@
     resid1_ref,
     normed_cross_ref,
     query_cross_ref,
-    mem_kv_ref,
     attn_cross_ref,
     total_cross_ref,
     resid2_ref,
@@ -1080,15 +1116,15 @@
     hidden_ref,
     resid3_ref,
     final_ref,
-    memory_ref,
+    mem_kv_ref,
     part_a_ref,
     part_b_ref,
     part_c_ref,
     sems,
 ):
     fetched = Fetch(
-        (part_c_hbm, part_b_hbm, memory_hbm, part_a_hbm),
-        (part_c_ref, part_b_ref, memory_ref, part_a_ref),
+        (part_c_hbm, part_b_hbm, mem_kv_hbm, part_a_hbm),
+        (part_c_ref, part_b_ref, mem_kv_ref, part_a_ref),
         sems,
     )
     first, length = query_span(lengths_ref, query_ref.shape[0])
@@ -1117,15 +1153,7 @@
     query_cross_ref[...] = mm(normed, part_c[:, 4 * HD : 5 * HD]).astype(bf16)
 
     part_b = fetched[1]
-    memory = fetched[2]
-    step = min(256, memory.shape[0])
-
-    def project(number, carry):
-        rows = pl.ds(pl.multiple_of(number * step, step), step)
-        mem_kv_ref[rows, :] = mm(memory[rows, :], part_b[:, ff : ff + 2 * HD]).astype(bf16)
-        return carry
-
-    lax.fori_loop(0, memory.shape[0] // step, project, 0)
+    mem_kv_ref = fetched[2]
     total_cross_ref[...] = jnp.zeros(total_cross_ref.shape, f32)
 
     def cross_pair(place, place_v):
@@ -1194,13 +1222,12 @@
     table_ref,
     bias_ref,
     mem_kv_hbm,
-    memory_hbm,
     part_a_hbm,
     part_b_hbm,
     part_c_hbm,
-    grad_a_hbm,
     grad_b_hbm,
-    memory_part_hbm,
+    gate_up_slope_ref,
+    cross_kv_slope_ref,
     grad_c_ref,
     query_slope_ref,
     kv_slope_ref,
@@ -1208,22 +1235,17 @@
     norm_grads_ref,
     bias_grad_ref,
     mem_kv_ref,
-    memory_ref,
     part_a_ref,
     part_b_ref,
     part_c_ref,
-    grad_a_ref,
     grad_b_ref,
-    memory_part_ref,
-    gate_up_slope_ref,
     cross_query_slope_ref,
-    cross_kv_slope_ref,
     sems,
     out_sems,
 ):
     fetched = Fetch(
-        (part_b_hbm, part_a_hbm, mem_kv_hbm, memory_hbm, part_c_hbm),
-        (part_b_ref, part_a_ref, mem_kv_ref, memory_ref, part_c_ref),
+        (part_b_hbm, part_a_hbm, mem_kv_hbm, part_c_hbm),
+        (part_b_ref, part_a_ref, mem_kv_ref, part_c_ref),
         sems,
     )
     first, length = query_span(lengths_ref, query_ref.shape[0])
@@ -1256,15 +1278,10 @@
     norm_grads_ref[2:3] = norm_grad
     grad2 = grad3 + back
 
-    def gate_up_grad(here):
-        grad_a_ref[:, here] = t_mm(normed_ff_ref[...], gate_up_slope_ref[:, here]).astype(bf16)
-
-    in_steps(2 * ff, 2 * FF_STEP, gate_up_grad)
-    copy_a = pltpu.make_async_copy(grad_a_ref, grad_a_hbm, out_sems.at[0])
-    copy_a.start()
-
     cross_in = grad2.astype(bf16)
-    grad_b_ref[:, ff + 2 * HD :] = t_mm(cross_in, attn_cross_ref[...]).astype(bf16)
+    grad_b_ref[:, ff:] = t_mm(cross_in, attn_cross_ref[...]).astype(bf16)
+    copy_b = pltpu.make_async_copy(grad_b_ref, grad_b_hbm, out_sems.at[0])
+    copy_b.start()
     out_slope = mm(cross_in, part_b[:, ff + 2 * HD :]).astype(bf16)
     mem_kv = fetched[2]
     cross_query_slope_ref[...] = out_slope
@@ -1294,27 +1311,7 @@
         cross_kv_slope_ref[:, place_v] = part[3].astype(bf16)
 
     in_steps(HD, 2 * HEAD, cross_pair_back, HD)
-    memory = fetched[3]
-
-    def memory_weights(here, there):
-        grad_b_ref[:, there] = t_mm(memory[...], cross_kv_slope_ref[:, here]).astype(bf16)
-
-    in_steps(2 * HD, FF_STEP, memory_weights, ff)
-    copy_b = pltpu.make_async_copy(grad_b_ref, grad_b_hbm, out_sems.at[1])
-    copy_b.start()
-    step = min(256, memory.shape[0])
-
-    def project(number, carry):
-        rows = pl.ds(pl.multiple_of(number * step, step), step)
-        memory_part_ref[rows, :] = mm_t(
-            cross_kv_slope_ref[rows, :], part_b[:, ff : ff + 2 * HD]
-        ).astype(bf16)
-        return carry
-
-    lax.fori_loop(0, memory.shape[0] // step, project, 0)
-    copy_m = pltpu.make_async_copy(memory_part_ref, memory_part_hbm, out_sems.at[2])
-    copy_m.start()
-    part_c = fetched[4]
+    part_c = fetched[3]
     query_slope = cross_query_slope_ref[...]
     grad_c_ref[:, HD : 2 * HD] = t_mm(normed_cross_ref[...], query_slope).astype(bf16)
     back, norm_grad = rms_back(
@@ -1373,37 +1370,81 @@
     low = (rest - middle.astype(f32)).astype(bf16)
     table = table_ref[...]
     bias_grad_ref[...] = mm_t(high, table) + (mm_t(middle, table) + mm_t(low, table))
-    copy_a.wait()
     copy_b.wait()
-    copy_m.wait()
+
+
+def project_memory(held, result):
+    memory, weight = held
+    step = min(256, memory.shape[0])
+
+    def one(number, carry):
+        rows = pl.ds(pl.multiple_of(number * step, step), step)
+        result[rows, :] = mm(memory[rows, :], weight[...]).astype(bf16)
+        return carry
+
+    lax.fori_loop(0, memory.shape[0] // step, one, 0)
+
+
+def gate_up_grads(held, result):
+    normed, slope = held
+
+    def one(here):
+        result[:, here] = t_mm(normed[...], slope[:, here]).astype(bf16)
+
+    in_steps(slope.shape[1], 2 * FF_STEP, one)
+
+
+def memory_weight_grads(held, result):
+    memory, slope, others = held
+    ff = others.shape[1] - HD
+    result[:, :ff] = others[:, :ff]
+    result[:, ff + 2 * HD :] = others[:, ff:]
+
+    def one(here, there):
+        result[:, there] = t_mm(memory[...], slope[:, here]).astype(bf16)
+
+    in_steps(2 * HD, FF_STEP, one, ff)
+
+
+def memory_slopes(held, result):
+    slope, weight = held
+    step = min(256, slope.shape[0])
+
+    def one(number, carry):
+        rows = pl.ds(pl.multiple_of(number * step, step), step)
+        result[rows, :] = mm_t(slope[rows, :], weight[...]).astype(bf16)
+        return carry
+
+    lax.fori_loop(0, slope.shape[0] // step, one, 0)
 
 
 def leave_kernel(
     query_slope_ref,
     kv_slope_ref,
-    normed_ref,
     resid0_ref,
     grad1_ref,
     gains_ref,
     norm_grads_ref,
-    part_grad_ref,
     part_c_ref,
-    grad_c_ref,
     grad0_ref,
+    all_grads_ref,
 ):
-    normed = normed_ref[...]
-    query_slope, kv_slope = query_slope_ref[...], kv_slope_ref[...]
-    slope = mm_t(query_slope, part_c_ref[:, :HD]) + mm_t(kv_slope, part_c_ref[:, HD : 3 * HD])
+    slope = mm_t(query_slope_ref[...], part_c_ref[:, :HD])
+    slope = slope + mm_t(kv_slope_ref[...], part_c_ref[:, HD : 3 * HD])
     back, norm_grad = rms_back(resid0_ref[...], gains_ref[0:1], slope)
     grad0_ref[...] = (grad1_ref[...] + back).astype(bf16)
-    grad_c_ref[:, :HD] = t_mm(normed, query_slope).astype(bf16)
-    grad_c_ref[:, HD : 3 * HD] = t_mm(normed, kv_slope).astype(bf16)
-    grad_c_ref[:, 3 * HD : 5 * HD] = part_grad_ref[...]
     where = lax.broadcasted_iota(jnp.int32, norm_grads_ref.shape, 0) == 0
-    norm_grads = jnp.where(where, norm_grad, norm_grads_ref[...]).astype(bf16)
+    all_grads_ref[...] = jnp.where(where, norm_grad, norm_grads_ref[...])
+
+
+def self_weight_grads(held, result):
+    query_slope, kv_slope, normed, norm_grads, others = held
+    result[:, :HD] = t_mm(normed[...], query_slope[...]).astype(bf16)
+    result[:, HD : 3 * HD] = t_mm(normed[...], kv_slope[...]).astype(bf16)
+    result[:, 3 * HD : 5 * HD] = others[...]
     row = lax.broadcasted_iota(jnp.int32, (norm_grads.shape[0], GAIN_PAD), 0)
     spread = (row == lanes_of(row.shape)).astype(bf16)
-    grad_c_ref[:, 5 * HD :] = t_mm(norm_grads, spread).astype(bf16)
+    result[:, 5 * HD :] = t_mm(norm_grads[...].astype(bf16), spread).astype(bf16)
 
 
 def local_kernel(name, kernel, outs, args, spaces="", out_spaces="", scratch=()):
@@ -1920,18 +1961,29 @@
         [((tok_dev, HD), bf16), ((tok_dev, 2 * HD), bf16), ((tok_dev, width), bf16), ((16, width), f32)],
         [resid0, part_c],
     )
-    (self_kv_all,) = exchange("self_keys", 2, [Gather(own_kv, "hc", "hc", sizes)])
+    self_kv_all, mem_kv = exchange(
+        "self_keys",
+        2,
+        [
+            Gather(own_kv, "hc", "hc", sizes),
+            Work(
+                (memory_all, part_b),
+                ((n_gy * mem_dev, 2 * HD), bf16),
+                project_memory,
+                0.5,
+                (None, (ff, 2 * HD)),
+            ),
+        ],
+    )
     self_kv_all = self_kv_all.reshape(seq, 2 * HD)
     rows_f32, rows_bf16, rows_heads = ((tok_dev, width), f32), ((tok_dev, width), bf16), ((tok_dev, HD), bf16)
     totals_shape = ((tok_dev, 128), f32)
-    all_mem = n_gy * mem_dev
     (
         attn_self,
         total_self,
         resid1,
         normed_cross,
         query_cross,
-        mem_kv,
         attn_cross,
         total_cross,
         resid2,
@@ -1949,7 +2001,6 @@
             rows_f32,
             rows_bf16,
             rows_heads,
-            ((all_mem, 2 * HD), bf16),
             rows_heads,
             totals_shape,
             rows_f32,
@@ -1960,9 +2011,9 @@
             rows_bf16,
         ],
         [lengths, query_self, self_kv_all, resid0, gain_rows, table, relative_bias]
-        + [memory_all, part_a, part_b, part_c],
+        + [mem_kv, part_a, part_b, part_c],
         "svvvvvvaaaa",
-        scratch=[pltpu.VMEM(full.shape, bf16) for full in (memory_all, part_a, part_b, part_c)]
+        scratch=[pltpu.VMEM(full.shape, bf16) for full in (mem_kv, part_a, part_b, part_c)]
         + [pltpu.SemaphoreType.DMA((4,))],
     )
 
@@ -1995,14 +2046,24 @@
         loss_rows = alive * (jnp.where(column == 0, log_total, 0.0) - picked)
         loss_rows = loss_rows.reshape(tokens // 128, 128)
 
-    grad_a, grad_b, memory_part, part_grad_c, query_slope, kv_slope, grad1, norm_grads, bias_grad = (
+    (
+        part_grad_b,
+        gate_up_slope,
+        cross_kv_slope,
+        part_grad_c,
+        query_slope,
+        kv_slope,
+        grad1,
+        norm_grads,
+        bias_grad,
+    ) = (
         local_kernel(
             "backward",
             backward_kernel,
             [
-                (part_a.shape, bf16),
-                (part_b.shape, bf16),
-                (memory_all.shape, bf16),
+                ((width, ff + HD), bf16),
+                ((tok_dev, 2 * ff), bf16),
+                (mem_kv.shape, bf16),
                 ((width, 2 * HD), bf16),
                 rows_heads,
                 ((seq, 2 * HD), bf16),
@@ -2012,38 +2073,53 @@
             ],
             [lengths, final_slope, resid3, hidden, gate_up, normed_ff, resid2, attn_cross]
             + [query_cross, total_cross, normed_cross, resid1, attn_self, query_self, self_kv_all]
-            + [total_self, gain_rows, table, relative_bias, mem_kv, memory_all, part_a, part_b, part_c],
-            "s" + "v" * 18 + "a" * 5,
-            "aaa" + "v" * 6,
-            [
-                pltpu.VMEM(full.shape, bf16)
-                for full in (mem_kv, memory_all, part_a, part_b, part_c, part_a, part_b, memory_all)
-            ]
+            + [total_self, gain_rows, table, relative_bias, mem_kv, part_a, part_b, part_c],
+            "s" + "v" * 18 + "a" * 4,
+            "a" + "v" * 8,
+            [pltpu.VMEM(full.shape, bf16) for full in (mem_kv, part_a, part_b, part_c)]
             + [
-                pltpu.VMEM((tok_dev, 2 * ff), bf16),
+                pltpu.VMEM((width, ff + HD), bf16),
                 pltpu.VMEM((tok_dev, HD), bf16),
-                pltpu.VMEM(mem_kv.shape, bf16),
-                pltpu.SemaphoreType.DMA((5,)),
-                pltpu.SemaphoreType.DMA((3,)),
+                pltpu.SemaphoreType.DMA((4,)),
+                pltpu.SemaphoreType.DMA((1,)),
             ],
         )
     )
-    (kv_slope,) = exchange(
+    kv_slope, grad_a, grad_b, memory_part = exchange(
         "key_slopes",
         6,
-        [Scatter(kv_slope.reshape(2, 2, tok_dev, 2 * HD), "ch", "hc", sizes, "", bf16)],
+        [
+            Scatter(kv_slope.reshape(2, 2, tok_dev, 2 * HD), "ch", "hc", sizes, "", bf16),
+            Work((normed_ff, gate_up_slope), (part_a.shape, bf16), gate_up_grads, 0.9),
+            Work(
+                (memory_all, cross_kv_slope, part_grad_b), (part_b.shape, bf16), memory_weight_grads, 0.91
+            ),
+            Work(
+                (cross_kv_slope, part_b),
+                (memory_all.shape, bf16),
+                memory_slopes,
+                0.92,
+                (None, (ff, 2 * HD)),
+            ),
+        ],
     )
-    grad_c, grad0 = local_kernel(
+    grad0, norm_grads = local_kernel(
         "leave",
         leave_kernel,
-        [(part_c.shape, bf16), rows_bf16],
-        [query_slope, kv_slope, normed_self, resid0, grad1, gain_rows, norm_grads, part_grad_c, part_c],
+        [rows_bf16, (gain_rows.shape, f32)],
+        [query_slope, kv_slope, resid0, grad1, gain_rows, norm_grads, part_c],
     )
-    slopes, head_grad = exchange(
+    slopes, grad_c, head_grad = exchange(
         "row_slopes",
         7,
         [
             Gather(grad0, "sh", "sh", sizes, merged),
+            Work(
+                (query_slope, kv_slope, normed_self, norm_grads, part_grad_c),
+                (part_c.shape, bf16),
+                self_weight_grads,
+                0.5,
+            ),
             Scatter(head_part.reshape(sizes["a"], 2, voc_dev, width), "ca", "ac", sizes),
         ],
     )

time: 276 us -> 269 us (0.975)
  Pallas kernels: 268 us -> 261 us
    pallas_call x5, Pallas kernels: 44.2 us -> 37.5 us  [local_kernel(): pl.pallas_call(kernel, name=name, out_shape=tuple((jax.ShapeDtypeStruct(s...]
where the time goes in v4:
time: 269 us; the launch traced here: 267 us
  Pallas kernels  261 us (97%)
  matrix products  5.38 us (2%)
    pallas_call x4, Pallas kernels, exchange(): pl.pallas_call(kernel, name=name, out_shape=tuple((job.out for job in job...  98.1 us
    pallas_call x1, Pallas kernels, opening(): pl.pallas_call(kernel, name=name, out_shape=tuple((job.out for job in wei...  73.1 us
    pallas_call x1, Pallas kernels, vocabulary(): pl.pallas_call(kernel, name=name, out_shape=(scatter.out, jax.ShapeDtypeS...  52.1 us
    pallas_call x5, Pallas kernels, local_kernel(): pl.pallas_call(kernel, name=name, out_shape=tuple((jax.ShapeDtypeStruct(s...  37.5 us
    dot_general x1, matrix products, t_dot(): return jnp.einsum('sd,sf->df', left, right, preferred_element_type=f32)  5.38 us

profile of v4, /device:TPU:0, one launch (start us, length us, event | category | flops | bytes accessed | tf_op | source)
XLA Modules:
  0.0 267.1 jit_solution(17583897641169248590)
XLA Ops:
  0.7 73.1 %start.1 = (bf16[2,2,4,2,16,2048]{5,4,3,2,1,0:T(8,128)(2,1)}, bf16[2,2,4,2,16,2176]{5,4,3,2,1,0:T(8,128)(2,1)}, bf16[2,2,4,2,16,2048]{5,4,3,2,1,0:T(8,128)(2,1)}...) custom-call(bf16[16,1024]{1,0:T(8,128)(2,1)} %refs_0_.1, ...), custom_call_target="tpu_custom_call" | custom-call | tf_op jit(solution)/shard_map/start/pallas_call | solution.py:1797
  73.7 2.9 %enter.1 = (bf16[128,384]{1,0:T(8,128)(2,1)}, bf16[128,768]{1,0:T(8,128)(2,1)}, bf16[128,512]{1,0:T(8,128)(2,1)}, f32[16,512]{1,0:T(8,128)}) custom-call(f32[128,512]{1,0:T(8,128)} %get-tuple-element.94.resid_ref.resid0_ref, bf16[512,2048]{1,0:T(8,128)(2,1)} %bitcast.32), custom_call_target="tpu_custom_call" | custom-call | tf_op jit(solution)/shard_map/enter/pallas_call | solution.py:1454
  76.6 9.8 %self_keys.1 = (bf16[2,2,128,768]{3,2,1,0:T(8,128)(2,1)}, bf16[1024,768]{1,0:T(8,128)(2,1)}) custom-call(bf16[128,768]{1,0:T(8,128)(2,1)} %get-tuple-element.97.refs_0_, bf16[1024,512]{1,0:T(8,128)(2,1)} %bitcast.38, bf16[512,2176]{1,0:T(8,128)(2,1)} %bitcast.28), custom_call_target="tpu_custom_call" | custom-call | tf_op jit(solution)/shard_map/self_keys/pallas_call | solution.py:917
  86.4 12.1 %forward.1 = (bf16[128,384]{1,0:T(8,128)(2,1)}, f32[128,128]{1,0:T(8,128)}, f32[128,512]{1,0:T(8,128)}, bf16[128,512]{1,0:T(8,128)(2,1)}, bf16[128,384]{1,0:T(8,...) custom-call(s32[2,4]{1,0:T(2,128)} %lengths_ref.5, ...), custom_call_target="tpu_custom_call" | custom-call | tf_op jit(solution)/shard_map/forward/pallas_call | solution.py:1454
  98.6 52.1 %vocabulary.1 = (f32[128,512]{1,0:T(8,128)}, bf16[2048,512]{1,0:T(8,128)(2,1)}, f32[8,128]{1,0:T(8,128)}) custom-call(bf16[128,512]{1,0:T(8,128)(2,1)} %get-tuple-element.104.refs_0_, bf16[2048,512]{1,0:T(8,128)(2,1)} %bitcast.44, s32[8,128]{1,0:T(8,128)} %get-tuple-element.106.refs_2_, s32[2,4]{1,0:T(2,128)} %lengths_ref.5), custom_call_target="tpu_custom_call" | custom-call | tf_op jit(solution)/shard_map/vocabulary/pallas_call | solution.py:1660
  150.7 15.6 %backward.1 = (bf16[512,1408]{1,0:T(8,128)(2,1)}, bf16[128,2048]{1,0:T(8,128)(2,1)}, bf16[1024,768]{1,0:T(8,128)(2,1)}, bf16[512,768]{1,0:T(8,128)(2,1)}, bf16[1...) custom-call(s32[2,4]{1,0:T(2,128)} %lengths_ref.5, ...), custom_call_target="tpu_custom_call" | custom-call | tf_op jit(solution)/shard_map/backward/pallas_call | solution.py:1454
  166.3 10.0 %key_slopes.1 = (bf16[128,768]{1,0:T(8,128)(2,1)}, bf16[512,2048]{1,0:T(8,128)(2,1)}, bf16[512,2176]{1,0:T(8,128)(2,1)}, bf16[1024,512]{1,0:T(8,128)(2,1)}) custom-call(bf16[2,2,128,768]{3,2,1,0:T(8,128)(2,1)} %bitcast.49, bf16[128,512]{1,0:T(8,128)(2,1)} %get-tuple-element.111.normed_ff_ref.refs_1_, bf16[128,2048]{1,0:T(8,128)(2,1)} %get-tuple-element.121.refs_2_, ...), custom_call_target="tpu_custom_call" | custom-call | tf_op jit(solution)/shard_map/key_slopes/pallas_call | solution.py:917
  176.4 3.2 %leave.1 = (bf16[128,512]{1,0:T(8,128)(2,1)}, f32[16,512]{1,0:T(8,128)}) custom-call(bf16[128,384]{1,0:T(8,128)(2,1)} %get-tuple-element.126.query_slope_ref.refs_1_, bf16[128,768]{1,0:T(8,128)(2,1)} %get-tuple-element.127.kv_slope_ref.refs_2_, f32[128,512]{1,0:T(8,128)} %get-tuple-element.94.resid_ref.resid0_ref, f32[128,512]{1,0:T(8,128)} %get-tuple-element.128.grad1_ref, ...), custom_call_target="tpu_custom_call" | custom-call | tf_op jit(solution)/shard_map/leave/pallas_call | solution.py:1454
  179.6 0.0 copy-start
  179.6 22.8 %row_slopes.1 = (bf16[4,2,128,512]{3,2,1,0:T(8,128)(2,1)}, bf16[512,2048]{1,0:T(8,128)(2,1)}, f32[512,512]{1,0:T(8,128)}) custom-call(bf16[128,512]{1,0:T(8,128)(2,1)} %get-tuple-element.130.refs_0_, bf16[128,384]{1,0:T(8,128)(2,1)} %get-tuple-element.126.query_slope_ref.refs_1_, bf16[128,768]{1,0:T(8,128)(2,1)} %get-tuple-element.127.kv_slope_ref.refs_2_, ...), custom_call_target="tpu_custom_call" | custom-call | tf_op jit(solution)/shard_map/row_slopes/pallas_call | solution.py:917
  202.4 0.0 copy-done
  202.4 5.4 %fusion.2 = bf16[2048,512]{1,0:T(8,128)(2,1)} fusion(bf16[1024,512]{1,0:T(8,128)(2,1)} %bitcast.57, s32[1024]{0:T(1024)S(1)} %bitcast.58), kind=kOutput, calls=%fused_computation.3 | convolution fusion | flops 2150629376 | bytes 3149824 | tf_op jit(solution)/shard_map/sd,sf->df/dot_general | solution.py:969
  207.8 55.4 %scatter_weights.1 = (f32[16,2048]{1,0:T(8,128)}, f32[16,2176]{1,0:T(8,128)}, f32[16,2048]{1,0:T(8,128)}, f32[512,512]{1,0:T(8,128)}, f32[2,128,512]{2,1,0:T(8,128)}, /*index=5*/f32[2,2,4,2,16,128]{5,4,3,2,1,0:T(8,128)}) custom-call(bf16[2,2,4,2,16,2048]{5,4,3,2,1,0:T(8,128)(2,1)} %bitcast.45, bf16[2,2,4,2,16,2176]{5,4,3,2,1,0:T(8,128)(2,1)} %bitcast.42, ...), custom_call_target="tpu_custom_call" | custom-call | tf_op jit(solution)/shard_map/scatter_weights/pallas_call | solution.py:917
  263.3 3.6 %tail.1 = (f32[1,1]{1,0:T(1,128)}, f32[2,1,128,512]{3,2,1,0:T(8,128)}, f32[512,512]{1,0:T(8,128)}, f32[512,512]{1,0:T(8,128)}, f32[6,32]{1,0:T(8,128)}, /*index=...) custom-call(s32[2,4]{1,0:T(2,128)} %lengths_ref.5, ...), custom_call_target="tpu_custom_call" | custom-call | tf_op jit(solution)/shard_map/tail/pallas_call | solution.py:1454
Async XLA Ops:
  179.6 22.8 %copy-start = (s32[8,128]{1,0:T(8,128)S(1)}, s32[8,128]{1,0:T(8,128)}, u32[]{:S(2)}) copy-start(s32[8,128]{1,0:T(8,128)} %get-tuple-element.136) | copy-start | bytes 12292

commit v5 on v4

--- a/solution.py
+++ b/solution.py
@@ -300,6 +300,54 @@
 
     def finish(self):
         self.back.wait()
+
+
+class EmbedPart:
+    def __init__(self, ids, span, gather):
+        self.value, self.gather = ids, gather
+        gather.out_spec = pl.BlockSpec(memory_space=pltpu.VMEM)
+        width = gather.value.shape[1]
+        self.out = jax.ShapeDtypeStruct((span, width), bf16)
+        self.in_spec = self.out_spec = pl.BlockSpec(memory_space=pltpu.VMEM)
+        self.scratch = [pltpu.VMEM((span, ids.shape[0] * ids.shape[1]), bf16)]
+        self.peers = []
+
+    def prepare(self, refs, place):
+        self.ids, self.result, self.chosen = refs
+
+    def events(self):
+        return [(0.6, self.choose), (15, self.run)]
+
+    def choose(self):
+        blocks, wide = self.ids.shape
+        span = self.chosen.shape[0]
+
+        def one(number, carry):
+            at = lax.broadcasted_iota(jnp.int32, (span, wide), 0) == self.ids[pl.ds(number, 1), :]
+            lanes = pl.ds(pl.multiple_of(number * wide, wide), wide)
+            self.chosen[:, lanes] = jnp.where(at, 1.0, 0.0).astype(bf16)
+            return carry
+
+        lax.fori_loop(0, blocks, one, 0)
+
+    def run(self):
+        gather = self.gather
+        gather.local.wait()
+        gather.local_done = True
+        for transfer in gather.transfers:
+            gather.arrive(transfer)
+        span, width = self.result.shape
+
+        def one(number, carry):
+            rows = pl.ds(pl.multiple_of(number * 256, 256), 256)
+            every = gather.target[...].reshape(self.chosen.shape[1], width)
+            self.result[rows, :] = mm(self.chosen[rows, :], every).astype(bf16)
+            return carry
+
+        lax.fori_loop(0, span // 256, one, 0)
+
+    def finish(self):
+        pass
 
 
 class PackedGather(Gather):
@@ -2109,11 +2157,13 @@
         [rows_bf16, (gain_rows.shape, f32)],
         [query_slope, kv_slope, resid0, grad1, gain_rows, norm_grads, part_c],
     )
-    slopes, grad_c, head_grad = exchange(
+    slope_gather = Gather(grad0, "sh", "sh", sizes, merged)
+    embed_job = [EmbedPart(local_ids.reshape(n_gy, tok_dev), span, slope_gather)] if small_tables else []
+    slopes, grad_c, head_grad, *embed_part = exchange(
         "row_slopes",
         7,
         [
-            Gather(grad0, "sh", "sh", sizes, merged),
+            slope_gather,
             Work(
                 (query_slope, kv_slope, normed_self, norm_grads, part_grad_c),
                 (part_c.shape, bf16),
@@ -2121,11 +2171,15 @@
                 0.5,
             ),
             Scatter(head_part.reshape(sizes["a"], 2, voc_dev, width), "ca", "ac", sizes),
-        ],
+        ]
+        + embed_job,
     )
-    embed_part = t_dot(
-        (local_ids[:, None] == columns[None, :]).astype(bf16), slopes.reshape(tokens, width)
-    ).astype(bf16)
+    if small_tables:
+        embed_part = embed_part[0]
+    else:
+        embed_part = t_dot(
+            (local_ids[:, None] == columns[None, :]).astype(bf16), slopes.reshape(tokens, width)
+        ).astype(bf16)
     sums = (grad_a, grad_b, grad_c)
     device_layout = (sizes["a"], 2, sizes["s"], 2)
     blocks = [part.reshape(device_layout + packed_shape(part, devices)) for part in sums]

time: 269 us -> 267 us (level)
  matrix products: 5.38 us -> 0 us
  Pallas kernels: 261 us -> 265 us
    dot_general x1 -> x0, matrix products: 5.38 us -> none  [t_dot(): return jnp.einsum('sd,sf->df', left, right, preferred_element_type=f32)]
    pallas_call x4, Pallas kernels: 98.1 us -> 102 us  [exchange(): pl.pallas_call(kernel, name=name, out_shape=tuple((job.out for job in job...]
where the time goes in v5:
time: 267 us; the launch traced here: 266 us
  Pallas kernels  265 us (99%)
    pallas_call x4, Pallas kernels, exchange(): pl.pallas_call(kernel, name=name, out_shape=tuple((job.out for job in job...  102 us
    pallas_call x1, Pallas kernels, opening(): pl.pallas_call(kernel, name=name, out_shape=tuple((job.out for job in wei...  73.1 us
    pallas_call x1, Pallas kernels, vocabulary(): pl.pallas_call(kernel, name=name, out_shape=(scatter.out, jax.ShapeDtypeS...  52.2 us
    pallas_call x5, Pallas kernels, local_kernel(): pl.pallas_call(kernel, name=name, out_shape=tuple((jax.ShapeDtypeStruct(s...  37.5 us

profile of v5, /device:TPU:0, one launch (start us, length us, event | category | flops | bytes accessed | tf_op | source)
XLA Modules:
  0.0 265.9 jit_solution(11740027756102379096)
XLA Ops:
  0.7 73.1 %start.1 = (bf16[2,2,4,2,16,2048]{5,4,3,2,1,0:T(8,128)(2,1)}, bf16[2,2,4,2,16,2176]{5,4,3,2,1,0:T(8,128)(2,1)}, bf16[2,2,4,2,16,2048]{5,4,3,2,1,0:T(8,128)(2,1)}...) custom-call(bf16[16,1024]{1,0:T(8,128)(2,1)} %refs_0_.1, ...), custom_call_target="tpu_custom_call" | custom-call | tf_op jit(solution)/shard_map/start/pallas_call | solution.py:1845
  73.7 2.9 %enter.1 = (bf16[128,384]{1,0:T(8,128)(2,1)}, bf16[128,768]{1,0:T(8,128)(2,1)}, bf16[128,512]{1,0:T(8,128)(2,1)}, f32[16,512]{1,0:T(8,128)}) custom-call(f32[128,512]{1,0:T(8,128)} %get-tuple-element.94.resid_ref.resid0_ref, bf16[512,2048]{1,0:T(8,128)(2,1)} %bitcast.29), custom_call_target="tpu_custom_call" | custom-call | tf_op jit(solution)/shard_map/enter/pallas_call | solution.py:1502
  76.6 9.8 %self_keys.1 = (bf16[2,2,128,768]{3,2,1,0:T(8,128)(2,1)}, bf16[1024,768]{1,0:T(8,128)(2,1)}) custom-call(bf16[128,768]{1,0:T(8,128)(2,1)} %get-tuple-element.97.refs_0_, bf16[1024,512]{1,0:T(8,128)(2,1)} %bitcast.35, bf16[512,2176]{1,0:T(8,128)(2,1)} %bitcast.25), custom_call_target="tpu_custom_call" | custom-call | tf_op jit(solution)/shard_map/self_keys/pallas_call | solution.py:965
  86.4 12.1 %forward.1 = (bf16[128,384]{1,0:T(8,128)(2,1)}, f32[128,128]{1,0:T(8,128)}, f32[128,512]{1,0:T(8,128)}, bf16[128,512]{1,0:T(8,128)(2,1)}, bf16[128,384]{1,0:T(8,...) custom-call(s32[2,4]{1,0:T(2,128)} %lengths_ref.5, ...), custom_call_target="tpu_custom_call" | custom-call | tf_op jit(solution)/shard_map/forward/pallas_call | solution.py:1502
  98.6 52.2 %vocabulary.1 = (f32[128,512]{1,0:T(8,128)}, bf16[2048,512]{1,0:T(8,128)(2,1)}, f32[8,128]{1,0:T(8,128)}) custom-call(bf16[128,512]{1,0:T(8,128)(2,1)} %get-tuple-element.104.refs_0_, bf16[2048,512]{1,0:T(8,128)(2,1)} %bitcast.41, s32[8,128]{1,0:T(8,128)} %get-tuple-element.106.refs_2_, s32[2,4]{1,0:T(2,128)} %lengths_ref.5), custom_call_target="tpu_custom_call" | custom-call | tf_op jit(solution)/shard_map/vocabulary/pallas_call | solution.py:1708
  150.8 15.6 %backward.1 = (bf16[512,1408]{1,0:T(8,128)(2,1)}, bf16[128,2048]{1,0:T(8,128)(2,1)}, bf16[1024,768]{1,0:T(8,128)(2,1)}, bf16[512,768]{1,0:T(8,128)(2,1)}, bf16[1...) custom-call(s32[2,4]{1,0:T(2,128)} %lengths_ref.5, ...), custom_call_target="tpu_custom_call" | custom-call | tf_op jit(solution)/shard_map/backward/pallas_call | solution.py:1502
  166.4 10.0 %key_slopes.1 = (bf16[128,768]{1,0:T(8,128)(2,1)}, bf16[512,2048]{1,0:T(8,128)(2,1)}, bf16[512,2176]{1,0:T(8,128)(2,1)}, bf16[1024,512]{1,0:T(8,128)(2,1)}) custom-call(bf16[2,2,128,768]{3,2,1,0:T(8,128)(2,1)} %bitcast.46, bf16[128,512]{1,0:T(8,128)(2,1)} %get-tuple-element.111.normed_ff_ref.refs_1_, bf16[128,2048]{1,0:T(8,128)(2,1)} %get-tuple-element.121.refs_2_, ...), custom_call_target="tpu_custom_call" | custom-call | tf_op jit(solution)/shard_map/key_slopes/pallas_call | solution.py:965
  176.3 3.2 %leave.1 = (bf16[128,512]{1,0:T(8,128)(2,1)}, f32[16,512]{1,0:T(8,128)}) custom-call(bf16[128,384]{1,0:T(8,128)(2,1)} %get-tuple-element.126.query_slope_ref.refs_1_, bf16[128,768]{1,0:T(8,128)(2,1)} %get-tuple-element.127.kv_slope_ref.refs_2_, f32[128,512]{1,0:T(8,128)} %get-tuple-element.94.resid_ref.resid0_ref, f32[128,512]{1,0:T(8,128)} %get-tuple-element.128.grad1_ref, ...), custom_call_target="tpu_custom_call" | custom-call | tf_op jit(solution)/shard_map/leave/pallas_call | solution.py:1502
  179.6 26.3 %row_slopes.1 = (bf16[4,2,128,512]{3,2,1,0:T(8,128)(2,1)}, bf16[512,2048]{1,0:T(8,128)(2,1)}, f32[512,512]{1,0:T(8,128)}, bf16[2048,512]{1,0:T(8,128)(2,1)}) custom-call(bf16[128,512]{1,0:T(8,128)(2,1)} %get-tuple-element.130.refs_0_, bf16[128,384]{1,0:T(8,128)(2,1)} %get-tuple-element.126.query_slope_ref.refs_1_, ...), custom_call_target="tpu_custom_call" | custom-call | tf_op jit(solution)/shard_map/row_slopes/pallas_call | solution.py:965
  205.9 56.2 %scatter_weights.1 = (f32[16,2048]{1,0:T(8,128)}, f32[16,2176]{1,0:T(8,128)}, f32[16,2048]{1,0:T(8,128)}, f32[512,512]{1,0:T(8,128)}, f32[2,128,512]{2,1,0:T(8,128)}, /*index=5*/f32[2,2,4,2,16,128]{5,4,3,2,1,0:T(8,128)}) custom-call(bf16[2,2,4,2,16,2048]{5,4,3,2,1,0:T(8,128)(2,1)} %bitcast.42, bf16[2,2,4,2,16,2176]{5,4,3,2,1,0:T(8,128)(2,1)} %bitcast.39, ...), custom_call_target="tpu_custom_call" | custom-call | tf_op jit(solution)/shard_map/scatter_weights/pallas_call | solution.py:965
  262.1 3.6 %tail.1 = (f32[1,1]{1,0:T(1,128)}, f32[2,1,128,512]{3,2,1,0:T(8,128)}, f32[512,512]{1,0:T(8,128)}, f32[512,512]{1,0:T(8,128)}, f32[6,32]{1,0:T(8,128)}, /*index=...) custom-call(s32[2,4]{1,0:T(2,128)} %lengths_ref.5, ...), custom_call_target="tpu_custom_call" | custom-call | tf_op jit(solution)/shard_map/tail/pallas_call | solution.py:1502
